TPU v7x, 32 devices: a whole 2x2x4 slice. The times are simulated.
32 devices in a mesh: pat: 4 (over z), vox: 8 (over y, x, core).
Axes of the slice: x: 2, y: 2, z: 4, core: 2. Of those that a mesh axis runs over, the one named last changes fastest.
Arguments:
- conductivity: float32 [16, 128, 128], P('vox'), may hold values from 0.3 to 1.5
- warm_forward: float32 [16, 32, 128, 128], P('vox', 'pat'), may hold values from -3 to 3
- warm_adjoint: float32 [16, 32, 128, 128], P('vox', 'pat'), may hold values from -3 to 3
- electrodes: int32 [128], replicated, may hold values from 0 to 262143
- patterns: int32 [32, 4], P('pat'), may hold values from 0 to 127, all different within a row
- observed: float32 [32], P('pat'), may hold values from -16 to 16
Outputs:
- gradient: float32 [16, 128, 128], P('vox')
- predicted: float32 [32], P('pat')
All inputs are finite; a program needn't handle non-finite values.
Results may differ from a plain program's by a relative error of at most 0.0003.
Values sent between devices are 32-bit elements; how exact they have to be, the bound alone decides.
No kernel may reach another device: no remote copies, remote signals or barrier semaphores. Data moves between devices by JAX's collectives and lax.ppermute only.
A program may use at most 64 MiB of HBM per device.

v0:
```python
import math

import jax
import jax.numpy as jnp
from jax import lax
from jax.sharding import PartitionSpec as P

ITERS = 2


leakage = 0.05


def extended(block, sides, width):
    for axis, dim in sides:
        count = lax.axis_size(axis)
        forward = [(i, i + 1) for i in range(count - 1)]
        backward = [(target, source) for source, target in forward]
        low = lax.ppermute(
            lax.slice_in_dim(block, block.shape[dim] - width, None, axis=dim), axis, forward
        )
        high = lax.ppermute(lax.slice_in_dim(block, 0, width, axis=dim), axis, backward)
        block = jnp.concatenate([low, block, high], axis=dim)
    return block


def both_sides(values, along_axis):
    lower_pad = [(0, 0)] * values.ndim
    upper_pad = [(0, 0)] * values.ndim
    lower_pad[along_axis] = (1, 0)
    upper_pad[along_axis] = (0, 1)
    return jnp.pad(values, lower_pad) + jnp.pad(values, upper_pad)


def spread(values, along_axis):
    lower_pad = [(0, 0)] * values.ndim
    upper_pad = [(0, 0)] * values.ndim
    lower_pad[along_axis] = (1, 0)
    upper_pad[along_axis] = (0, 1)
    return jnp.pad(values, lower_pad) - jnp.pad(values, upper_pad)


def operate(values, coeffs):
    depth_faces, row_faces, column_faces = coeffs
    padded = extended(values, (("vox", 0),), 1)
    flux_depth = depth_faces[:, None] * (padded[1:] - padded[:-1])
    result = leakage * values + (flux_depth[:-1] - flux_depth[1:])
    result = result + spread(row_faces[:, None] * (values[:, :, 1:] - values[:, :, :-1]), 2)
    result = result + spread(
        column_faces[:, None] * (values[:, :, :, 1:] - values[:, :, :, :-1]), 3
    )
    return result


def inner(left_factor, right_factor):
    return jnp.sum(left_factor * right_factor, axis=(0, 2, 3))


def widen(vector):
    return vector[None, :, None, None]


def pattern_sum(local_terms):
    return lax.psum(local_terms, "vox")


def solve_pattern(right_side, initial, coeffs, diagonal):
    solution = initial
    residue = right_side - operate(solution, coeffs)
    precond = residue / diagonal
    direction = precond
    current = pattern_sum(inner(residue, precond))
    for iteration in range(ITERS):
        applied = operate(direction, coeffs)
        step_size = current / pattern_sum(inner(direction, applied))
        solution = solution + widen(step_size) * direction
        residue = residue - widen(step_size) * applied
        if iteration + 1 < ITERS:
            precond = residue / diagonal
            following = pattern_sum(inner(residue, precond))
            direction = precond + widen(following / current) * direction
            current = following
    return solution


def per_device(conductivity, warm_forward, warm_adjoint, electrodes, patterns, observed):
    plane_count, pattern_count, row_count, column_count = warm_forward.shape
    position = lax.axis_index("vox")
    layers = lax.axis_size("vox")
    strength = 2.0 * math.sqrt(layers * plane_count * row_count * column_count)
    data_weight = 0.1 * strength
    lower_open = (position > 0).astype(jnp.float32)
    upper_open = (position < layers - 1).astype(jnp.float32)
    padded_sigma = extended(conductivity, (("vox", 0),), 1)
    face_mask = jnp.concatenate(
        [lower_open[None], jnp.ones((plane_count - 1,), jnp.float32), upper_open[None]]
    )
    depth_faces = 0.5 * (padded_sigma[1:] + padded_sigma[:-1]) * face_mask[:, None, None]
    row_faces = 0.5 * (conductivity[:, 1:] + conductivity[:, :-1])
    column_faces = 0.5 * (conductivity[:, :, 1:] + conductivity[:, :, :-1])
    coeffs = (depth_faces, row_faces, column_faces)
    diagonal = (
        leakage
        + (depth_faces[:-1] + depth_faces[1:])
        + both_sides(row_faces, 1)
        + both_sides(column_faces, 2)
    )
    diagonal = diagonal[:, None]
    electrode_ids = jnp.arange(electrodes.shape[0], dtype=jnp.int32)
    picked = jnp.sum(
        jnp.where(
            patterns[:, :, None] == electrode_ids[None, None, :], electrodes[None, None, :], 0
        ),
        axis=2,
    )
    offset = position * (plane_count * row_count * column_count)
    local_cell = picked - offset
    grid_shape = (plane_count, 1, row_count, column_count)
    cell_index = (
        lax.broadcasted_iota(jnp.int32, grid_shape, 0) * row_count
        + lax.broadcasted_iota(jnp.int32, grid_shape, 2)
    ) * column_count + lax.broadcasted_iota(jnp.int32, grid_shape, 3)

    def marker(which_one):
        return (cell_index == local_cell[:, which_one][None, :, None, None]).astype(jnp.float32)

    forward = solve_pattern(strength * (marker(0) - marker(1)), warm_forward, coeffs, diagonal)
    probe_weights = marker(2) - marker(3)
    predicted = lax.psum(inner(probe_weights, forward), "vox")
    misfit = predicted - observed
    adjoint = solve_pattern(
        widen(data_weight * misfit) * probe_weights, warm_adjoint, coeffs, diagonal
    )
    stacked = jnp.concatenate([forward, adjoint], axis=1)
    padded_pair = extended(stacked, (("vox", 0),), 1)
    padded_forward = padded_pair[:, :pattern_count]
    padded_adjoint = padded_pair[:, pattern_count:]
    depth_products = jnp.sum(
        (padded_forward[1:] - padded_forward[:-1]) * (padded_adjoint[1:] - padded_adjoint[:-1]),
        axis=1,
    )
    depth_products = depth_products * face_mask[:, None, None]
    grad_depth = depth_products[:-1] + depth_products[1:]
    row_products = jnp.sum(
        (forward[:, :, 1:] - forward[:, :, :-1]) * (adjoint[:, :, 1:] - adjoint[:, :, :-1]), axis=1
    )
    column_products = jnp.sum(
        (forward[:, :, :, 1:] - forward[:, :, :, :-1])
        * (adjoint[:, :, :, 1:] - adjoint[:, :, :, :-1]),
        axis=1,
    )
    local_gradient = -0.5 * (
        grad_depth + both_sides(row_products, 1) + both_sides(column_products, 2)
    )
    gradient = lax.psum(local_gradient, "pat")
    return (gradient, predicted)


def solution(mesh):
    in_specs = (
        P("vox", None, None),
        P("vox", "pat", None, None),
        P("vox", "pat", None, None),
        P(),
        P("pat", None),
        P("pat"),
    )
    out_specs = (P("vox", None, None), P("pat"))
    return jax.shard_map(
        per_device, mesh=mesh, in_specs=in_specs, out_specs=out_specs, check_vma=False
    )
```

profile of v0, /device:TPU:0, one launch (start us, length us, event | category | flops | bytes accessed | tf_op | source)
XLA Modules:
  0.0 282.5 jit_solution(13601715273596078150)
XLA Ops:
  9.5 3.0 %collective-permute-start.1 = (f32[1,128,128]{2,1,0:T(8,128)S(1)}, f32[1,128,128]{2,1,0:T(8,128)S(1)}, u32[]{:S(2)}, u32[]{:S(2)}) collective-permute-start(f32[1,128,128]{2,1,0:T(8,128)S(1)} %get-tuple-element.42), channel_id=1, source_target_pairs={{0,1},{1,2},{2,3},{3,4},{4,5},{5,6},{6,7},{8,9},{9,10},{10,11},{11... | collective-permute-start | bytes 196616 | tf_op jit(solution)/shard_map/ppermute | solution.py:19
  12.5 2.1 fusion.61
  16.1 5.9 %collective-permute-start.3 = (f32[1,8,128,128]{3,2,1,0:T(8,128)S(1)}, f32[1,8,128,128]{3,2,1,0:T(8,128)}, u32[]{:S(2)}, u32[]{:S(2)}) collective-permute-start(f32[1,8,128,128]{3,2,1,0:T(8,128)S(1)} %get-tuple-element.32), channel_id=1, source_target_pairs={{0,1},{1,2},{2,3},{3,4},{4,5},{5,6},{6,7},{8,9},{9,10},{10,11},{11... | collective-permute-start | bytes 1572872 | tf_op jit(solution)/shard_map/ppermute | solution.py:19
  23.1 3.7 %collective-permute-start.9 = (f32[1,8,128,128]{3,2,1,0:T(8,128)}, f32[1,8,128,128]{3,2,1,0:T(8,128)}, u32[]{:S(2)}, u32[]{:S(2)}) collective-permute-start(f32[1,8,128,128]{3,2,1,0:T(8,128)} %get-tuple-element.34), channel_id=1, source_target_pairs={{0,1},{1,2},{2,3},{3,4},{4,5},{5,6},{6,7},{8,9},{9,10},{10,11},{11... | collective-permute-start | bytes 1572872 | tf_op jit(solution)/shard_map/ppermute | solution.py:19
  32.5 3.3 %collective-permute-start.5 = (f32[1,8,128,128]{3,2,1,0:T(8,128)S(1)}, f32[1,8,128,128]{3,2,1,0:T(8,128)S(1)}, u32[]{:S(2)}, u32[]{:S(2)}) collective-permute-start(f32[1,8,128,128]{3,2,1,0:T(8,128)S(1)} %get-tuple-element.30), channel_id=1, source_target_pairs={{0,1},{1,2},{2,3},{3,4},{4,5},{5,6},{6,7},{8,9},{9,10},{10,11},{11... | collective-permute-start | bytes 1572872 | tf_op jit(solution)/shard_map/ppermute | solution.py:19
  37.5 1.7 multiply_reduce_fusion.5
  39.2 27.2 %all-reduce.33 = (f32[8]{0:T(128)S(1)}, f32[8]{0:T(128)S(1)}) all-reduce(f32[8]{0:T(128)S(1)} %get-tuple-element.5, f32[8]{0:T(128)S(1)} %get-tuple-element.4), channel_id=1, replica_groups=mesh['pat'=4,'vox'=8] {'vox'}, use_global_device_ids=true, to_apply=%region_2.3 | all-reduce | flops 16 | bytes 128 | tf_op jit(solution)/shard_map/psum | solution.py:64
  66.5 1.6 multiply_reduce_fusion.4
  69.3 15.8 %psum.72 = f32[8]{0:T(128)S(1)} all-reduce(f32[8]{0:T(128)S(1)} %multiply_reduce_fusion.4), channel_id=1, replica_groups=mesh['pat'=4,'vox'=8] {'vox'}, use_global_device_ids=true, to_apply=%region_6.7 | all-reduce | flops 8 | bytes 64 | tf_op jit(solution)/shard_map/psum | solution.py:64
  85.2 1.8 multiply_add_fusion.3
  88.4 3.2 %collective-permute-start.7 = (f32[1,8,128,128]{3,2,1,0:T(8,128)S(1)}, f32[1,8,128,128]{3,2,1,0:T(8,128)S(1)}, u32[]{:S(2)}, u32[]{:S(2)}) collective-permute-start(f32[1,8,128,128]{3,2,1,0:T(8,128)S(1)} %get-tuple-element.28), channel_id=1, source_target_pairs={{0,1},{1,2},{2,3},{3,4},{4,5},{5,6},{6,7},{8,9},{9,10},{10,11},{11... | collective-permute-start | bytes 1572872 | tf_op jit(solution)/shard_map/ppermute | solution.py:19
  91.6 1.6 fusion.29
  94.5 2.8 fusion.4
  98.0 20.6 %psum.73 = f32[8]{0:T(128)S(1)} all-reduce(f32[8]{0:T(128)S(1)} %fusion.35), channel_id=1, replica_groups=mesh['pat'=4,'vox'=8] {'vox'}, use_global_device_ids=true, to_apply=%region_8.9 | all-reduce | flops 8 | bytes 64 | tf_op jit(solution)/shard_map/psum | solution.py:64
  118.6 2.8 multiply_reduce_fusion.3
  121.4 12.4 %psum.74 = f32[8]{0:T(128)S(1)} all-reduce(f32[8]{0:T(128)S(1)} %get-tuple-element.15), channel_id=1, replica_groups=mesh['pat'=4,'vox'=8] {'vox'}, use_global_device_ids=true, to_apply=%region_10.11 | all-reduce | flops 8 | bytes 64 | tf_op jit(solution)/shard_map/psum | solution.py:129
  133.9 3.7 %broadcast_divide_fusion = (f32[2,8,128,128]{3,2,1,0:T(8,128)S(1)}, f32[2,8,128,128]{3,2,1,0:T(8,128)S(1)}) fusion(f32[2,128,128]{2,1,0:T(8,128)S(1)} %fusion.51, f32[2,8,128,127]{3,2,1,0:T(8,128)} %get-tuple-element.41, f32[2,8,127,128]{3,2,1,0:T(8,128)} %get-tuple-element.39, f32[3,8,128,128]{3,2,1,0:T(8,128)} %get-tuple-element.37, ...), kind=kLoop, calls=%fused_computation.94 | loop fusion | flops 3932160 | bytes 7585888 | tf_op jit(solution)/shard_map/div | solution.py:70
  139.0 3.2 %collective-permute-start.11 = (f32[1,8,128,128]{3,2,1,0:T(8,128)S(1)}, f32[1,8,128,128]{3,2,1,0:T(8,128)S(1)}, u32[]{:S(2)}, u32[]{:S(2)}) collective-permute-start(f32[1,8,128,128]{3,2,1,0:T(8,128)S(1)} %get-tuple-element.26), channel_id=1, source_target_pairs={{0,1},{1,2},{2,3},{3,4},{4,5},{5,6},{6,7},{8,9},{9,10},{10,11},{11... | collective-permute-start | bytes 1572872 | tf_op jit(solution)/shard_map/ppermute | solution.py:19
  144.7 20.3 %all-reduce.32 = (f32[8]{0:T(128)S(1)}, f32[8]{0:T(128)S(1)}) all-reduce(f32[8]{0:T(128)S(1)} %get-tuple-element.3, f32[8]{0:T(128)S(1)} %get-tuple-element.2), channel_id=1, replica_groups=mesh['pat'=4,'vox'=8] {'vox'}, use_global_device_ids=true, to_apply=%region_12.13 | all-reduce | flops 16 | bytes 128 | tf_op jit(solution)/shard_map/psum | solution.py:64
  165.4 12.6 %psum.77 = f32[8]{0:T(128)S(1)} all-reduce(f32[8]{0:T(128)S(1)} %multiply_reduce_fusion), channel_id=1, replica_groups=mesh['pat'=4,'vox'=8] {'vox'}, use_global_device_ids=true, to_apply=%region_16.17 | all-reduce | flops 8 | bytes 64 | tf_op jit(solution)/shard_map/psum | solution.py:64
  180.9 3.2 %collective-permute-start.13 = (f32[1,8,128,128]{3,2,1,0:T(8,128)S(1)}, f32[1,8,128,128]{3,2,1,0:T(8,128)S(1)}, u32[]{:S(2)}, u32[]{:S(2)}) collective-permute-start(f32[1,8,128,128]{3,2,1,0:T(8,128)S(1)} %get-tuple-element.24), channel_id=1, source_target_pairs={{0,1},{1,2},{2,3},{3,4},{4,5},{5,6},{6,7},{8,9},{9,10},{10,11},{11... | collective-permute-start | bytes 1572872 | tf_op jit(solution)/shard_map/ppermute | solution.py:19
  186.5 20.7 %psum.78 = f32[8]{0:T(128)S(1)} all-reduce(f32[8]{0:T(128)S(1)} %fusion.19), channel_id=1, replica_groups=mesh['pat'=4,'vox'=8] {'vox'}, use_global_device_ids=true, to_apply=%region_18.19 | all-reduce | flops 8 | bytes 64 | tf_op jit(solution)/shard_map/psum | solution.py:64
  210.0 3.1 %collective-permute-start.15 = (f32[1,16,128,128]{3,2,1,0:T(8,128)S(1)}, f32[1,16,128,128]{3,2,1,0:T(8,128)S(1)}, u32[]{:S(2)}, u32[]{:S(2)}) collective-permute-start(f32[1,16,128,128]{3,2,1,0:T(8,128)S(1)} %get-tuple-element.23), channel_id=1, source_target_pairs={{0,1},{1,2},{2,3},{3,4},{4,5},{5,6},{6,7},{8,9},{9,10},{10,11},{11... | collective-permute-start | bytes 3145736 | tf_op jit(solution)/shard_map/ppermute | solution.py:19
  217.7 56.4 %all-reduce.36.cloned.1.call-done = f32[2,128,128]{2,1,0:T(8,128)} async-done(((f32[2,128,128]{2,1,0:T(8,128)}), f32[2,128,128]{2,1,0:T(8,128)}) %all-reduce.36.cloned.1.call-update) | async-done | bytes 131088 | tf_op jit(solution)/shard_map/psum | solution.py:155
  (120 shorter events, 34.9 us)
Async XLA Ops:
  7.2 14.8 %copy-start = (f32[2,8,128,128]{3,2,1,0:T(8,128)S(1)}, f32[2,8,128,128]{3,2,1,0:T(8,128)}, u32[]{:S(2)}) copy-start(f32[2,8,128,128]{3,2,1,0:T(8,128)} %param.8) | copy-start | bytes 3145732
  7.2 266.9 %all-reduce.36.cloned.1.call-start = ((), (), s32[]{:S(2)}) async-start(), calls=%async_computation | async-start | bytes 262144 | tf_op jit(solution)/shard_map/psum | solution.py:155
  8.2 20.3 %collective-permute-start = (f32[1,128,128]{2,1,0:T(8,128)S(1)}, f32[1,128,128]{2,1,0:T(8,128)S(1)}, u32[]{:S(2)}, u32[]{:S(2)}) collective-permute-start(f32[1,128,128]{2,1,0:T(8,128)S(1)} %get-tuple-element.43), channel_id=1, source_target_pairs={{1,0},{2,1},{3,2},{4,3},{5,4},{6,5},{7,6},{9,8},{10,9},{11,10},{12... | collective-permute-start | bytes 196616 | tf_op jit(solution)/shard_map/ppermute | solution.py:22
  9.5 19.0 %collective-permute-start.1 = (f32[1,128,128]{2,1,0:T(8,128)S(1)}, f32[1,128,128]{2,1,0:T(8,128)S(1)}, u32[]{:S(2)}, u32[]{:S(2)}) collective-permute-start(f32[1,128,128]{2,1,0:T(8,128)S(1)} %get-tuple-element.42), channel_id=1, source_target_pairs={{0,1},{1,2},{2,3},{3,4},{4,5},{5,6},{6,7},{8,9},{9,10},{10,11},{11... | collective-permute-start | bytes 196616 | tf_op jit(solution)/shard_map/ppermute | solution.py:19
  14.6 13.0 %copy-start.17 = (s32[8,4]{0,1:T(4,128)S(1)}, s32[8,4]{0,1:T(4,128)}, u32[]{:S(2)}) copy-start(s32[8,4]{0,1:T(4,128)} %param.10) | copy-start | bytes 388
  14.6 13.0 %copy-start.18 = (s32[128]{0:T(128)S(1)}, s32[128]{0:T(128)}, u32[]{:S(2)}) copy-start(s32[128]{0:T(128)} %param.9) | copy-start | bytes 1540
  14.6 13.3 %copy-start.1 = (f32[2,8,128,128]{3,2,1,0:T(8,128)S(1)}, f32[2,8,128,128]{3,2,1,0:T(8,128)}, u32[]{:S(2)}) copy-start(f32[2,8,128,128]{3,2,1,0:T(8,128)} %param.7) | copy-start | bytes 3145732
  14.6 14.1 %collective-permute-start.2 = (f32[1,8,128,128]{3,2,1,0:T(8,128)}, f32[1,8,128,128]{3,2,1,0:T(8,128)}, u32[]{:S(2)}, u32[]{:S(2)}) collective-permute-start(f32[1,8,128,128]{3,2,1,0:T(8,128)} %get-tuple-element.33), channel_id=1, source_target_pairs={{1,0},{2,1},{3,2},{4,3},{5,4},{6,5},{7,6},{9,8},{10,9},{11,10},{12... | collective-permute-start | bytes 1572872 | tf_op jit(solution)/shard_map/ppermute | solution.py:22
  16.1 12.7 %collective-permute-start.3 = (f32[1,8,128,128]{3,2,1,0:T(8,128)S(1)}, f32[1,8,128,128]{3,2,1,0:T(8,128)}, u32[]{:S(2)}, u32[]{:S(2)}) collective-permute-start(f32[1,8,128,128]{3,2,1,0:T(8,128)S(1)} %get-tuple-element.32), channel_id=1, source_target_pairs={{0,1},{1,2},{2,3},{3,4},{4,5},{5,6},{6,7},{8,9},{9,10},{10,11},{11... | collective-permute-start | bytes 1572872 | tf_op jit(solution)/shard_map/ppermute | solution.py:19
  23.1 71.4 %collective-permute-start.9 = (f32[1,8,128,128]{3,2,1,0:T(8,128)}, f32[1,8,128,128]{3,2,1,0:T(8,128)}, u32[]{:S(2)}, u32[]{:S(2)}) collective-permute-start(f32[1,8,128,128]{3,2,1,0:T(8,128)} %get-tuple-element.34), channel_id=1, source_target_pairs={{0,1},{1,2},{2,3},{3,4},{4,5},{5,6},{6,7},{8,9},{9,10},{10,11},{11... | collective-permute-start | bytes 1572872 | tf_op jit(solution)/shard_map/ppermute | solution.py:19
  30.9 35.5 %copy-start.3 = (f32[2,8,128,128]{3,2,1,0:T(8,128)}, f32[2,8,128,128]{3,2,1,0:T(8,128)S(1)}, u32[]{:S(2)}) copy-start(f32[2,8,128,128]{3,2,1,0:T(8,128)S(1)} %get-tuple-element.19) | copy-start | bytes 3145732
  31.0 5.3 %collective-permute-start.4 = (f32[1,8,128,128]{3,2,1,0:T(8,128)S(1)}, f32[1,8,128,128]{3,2,1,0:T(8,128)S(1)}, u32[]{:S(2)}, u32[]{:S(2)}) collective-permute-start(f32[1,8,128,128]{3,2,1,0:T(8,128)S(1)} %get-tuple-element.31), channel_id=1, source_target_pairs={{1,0},{2,1},{3,2},{4,3},{5,4},{6,5},{7,6},{9,8},{10,9},{11,10},{12... | collective-permute-start | bytes 1572872 | tf_op jit(solution)/shard_map/ppermute | solution.py:22
  32.5 4.8 %collective-permute-start.5 = (f32[1,8,128,128]{3,2,1,0:T(8,128)S(1)}, f32[1,8,128,128]{3,2,1,0:T(8,128)S(1)}, u32[]{:S(2)}, u32[]{:S(2)}) collective-permute-start(f32[1,8,128,128]{3,2,1,0:T(8,128)S(1)} %get-tuple-element.30), channel_id=1, source_target_pairs={{0,1},{1,2},{2,3},{3,4},{4,5},{5,6},{6,7},{8,9},{9,10},{10,11},{11... | collective-permute-start | bytes 1572872 | tf_op jit(solution)/shard_map/ppermute | solution.py:19
  68.0 26.5 %collective-permute-start.8 = (f32[1,8,128,128]{3,2,1,0:T(8,128)}, f32[1,8,128,128]{3,2,1,0:T(8,128)}, u32[]{:S(2)}, u32[]{:S(2)}) collective-permute-start(f32[1,8,128,128]{3,2,1,0:T(8,128)} %get-tuple-element.35), channel_id=1, source_target_pairs={{1,0},{2,1},{3,2},{4,3},{5,4},{6,5},{7,6},{9,8},{10,9},{11,10},{12... | collective-permute-start | bytes 1572872 | tf_op jit(solution)/shard_map/ppermute | solution.py:22
  87.1 7.4 %collective-permute-start.6 = (f32[1,8,128,128]{3,2,1,0:T(8,128)S(1)}, f32[1,8,128,128]{3,2,1,0:T(8,128)S(1)}, u32[]{:S(2)}, u32[]{:S(2)}) collective-permute-start(f32[1,8,128,128]{3,2,1,0:T(8,128)S(1)} %get-tuple-element.29), channel_id=1, source_target_pairs={{1,0},{2,1},{3,2},{4,3},{5,4},{6,5},{7,6},{9,8},{10,9},{11,10},{12... | collective-permute-start | bytes 1572872 | tf_op jit(solution)/shard_map/ppermute | solution.py:22
  88.4 6.1 %collective-permute-start.7 = (f32[1,8,128,128]{3,2,1,0:T(8,128)S(1)}, f32[1,8,128,128]{3,2,1,0:T(8,128)S(1)}, u32[]{:S(2)}, u32[]{:S(2)}) collective-permute-start(f32[1,8,128,128]{3,2,1,0:T(8,128)S(1)} %get-tuple-element.28), channel_id=1, source_target_pairs={{0,1},{1,2},{2,3},{3,4},{4,5},{5,6},{6,7},{8,9},{9,10},{10,11},{11... | collective-permute-start | bytes 1572872 | tf_op jit(solution)/shard_map/ppermute | solution.py:19
  118.6 15.3 %copy-start.19 = (f32[8]{0:T(128)S(1)}, f32[8]{0:T(128)}, u32[]{:S(2)}) copy-start(f32[8]{0:T(128)} %param.11) | copy-start | bytes 100
  137.7 5.0 %collective-permute-start.10 = (f32[1,8,128,128]{3,2,1,0:T(8,128)S(1)}, f32[1,8,128,128]{3,2,1,0:T(8,128)S(1)}, u32[]{:S(2)}, u32[]{:S(2)}) collective-permute-start(f32[1,8,128,128]{3,2,1,0:T(8,128)S(1)} %get-tuple-element.27), channel_id=1, source_target_pairs={{1,0},{2,1},{3,2},{4,3},{5,4},{6,5},{7,6},{9,8},{10,9},{11,10},{12... | collective-permute-start | bytes 1572872 | tf_op jit(solution)/shard_map/ppermute | solution.py:22
  139.0 4.7 %collective-permute-start.11 = (f32[1,8,128,128]{3,2,1,0:T(8,128)S(1)}, f32[1,8,128,128]{3,2,1,0:T(8,128)S(1)}, u32[]{:S(2)}, u32[]{:S(2)}) collective-permute-start(f32[1,8,128,128]{3,2,1,0:T(8,128)S(1)} %get-tuple-element.26), channel_id=1, source_target_pairs={{0,1},{1,2},{2,3},{3,4},{4,5},{5,6},{6,7},{8,9},{9,10},{10,11},{11... | collective-permute-start | bytes 1572872 | tf_op jit(solution)/shard_map/ppermute | solution.py:19
  144.7 33.3 %copy-start.4 = (f32[2,8,128,128]{3,2,1,0:T(8,128)}, f32[2,8,128,128]{3,2,1,0:T(8,128)S(1)}, u32[]{:S(2)}) copy-start(f32[2,8,128,128]{3,2,1,0:T(8,128)S(1)} %get-tuple-element.12) | copy-start | bytes 3145732
  179.6 5.0 %collective-permute-start.12 = (f32[1,8,128,128]{3,2,1,0:T(8,128)S(1)}, f32[1,8,128,128]{3,2,1,0:T(8,128)S(1)}, u32[]{:S(2)}, u32[]{:S(2)}) collective-permute-start(f32[1,8,128,128]{3,2,1,0:T(8,128)S(1)} %get-tuple-element.25), channel_id=1, source_target_pairs={{1,0},{2,1},{3,2},{4,3},{5,4},{6,5},{7,6},{9,8},{10,9},{11,10},{12... | collective-permute-start | bytes 1572872 | tf_op jit(solution)/shard_map/ppermute | solution.py:22
  180.9 4.7 %collective-permute-start.13 = (f32[1,8,128,128]{3,2,1,0:T(8,128)S(1)}, f32[1,8,128,128]{3,2,1,0:T(8,128)S(1)}, u32[]{:S(2)}, u32[]{:S(2)}) collective-permute-start(f32[1,8,128,128]{3,2,1,0:T(8,128)S(1)} %get-tuple-element.24), channel_id=1, source_target_pairs={{0,1},{1,2},{2,3},{3,4},{4,5},{5,6},{6,7},{8,9},{9,10},{10,11},{11... | collective-permute-start | bytes 1572872 | tf_op jit(solution)/shard_map/ppermute | solution.py:19
  208.7 5.3 %collective-permute-start.14 = (f32[1,16,128,128]{3,2,1,0:T(8,128)S(1)}, f32[1,16,128,128]{3,2,1,0:T(8,128)S(1)}, u32[]{:S(2)}, u32[]{:S(2)}) collective-permute-start(f32[1,16,128,128]{3,2,1,0:T(8,128)S(1)} %get-tuple-element.22), channel_id=1, source_target_pairs={{1,0},{2,1},{3,2},{4,3},{5,4},{6,5},{7,6},{9,8},{10,9},{11,10},{12... | collective-permute-start | bytes 3145736 | tf_op jit(solution)/shard_map/ppermute | solution.py:22
  210.0 5.3 %collective-permute-start.15 = (f32[1,16,128,128]{3,2,1,0:T(8,128)S(1)}, f32[1,16,128,128]{3,2,1,0:T(8,128)S(1)}, u32[]{:S(2)}, u32[]{:S(2)}) collective-permute-start(f32[1,16,128,128]{3,2,1,0:T(8,128)S(1)} %get-tuple-element.23), channel_id=1, source_target_pairs={{0,1},{1,2},{2,3},{3,4},{4,5},{5,6},{6,7},{8,9},{9,10},{10,11},{11... | collective-permute-start | bytes 3145736 | tf_op jit(solution)/shard_map/ppermute | solution.py:19
  (14 other events, 56.4 us)
Sparse Core Ops, SparseCore 0:
  217.8 56.2 all-reduce.35
where the time goes:
time: 283 us; the launch traced here: 282 us
  blocking collectives  130 us (46%)
  waiting for transfers between devices  60.6 us (21%)
  starting transfers between devices  39.3 us (14%)
  other arithmetic  31.2 us (11%)
  between operations  14.7 us (5%)
  local copies, waits for them, and re-layouts  7.01 us (2%)
    psum x6, blocking collectives, pattern_sum(): return lax.psum(local_terms, 'vox')  117 us
    psum x1, waiting for transfers between devices, per_device(): gradient = lax.psum(local_gradient, 'pat')  56.4 us
    ppermute x8, starting transfers between devices, extended(): lax.ppermute(lax.slice_in_dim(block, block.shape[dim] - width, None, axis...  28.6 us
    psum x1, blocking collectives, per_device(): predicted = lax.psum(inner(probe_weights, forward), 'vox')  12.4 us
    ppermute x8, starting transfers between devices, extended(): lax.ppermute(lax.slice_in_dim(block, 0, width, axis=dim), axis, backward)  10.6 us
    reduce_sum x7, other arithmetic, inner(): return jnp.sum(left_factor * right_factor, axis=(0, 2, 3))  8.68 us
  transfers between devices with their start and end apart: 17, of which 5 were waited for; matrix products, arithmetic and copies ran while one was open for 6% of the time, Pallas kernels for 0%

commit v1 on v0

--- a/solution.py
+++ b/solution.py
@@ -1,14 +1,373 @@
+import functools
 import math
 
 import jax
 import jax.numpy as jnp
 from jax import lax
+from jax.experimental import pallas as pl
+from jax.experimental.pallas import tpu as pltpu
 from jax.sharding import PartitionSpec as P
 
 ITERS = 2
 
 
 leakage = 0.05
+
+CORES = 2
+SPARE = 8
+
+VMEM = pl.BlockSpec(memory_space=pltpu.VMEM)
+SMEM = pl.BlockSpec(memory_space=pltpu.SMEM)
+
+
+def call(body, out_shape, scratch=(), smem=0, smem_out=0, operands=()):
+    single = not isinstance(out_shape, (tuple, list))
+    outs = [out_shape] if single else list(out_shape)
+    specs = [VMEM] * (len(outs) - smem_out) + [SMEM] * smem_out
+    moved = sum(4 * a.size for a in operands) + sum(4 * o.size for o in outs)
+    return pl.pallas_call(
+        body,
+        out_shape=outs[0] if single else outs,
+        in_specs=[SMEM] * smem + [VMEM] * (len(operands) - smem),
+        out_specs=specs[0] if single else specs,
+        scratch_shapes=list(scratch),
+        cost_estimate=pl.CostEstimate(flops=8 * moved, bytes_accessed=moved, transcendentals=0),
+    )(*operands)
+
+
+def shape(*dims):
+    return jax.ShapeDtypeStruct(dims, jnp.float32)
+
+
+def total(acc):
+    return jnp.sum(acc, keepdims=True)
+
+
+def fold(plane):
+    rows, columns = plane.shape
+    return jnp.sum(plane.reshape(rows // 8, 8, columns), axis=0)
+
+
+def ahead(plane, axis):
+    return pltpu.roll(plane, plane.shape[axis] - 1, axis)
+
+
+def behind(plane, axis):
+    return pltpu.roll(plane, 1, axis)
+
+
+def split_kernel(place, forward, adjoint, forward_out, adjoint_out):
+    chips = forward_out.shape[1]
+    first = (1 - place[1]) * chips
+    forward_out[...] = forward[:, pl.ds(first, chips)]
+    adjoint_out[...] = adjoint[:, pl.ds(first, chips)]
+
+
+def pack_kernel(place, field, got, *outs):
+    chips = len(outs)
+    planes = field.shape[0]
+    chip, core = place[0], place[1]
+    for step, out in enumerate(outs):
+        other = chip ^ step
+        for plane in range(planes):
+            out[core * planes + plane] = field[plane, core * chips + other]
+            out[(1 - core) * planes + plane] = got[plane, other]
+
+
+def coefficient_kernel(place, own, others, depth, rows, columns, inverse, sigma):
+    chips, planes = own.shape[:2]
+    chip, core = place[0], place[1]
+    per_chip = CORES * planes
+    for step in range(chips):
+        base = (chip ^ step) * per_chip
+        for plane in range(planes):
+            sigma[base + core * planes + plane] = own[step, plane]
+            sigma[base + (1 - core) * planes + plane] = others[step, plane]
+    count, height, width = sigma.shape
+    row_open = lax.broadcasted_iota(jnp.int32, (height, width), 0) < height - 1
+    column_open = lax.broadcasted_iota(jnp.int32, (height, width), 1) < width - 1
+
+    def step(level, below):
+        here = sigma[level]
+        above = sigma[jnp.minimum(level + 1, count - 1)]
+        face_depth = jnp.where(level < count - 1, 0.5, 0.0) * (here + above)
+        face_row = jnp.where(row_open, 0.5 * (here + ahead(here, 0)), 0.0)
+        face_column = jnp.where(column_open, 0.5 * (here + ahead(here, 1)), 0.0)
+        depth[level] = face_depth
+        rows[level] = face_row
+        columns[level] = face_column
+        diagonal = (
+            leakage
+            + (below + face_depth)
+            + (face_row + behind(face_row, 0))
+            + (face_column + behind(face_column, 1))
+        )
+        inverse[level] = 1.0 / diagonal
+        return face_depth
+
+    lax.fori_loop(0, count, step, jnp.zeros((height, width), jnp.float32))
+
+
+def applied_planes(vector, depth, rows, columns, body, start):
+    count, height, width = vector.shape
+
+    def step(level, carry):
+        here, below, rest = carry
+        above = vector[jnp.minimum(level + 1, count - 1)]
+        flux_depth = depth[level] * (above - here)
+        flux_row = rows[level] * (ahead(here, 0) - here)
+        flux_column = columns[level] * (ahead(here, 1) - here)
+        result = leakage * here + (below - flux_depth)
+        result = result + (behind(flux_row, 0) - flux_row)
+        result = result + (behind(flux_column, 1) - flux_column)
+        return above, flux_depth, body(level, here, result, rest)
+
+    zero = jnp.zeros((height, width), jnp.float32)
+    return lax.fori_loop(0, count, step, (vector[0], zero, start))[2]
+
+
+def add_at(ref, cell, value):
+    count, height, width = ref.shape
+    column = cell % width
+    row = (cell // width) % height
+    level = cell // (width * height)
+    lane = lax.broadcasted_iota(jnp.int32, (1, width), 1)
+    ref[level, pl.ds(row, 1), :] += jnp.where(lane == column, value, 0.0)
+
+
+def value_at(ref, cell):
+    count, height, width = ref.shape
+    column = cell % width
+    row = (cell // width) % height
+    level = cell // (width * height)
+    lane = lax.broadcasted_iota(jnp.int32, (1, width), 1)
+    return total(jnp.where(lane == column, ref[level, pl.ds(row, 1), :], 0.0))
+
+
+def gather_blocks(chip, blocks, field):
+    for step, block in enumerate(blocks):
+        field[pl.ds((chip ^ step) * block.shape[0], block.shape[0])] = block[...]
+
+
+def solve_in_place(field, depth, rows, columns, inverse, residue, precond, applied, direction, end):
+    count, height, width = field.shape
+    nothing = jnp.zeros((8, width), jnp.float32)
+
+    def first(level, here, product, acc):
+        left = residue[level] - product
+        scaled = left * inverse[level]
+        residue[level] = left
+        precond[level] = scaled
+        return acc + fold(left * scaled)
+
+    current = total(applied_planes(field, depth, rows, columns, first, nothing))
+
+    def second(level, here, product, acc):
+        applied[level] = product
+        return acc + fold(here * product)
+
+    step_size = current / total(applied_planes(precond, depth, rows, columns, second, nothing))
+
+    def third(level, acc):
+        left = residue[level] - step_size * applied[level]
+        scaled = left * inverse[level]
+        direction[level] = scaled
+        return acc + fold(left * scaled)
+
+    following = total(lax.fori_loop(0, count, third, nothing))
+    ratio = following / current
+
+    def fourth(level, carry):
+        before, acc = carry
+        here = direction[level] + ratio * precond[level]
+        direction[level] = here
+        along_depth = here - before
+        along_row = ahead(here, 0) - here
+        along_column = ahead(here, 1) - here
+        face_depth = jnp.where(level > 0, depth[jnp.maximum(level - 1, 0)], 0.0)
+        terms = leakage * here * here + face_depth * along_depth * along_depth
+        terms = terms + rows[level] * along_row * along_row
+        terms = terms + columns[level] * along_column * along_column
+        return here, acc + fold(terms)
+
+    zero = jnp.zeros((height, width), jnp.float32)
+    energy = total(lax.fori_loop(0, count, fourth, (zero, nothing))[1])
+    last_size = following / energy
+
+    def fifth(level, carry):
+        end(level, field[level] + step_size * precond[level] + last_size * direction[level])
+        return carry
+
+    lax.fori_loop(0, count, fifth, 0)
+
+
+def electrode(place, electrodes, patterns, which):
+    return electrodes[patterns[place[2], which]]
+
+
+def clear(ref):
+    def step(level, carry):
+        ref[level] = jnp.zeros(ref.shape[1:], ref.dtype)
+        return carry
+
+    lax.fori_loop(0, ref.shape[0], step, 0)
+
+
+def forward_kernel(
+    strength, chips, place, electrodes, patterns, *refs
+):
+    depth, rows, columns, inverse = refs[:4]
+    blocks = refs[4 : 4 + chips]
+    result, voltage, field, residue, precond, applied, direction = refs[4 + chips :]
+    gather_blocks(place[0], blocks, field)
+    clear(residue)
+    add_at(residue, electrode(place, electrodes, patterns, 0), strength)
+    add_at(residue, electrode(place, electrodes, patterns, 1), -strength)
+
+    def end(level, plane):
+        result[level] = plane
+
+    solve_in_place(
+        field, depth, rows, columns, inverse, residue, precond, applied, direction, end
+    )
+    plus = value_at(result, electrode(place, electrodes, patterns, 2))
+    minus = value_at(result, electrode(place, electrodes, patterns, 3))
+    voltage[...] = jnp.broadcast_to(plus - minus, voltage.shape)
+
+
+def adjoint_kernel(
+    weight, chips, place, electrodes, patterns, observed, *refs
+):
+    depth, rows, columns, inverse, forward, voltage = refs[:6]
+    blocks = refs[6 : 6 + chips]
+    kept, given, field, residue, precond, applied, direction = refs[6 + chips :]
+    chip, core = place[0], place[1]
+    gather_blocks(chip, blocks, field)
+    clear(residue)
+    weighted = weight * (voltage[0:1, :] - observed[place[2]])
+    add_at(residue, electrode(place, electrodes, patterns, 2), weighted)
+    add_at(residue, electrode(place, electrodes, patterns, 3), -weighted)
+
+    def end(level, plane):
+        field[level] = plane
+
+    solve_in_place(
+        field, depth, rows, columns, inverse, residue, precond, applied, direction, end
+    )
+    count, height, width = field.shape
+    planes = count // (CORES * chips)
+    row_open = lax.broadcasted_iota(jnp.int32, (height, width), 0) < height - 1
+    column_open = lax.broadcasted_iota(jnp.int32, (height, width), 1) < width - 1
+
+    def step(level, below):
+        left, right = forward[level], field[level]
+        above = jnp.minimum(level + 1, count - 1)
+        product_depth = (forward[above] - left) * (field[above] - right)
+        product_row = (ahead(left, 0) - left) * (ahead(right, 0) - right)
+        product_row = jnp.where(row_open, product_row, 0.0)
+        product_column = (ahead(left, 1) - left) * (ahead(right, 1) - right)
+        product_column = jnp.where(column_open, product_column, 0.0)
+        plane = -0.5 * (
+            (below + product_depth)
+            + (product_row + behind(product_row, 0))
+            + (product_column + behind(product_column, 1))
+        )
+        block = (level // (CORES * planes)) ^ chip
+        owner = (level // planes) % CORES
+        start = pl.multiple_of((level % planes) * height, height)
+
+        @pl.when(owner == core)
+        def _():
+            kept[block, pl.ds(start, height), :] = plane
+
+        @pl.when(owner != core)
+        def _():
+            given[block, pl.ds(start, height), :] = plane
+
+        return product_depth
+
+    lax.fori_loop(0, count, step, jnp.zeros((height, width), jnp.float32))
+    lane = lax.broadcasted_iota(jnp.int32, (SPARE, width), 1)
+    note = jnp.where(lane == place[2], voltage[...], 0.0)
+    for block in range(chips):
+        kept[block, planes * height :, :] = note
+        given[block, planes * height :, :] = note
+
+
+def swap(values, axis, size, bit):
+    return lax.ppermute(values, axis, [(i, i ^ bit) for i in range(size)])
+
+
+def per_device_exchanged(
+    conductivity, warm_forward, warm_adjoint, electrodes, patterns, observed
+):
+    plane_count, pattern_count, row_count, column_count = warm_forward.shape
+    layers = lax.axis_size("vox")
+    groups = lax.axis_size("pat")
+    chips = layers // CORES
+    strength = 2.0 * math.sqrt(layers * plane_count * row_count * column_count)
+    position = lax.axis_index("vox")
+    chip, core = position // CORES, position % CORES
+    place = jnp.stack([chip, core, core * chips + chip]).astype(jnp.int32)
+    levels = layers * plane_count
+    whole = (levels, row_count, column_count)
+
+    sigma = [conductivity] + [
+        swap(conductivity, "vox", layers, CORES * step) for step in range(1, chips)
+    ]
+    half = shape(plane_count, chips, row_count, column_count)
+    give_forward, give_adjoint = call(
+        split_kernel, [half, half], smem=1, operands=(place, warm_forward, warm_adjoint)
+    )
+
+    def exchanged(field, give):
+        got = swap(give, "vox", layers, 1)
+        part = shape(CORES * plane_count, row_count, column_count)
+        packed = call(pack_kernel, [part] * chips, smem=1, operands=(place, field, got))
+        return [packed[0]] + [
+            swap(packed[step], "vox", layers, CORES * step) for step in range(1, chips)
+        ]
+
+    forward_blocks = exchanged(warm_forward, give_forward)
+    adjoint_blocks = exchanged(warm_adjoint, give_adjoint)
+    own_sigma = jnp.stack(sigma)
+    other_sigma = swap(own_sigma, "vox", layers, 1)
+    coefficients = call(
+        coefficient_kernel,
+        [shape(*whole)] * 4,
+        scratch=[pltpu.VMEM(whole, jnp.float32)],
+        smem=1,
+        operands=(place, own_sigma, other_sigma),
+    )
+    scratch = [pltpu.VMEM(whole, jnp.float32)] * 5
+    forward, voltage = call(
+        functools.partial(forward_kernel, strength, chips),
+        [shape(*whole), shape(SPARE, column_count)],
+        scratch=scratch,
+        smem=3,
+        operands=(place, electrodes, patterns, *coefficients, *forward_blocks),
+    )
+    block = plane_count * row_count + SPARE
+    kept, given = call(
+        functools.partial(adjoint_kernel, 0.1 * strength, chips),
+        [shape(chips, block, column_count)] * 2,
+        scratch=scratch,
+        smem=4,
+        operands=(
+            place, electrodes, patterns, observed, *coefficients, forward, voltage, *adjoint_blocks
+        ),
+    )
+    summed = kept + swap(given, "vox", layers, 1)
+    mine = summed[0]
+    for step in range(1, chips):
+        mine = mine + swap(summed[step], "vox", layers, CORES * step)
+    predicted = mine[plane_count * row_count, :pattern_count]
+    gradient = mine[: plane_count * row_count].reshape(plane_count, row_count, column_count)
+    bit = 1
+    while bit < groups:
+        gradient = gradient + swap(gradient, "pat", groups, bit)
+        bit *= 2
+    return gradient, predicted
 
 
 def extended(block, sides, width):
@@ -83,7 +442,7 @@
     return solution
 
 
-def per_device(conductivity, warm_forward, warm_adjoint, electrodes, patterns, observed):
+def per_device_in_place(conductivity, warm_forward, warm_adjoint, electrodes, patterns, observed):
     plane_count, pattern_count, row_count, column_count = warm_forward.shape
     position = lax.axis_index("vox")
     layers = lax.axis_size("vox")
@@ -156,6 +515,15 @@
     return (gradient, predicted)
 
 
+def per_device(conductivity, warm_forward, *rest):
+    size = lax.axis_size("vox")
+    groups = lax.axis_size("pat")
+    exchange = warm_forward.shape[1] == size and size % CORES == 0
+    exchange = exchange and size & (size - 1) == 0 and groups & (groups - 1) == 0
+    form = per_device_exchanged if exchange else per_device_in_place
+    return form(conductivity, warm_forward, *rest)
+
+
 def solution(mesh):
     in_specs = (
         P("vox", None, None),

time: 283 us -> 92.8 us (0.33)
  blocking collectives: 130 us -> 0 us
  Pallas kernels: 0 us -> 39.4 us
  waiting for transfers between devices: 60.6 us -> 25.9 us
  other arithmetic: 31.2 us -> 2.43 us
  starting transfers between devices: 39.3 us -> 19.4 us
  between operations: 14.7 us -> 0.8 us
    psum x7 -> x0, blocking collectives: 130 us -> none  [the longest x6 117 us: pattern_sum(): return lax.psum(local_terms, 'vox')]
    psum x1 -> x0, waiting for transfers between devices: 56.4 us -> none  [per_device(): gradient = lax.psum(local_gradient, 'pat')]
    pallas_call x0 -> x6, Pallas kernels: none -> 39.4 us  [call(): pl.pallas_call(body, out_shape=outs[0] if single else outs, in_specs=[SME...]
    ppermute x16 -> x18, waiting for transfers between devices: 4.17 us -> 25.9 us  [swap(): return lax.ppermute(values, axis, [(i, i ^ bit) for i in range(size)])]
    ppermute x16 -> x18, starting transfers between devices: 39.2 us -> 19.4 us  [swap(): return lax.ppermute(values, axis, [(i, i ^ bit) for i in range(size)])]
    mul x23 -> x0, other arithmetic: 10.6 us -> none  [the longest x5 4.72 us: operate(): flux_depth = depth_faces[:, None] * (padded[1:] - padded[:-1])]
    reduce_sum x11 -> x0, other arithmetic: 10.4 us -> none  [the longest x7 8.68 us: inner(): return jnp.sum(left_factor * right_factor, axis=(0, 2, 3))]
    div x8 -> x0, other arithmetic: 4.6 us -> none  [the longest x2 4.56 us: solve_pattern(): precond = residue / diagonal]
  transfers between devices with their start and end apart: 17 -> 18, of which waited for: 5 -> 10; matrix products, arithmetic and copies ran while one was open for 6% -> 1% of each run, Pallas kernels for 0% -> 24%
where the time goes in v1:
time: 92.8 us; the launch traced here: 92.5 us
  Pallas kernels  39.4 us (42%)
  waiting for transfers between devices  25.9 us (28%)
  starting transfers between devices  19.4 us (21%)
  local copies, waits for them, and re-layouts  4.58 us (5%)
  other arithmetic  2.43 us (3%)
    pallas_call x6, Pallas kernels, call(): pl.pallas_call(body, out_shape=outs[0] if single else outs, in_specs=[SME...  39.4 us
    ppermute x18, waiting for transfers between devices, swap(): return lax.ppermute(values, axis, [(i, i ^ bit) for i in range(size)])  25.9 us
    ppermute x18, starting transfers between devices, swap(): return lax.ppermute(values, axis, [(i, i ^ bit) for i in range(size)])  19.4 us
    unnamed x25, local copies, waits for them, and re-layouts  4.03 us
  transfers between devices with their start and end apart: 18, of which 10 were waited for; matrix products, arithmetic and copies ran while one was open for 1% of the time, Pallas kernels for 24%

profile of v1, /device:TPU:0, one launch (start us, length us, event | category | flops | bytes accessed | tf_op | source)
XLA Modules:
  0.0 92.5 jit_solution(1785959938758452180)
XLA Ops:
  1.2 2.7 %shard_map.78 = (f32[2,4,128,128]{3,2,1,0:T(8,128)}, f32[2,4,128,128]{3,2,1,0:T(8,128)}) custom-call(s32[3]{0:T(128)} %pad_add_fusion.place, f32[2,8,128,128]{3,2,1,0:T(8,128)} %field.2, f32[2,8,128,128]{3,2,1,0:T(8,128)} %field.3), custom_call_target="tpu_custom_call" | custom-call | flops 25165920 | bytes 3145740 | tf_op jit(solution)/shard_map/pallas_call | solution.py:28
  4.4 2.5 %collective-permute-start = (f32[2,128,128]{2,1,0:T(8,128)S(1)}, f32[2,128,128]{2,1,0:T(8,128)S(1)}, u32[]{:S(2)}, u32[]{:S(2)}) collective-permute-start(f32[2,128,128]{2,1,0:T(8,128)S(1)} %copy-done.10), channel_id=1, source_target_pairs={{0,2},{1,3},{2,0},{3,1},{4,6},{5,7},{6,4},{7,5},{8,10},{9,11},{10,... | collective-permute-start | bytes 393224 | tf_op jit(solution)/shard_map/ppermute | solution.py:298
  6.9 1.5 %collective-permute-start.2 = (f32[2,128,128]{2,1,0:T(8,128)S(1)}, f32[2,128,128]{2,1,0:T(8,128)S(1)}, u32[]{:S(2)}, u32[]{:S(2)}) collective-permute-start(f32[2,128,128]{2,1,0:T(8,128)S(1)} %copy-done.10), channel_id=1, source_target_pairs={{0,6},{1,7},{2,4},{3,5},{4,2},{5,3},{6,0},{7,1},{8,14},{9,15},{10,... | collective-permute-start | bytes 393224 | tf_op jit(solution)/shard_map/ppermute | solution.py:298
  8.4 2.8 %collective-permute-done = f32[2,128,128]{2,1,0:T(8,128)S(1)} collective-permute-done((f32[2,128,128]{2,1,0:T(8,128)S(1)}, f32[2,128,128]{2,1,0:T(8,128)S(1)}, u32[]{:S(2)}, u32[]{:S(2)}) %collective-permute-start) | collective-permute-done | bytes 131104 | tf_op jit(solution)/shard_map/ppermute | solution.py:298
  11.2 3.9 %collective-permute-done.2 = f32[2,128,128]{2,1,0:T(8,128)S(1)} collective-permute-done((f32[2,128,128]{2,1,0:T(8,128)S(1)}, f32[2,128,128]{2,1,0:T(8,128)S(1)}, u32[]{:S(2)}, u32[]{:S(2)}) %collective-permute-start.2) | collective-permute-done | bytes 131104 | tf_op jit(solution)/shard_map/ppermute | solution.py:298
  15.1 1.4 %collective-permute-done.1 = f32[2,128,128]{2,1,0:T(8,128)S(1)} collective-permute-done((f32[2,128,128]{2,1,0:T(8,128)S(1)}, f32[2,128,128]{2,1,0:T(8,128)S(1)}, u32[]{:S(2)}, u32[]{:S(2)}) %collective-permute-start.1) | collective-permute-done | bytes 131104 | tf_op jit(solution)/shard_map/ppermute | solution.py:298
  17.6 2.4 %shard_map.79 = (f32[4,128,128]{2,1,0:T(8,128)}, f32[4,128,128]{2,1,0:T(8,128)}, f32[4,128,128]{2,1,0:T(8,128)}, f32[4,128,128]{2,1,0:T(8,128)}) custom-call(s32[3]{0:T(128)} %pad_add_fusion.place, f32[2,8,128,128]{3,2,1,0:T(8,128)} %field.2, f32[2,4,128,128]{3,2,1,0:T(8,128)} %copy-done.2), custom_call_target="tpu_custom_call" | custom-call | flops 20971616 | bytes 2621452 | tf_op jit(solution)/shard_map/pallas_call | solution.py:28
  20.0 1.5 %collective-permute-start.5 = (f32[4,128,128]{2,1,0:T(8,128)}, f32[4,128,128]{2,1,0:T(8,128)S(1)}, u32[]{:S(2)}, u32[]{:S(2)}) collective-permute-start(f32[4,128,128]{2,1,0:T(8,128)} %get-tuple-element.26), channel_id=1, source_target_pairs={{0,2},{1,3},{2,0},{3,1},{4,6},{5,7},{6,4},{7,5},{8,10},{9,11},{10,... | collective-permute-start | bytes 786440 | tf_op jit(solution)/shard_map/ppermute | solution.py:298
  22.0 1.5 %collective-permute-start.7 = (f32[4,128,128]{2,1,0:T(8,128)}, f32[4,128,128]{2,1,0:T(8,128)S(1)}, u32[]{:S(2)}, u32[]{:S(2)}) collective-permute-start(f32[4,128,128]{2,1,0:T(8,128)} %get-tuple-element.28), channel_id=1, source_target_pairs={{0,6},{1,7},{2,4},{3,5},{4,2},{5,3},{6,0},{7,1},{8,14},{9,15},{10,... | collective-permute-start | bytes 786440 | tf_op jit(solution)/shard_map/ppermute | solution.py:298
  24.3 2.4 %shard_map.81 = (f32[4,128,128]{2,1,0:T(8,128)}, f32[4,128,128]{2,1,0:T(8,128)}, f32[4,128,128]{2,1,0:T(8,128)}, f32[4,128,128]{2,1,0:T(8,128)}) custom-call(s32[3]{0:T(128)} %pad_add_fusion.place, f32[2,8,128,128]{3,2,1,0:T(8,128)} %field.3, f32[2,4,128,128]{3,2,1,0:T(8,128)} %copy-done.1), custom_call_target="tpu_custom_call" | custom-call | flops 20971616 | bytes 2621452 | tf_op jit(solution)/shard_map/pallas_call | solution.py:28
  26.7 1.5 %collective-permute-start.9 = (f32[4,128,128]{2,1,0:T(8,128)}, f32[4,128,128]{2,1,0:T(8,128)S(1)}, u32[]{:S(2)}, u32[]{:S(2)}) collective-permute-start(f32[4,128,128]{2,1,0:T(8,128)} %get-tuple-element.33), channel_id=1, source_target_pairs={{0,2},{1,3},{2,0},{3,1},{4,6},{5,7},{6,4},{7,5},{8,10},{9,11},{10,... | collective-permute-start | bytes 786440 | tf_op jit(solution)/shard_map/ppermute | solution.py:298
  29.4 1.4 %collective-permute-start.11 = (f32[4,128,128]{2,1,0:T(8,128)}, f32[4,128,128]{2,1,0:T(8,128)S(1)}, u32[]{:S(2)}, u32[]{:S(2)}) collective-permute-start(f32[4,128,128]{2,1,0:T(8,128)} %get-tuple-element.35), channel_id=1, source_target_pairs={{0,6},{1,7},{2,4},{3,5},{4,2},{5,3},{6,0},{7,1},{8,14},{9,15},{10,... | collective-permute-start | bytes 786440 | tf_op jit(solution)/shard_map/ppermute | solution.py:298
  31.5 5.8 %shard_map.77 = (f32[16,128,128]{2,1,0:T(8,128)}, f32[16,128,128]{2,1,0:T(8,128)}, f32[16,128,128]{2,1,0:T(8,128)}, f32[16,128,128]{2,1,0:T(8,128)}) custom-call(s32[3]{0:T(128)} %pad_add_fusion.place, f32[4,2,128,128]{3,2,1,0:T(8,128)} %copy-done, f32[4,2,128,128]{3,2,1,0:T(8,128)} %copy-done.3), custom_call_target="tpu_custom_call" | custom-call | flops 41943136 | bytes 5242892 | tf_op jit(solution)/shard_map/pallas_call | solution.py:28
  38.1 11.5 %shard_map.80 = (f32[16,128,128]{2,1,0:T(8,128)}, f32[8,128]{1,0:T(8,128)}) custom-call(s32[3]{0:T(128)} %pad_add_fusion.place, s32[128]{0:T(128)} %electrodes.3, s32[8,4]{1,0:T(8,128)} %copy.9.patterns, f32[16,128,128]{2,1,0:T(8,128)} %get-tuple-element.20.refs_0_, f32[16,128,128]{2,1,0:T(8,128)} %get-tuple-element.21.refs_1_, ...), custom_call_target="tpu_custom_call" | custom-call | flops 50369632 | bytes 6296204 | tf_op jit(solution)/shard_map/pallas_call | solution.py:28
  50.5 14.6 %shard_map.82 = (f32[4,264,128]{2,1,0:T(8,128)}, f32[4,264,128]{2,1,0:T(8,128)}) custom-call(s32[3]{0:T(128)} %pad_add_fusion.place, s32[128]{0:T(128)} %electrodes.3, s32[8,4]{1,0:T(8,128)} %copy.9.patterns, f32[8]{0:T(128)} %observed.1, f32[16,128,128]{2,1,0:T(8,128)} %get-tuple-element.20.refs_0_, f32[16,128,128]{2,1,0:T(8,128)} %get-tuple-element.21.refs_1_, ...), custom_call_target="tpu_custom_call" | custom-call | flops 59020640 | bytes 7377580 | tf_op jit(solution)/shard_map/pallas_call | solution.py:28
  65.1 2.1 %collective-permute-done.12 = f32[4,264,128]{2,1,0:T(8,128)S(1)} collective-permute-done((f32[4,264,128]{2,1,0:T(8,128)}, f32[4,264,128]{2,1,0:T(8,128)S(1)}, u32[]{:S(2)}, u32[]{:S(2)}) %collective-permute-start.12) | collective-permute-done | bytes 540704 | tf_op jit(solution)/shard_map/ppermute | solution.py:298
  69.4 2.1 %collective-permute-start.15 = (f32[264,128]{1,0:T(8,128)S(1)}, f32[264,128]{1,0:T(8,128)S(1)}, u32[]{:S(2)}, u32[]{:S(2)}) collective-permute-start(f32[264,128]{1,0:T(8,128)S(1)} %get-tuple-element.39), channel_id=1, source_target_pairs={{0,6},{1,7},{2,4},{3,5},{4,2},{5,3},{6,0},{7,1},{8,14},{9,15},{10,... | collective-permute-start | bytes 405512 | tf_op jit(solution)/shard_map/ppermute | solution.py:298
  72.0 3.0 %collective-permute-done.13 = f32[264,128]{1,0:T(8,128)S(1)} collective-permute-done((f32[264,128]{1,0:T(8,128)S(1)}, f32[264,128]{1,0:T(8,128)S(1)}, u32[]{:S(2)}, u32[]{:S(2)}) %collective-permute-start.13) | collective-permute-done | bytes 135200 | tf_op jit(solution)/shard_map/ppermute | solution.py:298
  74.9 3.1 %collective-permute-done.15 = f32[264,128]{1,0:T(8,128)S(1)} collective-permute-done((f32[264,128]{1,0:T(8,128)S(1)}, f32[264,128]{1,0:T(8,128)S(1)}, u32[]{:S(2)}, u32[]{:S(2)}) %collective-permute-start.15) | collective-permute-done | bytes 135200 | tf_op jit(solution)/shard_map/ppermute | solution.py:298
  78.1 1.4 %collective-permute-done.14 = f32[264,128]{1,0:T(8,128)S(1)} collective-permute-done((f32[264,128]{1,0:T(8,128)S(1)}, f32[264,128]{1,0:T(8,128)S(1)}, u32[]{:S(2)}, u32[]{:S(2)}) %collective-permute-start.14) | collective-permute-done | bytes 135200 | tf_op jit(solution)/shard_map/ppermute | solution.py:298
  79.5 1.6 %collective-permute-start.16 = (f32[2,128,128]{2,1,0:T(8,128)S(1)}, f32[2,128,128]{2,1,0:T(8,128)S(1)}, u32[]{:S(2)}, u32[]{:S(2)}) collective-permute-start(f32[2,128,128]{2,1,0:T(8,128)S(1)} %bitcast.24), channel_id=1, source_target_pairs={{0,8},{8,0},{16,24},{24,16},{1,9},{9,1},{17,25},{25,17},{2,10},{10... | collective-permute-start | bytes 393224 | tf_op jit(solution)/shard_map/ppermute | solution.py:298
  81.1 3.4 %collective-permute-done.16 = f32[2,128,128]{2,1,0:T(8,128)S(1)} collective-permute-done((f32[2,128,128]{2,1,0:T(8,128)S(1)}, f32[2,128,128]{2,1,0:T(8,128)S(1)}, u32[]{:S(2)}, u32[]{:S(2)}) %collective-permute-start.16) | collective-permute-done | bytes 131104 | tf_op jit(solution)/shard_map/ppermute | solution.py:298
  84.5 2.7 %collective-permute-start.17 = (f32[2,128,128]{2,1,0:T(8,128)S(1)}, f32[2,128,128]{2,1,0:T(8,128)S(1)}, u32[]{:S(2)}, u32[]{:S(2)}) collective-permute-start(f32[2,128,128]{2,1,0:T(8,128)S(1)} %add.32), channel_id=1, source_target_pairs={{0,16},{8,24},{16,0},{24,8},{1,17},{9,25},{17,1},{25,9},{2,18},{10... | collective-permute-start | bytes 393224 | tf_op jit(solution)/shard_map/ppermute | solution.py:298
  87.7 4.2 %collective-permute-done.17 = f32[2,128,128]{2,1,0:T(8,128)S(1)} collective-permute-done((f32[2,128,128]{2,1,0:T(8,128)S(1)}, f32[2,128,128]{2,1,0:T(8,128)S(1)}, u32[]{:S(2)}, u32[]{:S(2)}) %collective-permute-start.17) | collective-permute-done | bytes 131104 | tf_op jit(solution)/shard_map/ppermute | solution.py:298
  (52 shorter events, 10.8 us)
Async XLA Ops:
  1.2 3.2 %copy-start.10 = (f32[2,128,128]{2,1,0:T(8,128)S(1)}, f32[2,128,128]{2,1,0:T(8,128)}, u32[]{:S(2)}) copy-start(f32[2,128,128]{2,1,0:T(8,128)} %param.6) | copy-start | bytes 393220
  3.9 12.8 %collective-permute-start.4 = (f32[2,4,128,128]{3,2,1,0:T(8,128)}, f32[2,4,128,128]{3,2,1,0:T(8,128)S(1)}, u32[]{:S(2)}, u32[]{:S(2)}) collective-permute-start(f32[2,4,128,128]{3,2,1,0:T(8,128)} %get-tuple-element.24), channel_id=1, source_target_pairs={{0,1},{1,0},{2,3},{3,2},{4,5},{5,4},{6,7},{7,6},{8,9},{9,8},{10,11... | collective-permute-start | bytes 1572872 | tf_op jit(solution)/shard_map/ppermute | solution.py:298
  4.4 6.9 %collective-permute-start = (f32[2,128,128]{2,1,0:T(8,128)S(1)}, f32[2,128,128]{2,1,0:T(8,128)S(1)}, u32[]{:S(2)}, u32[]{:S(2)}) collective-permute-start(f32[2,128,128]{2,1,0:T(8,128)S(1)} %copy-done.10), channel_id=1, source_target_pairs={{0,2},{1,3},{2,0},{3,1},{4,6},{5,7},{6,4},{7,5},{8,10},{9,11},{10,... | collective-permute-start | bytes 393224 | tf_op jit(solution)/shard_map/ppermute | solution.py:298
  6.9 8.2 %collective-permute-start.2 = (f32[2,128,128]{2,1,0:T(8,128)S(1)}, f32[2,128,128]{2,1,0:T(8,128)S(1)}, u32[]{:S(2)}, u32[]{:S(2)}) collective-permute-start(f32[2,128,128]{2,1,0:T(8,128)S(1)} %copy-done.10), channel_id=1, source_target_pairs={{0,6},{1,7},{2,4},{3,5},{4,2},{5,3},{6,0},{7,1},{8,14},{9,15},{10,... | collective-permute-start | bytes 393224 | tf_op jit(solution)/shard_map/ppermute | solution.py:298
  8.4 8.1 %collective-permute-start.1 = (f32[2,128,128]{2,1,0:T(8,128)S(1)}, f32[2,128,128]{2,1,0:T(8,128)S(1)}, u32[]{:S(2)}, u32[]{:S(2)}) collective-permute-start(f32[2,128,128]{2,1,0:T(8,128)S(1)} %copy-done.10), channel_id=1, source_target_pairs={{0,4},{1,5},{2,6},{3,7},{4,0},{5,1},{6,2},{7,3},{8,12},{9,13},{10,... | collective-permute-start | bytes 393224 | tf_op jit(solution)/shard_map/ppermute | solution.py:298
  8.4 15.0 %collective-permute-start.8 = (f32[2,4,128,128]{3,2,1,0:T(8,128)}, f32[2,4,128,128]{3,2,1,0:T(8,128)S(1)}, u32[]{:S(2)}, u32[]{:S(2)}) collective-permute-start(f32[2,4,128,128]{3,2,1,0:T(8,128)} %get-tuple-element.31), channel_id=1, source_target_pairs={{0,1},{1,0},{2,3},{3,2},{4,5},{5,4},{6,7},{7,6},{8,9},{9,8},{10,11... | collective-permute-start | bytes 1572872 | tf_op jit(solution)/shard_map/ppermute | solution.py:298
  16.5 3.5 %copy-start = (f32[4,2,128,128]{3,2,1,0:T(8,128)}, f32[4,2,128,128]{3,2,1,0:T(8,128)S(1)}, u32[]{:S(2)}) copy-start(f32[4,2,128,128]{3,2,1,0:T(8,128)S(1)} %pad_maximum_fusion.own) | copy-start | bytes 1572868
  16.5 11.7 %collective-permute-start.3 = (f32[4,2,128,128]{3,2,1,0:T(8,128)S(1)}, f32[4,2,128,128]{3,2,1,0:T(8,128)S(1)}, u32[]{:S(2)}, u32[]{:S(2)}) collective-permute-start(f32[4,2,128,128]{3,2,1,0:T(8,128)S(1)} %pad_maximum_fusion.own), channel_id=1, source_target_pairs={{0,1},{1,0},{2,3},{3,2},{4,5},{5,4},{6,7},{7,6},{8,9},{9,8},{10,11... | collective-permute-start | bytes 1572872 | tf_op jit(solution)/shard_map/ppermute | solution.py:298
  16.6 0.9 copy-start.2
  20.0 9.4 %collective-permute-start.5 = (f32[4,128,128]{2,1,0:T(8,128)}, f32[4,128,128]{2,1,0:T(8,128)S(1)}, u32[]{:S(2)}, u32[]{:S(2)}) collective-permute-start(f32[4,128,128]{2,1,0:T(8,128)} %get-tuple-element.26), channel_id=1, source_target_pairs={{0,2},{1,3},{2,0},{3,1},{4,6},{5,7},{6,4},{7,5},{8,10},{9,11},{10,... | collective-permute-start | bytes 786440 | tf_op jit(solution)/shard_map/ppermute | solution.py:298
  21.5 15.8 %collective-permute-start.6 = (f32[4,128,128]{2,1,0:T(8,128)}, f32[4,128,128]{2,1,0:T(8,128)S(1)}, u32[]{:S(2)}, u32[]{:S(2)}) collective-permute-start(f32[4,128,128]{2,1,0:T(8,128)} %get-tuple-element.27), channel_id=1, source_target_pairs={{0,4},{1,5},{2,6},{3,7},{4,0},{5,1},{6,2},{7,3},{8,12},{9,13},{10,... | collective-permute-start | bytes 786440 | tf_op jit(solution)/shard_map/ppermute | solution.py:298
  22.0 15.3 %collective-permute-start.7 = (f32[4,128,128]{2,1,0:T(8,128)}, f32[4,128,128]{2,1,0:T(8,128)S(1)}, u32[]{:S(2)}, u32[]{:S(2)}) collective-permute-start(f32[4,128,128]{2,1,0:T(8,128)} %get-tuple-element.28), channel_id=1, source_target_pairs={{0,6},{1,7},{2,4},{3,5},{4,2},{5,3},{6,0},{7,1},{8,14},{9,15},{10,... | collective-permute-start | bytes 786440 | tf_op jit(solution)/shard_map/ppermute | solution.py:298
  26.7 4.1 %copy-start.11 = (s32[8,4]{0,1:T(4,128)S(1)}, s32[8,4]{0,1:T(4,128)}, u32[]{:S(2)}) copy-start(s32[8,4]{0,1:T(4,128)} %param.10) | copy-start | bytes 388
  26.7 22.9 %collective-permute-start.9 = (f32[4,128,128]{2,1,0:T(8,128)}, f32[4,128,128]{2,1,0:T(8,128)S(1)}, u32[]{:S(2)}, u32[]{:S(2)}) collective-permute-start(f32[4,128,128]{2,1,0:T(8,128)} %get-tuple-element.33), channel_id=1, source_target_pairs={{0,2},{1,3},{2,0},{3,1},{4,6},{5,7},{6,4},{7,5},{8,10},{9,11},{10,... | collective-permute-start | bytes 786440 | tf_op jit(solution)/shard_map/ppermute | solution.py:298
  28.2 3.3 %copy-start.3 = (f32[4,2,128,128]{3,2,1,0:T(8,128)}, f32[4,2,128,128]{3,2,1,0:T(8,128)S(1)}, u32[]{:S(2)}) copy-start(f32[4,2,128,128]{3,2,1,0:T(8,128)S(1)} %collective-permute-done.3.others) | copy-start | bytes 1572868
  28.2 21.4 %collective-permute-start.10 = (f32[4,128,128]{2,1,0:T(8,128)}, f32[4,128,128]{2,1,0:T(8,128)S(1)}, u32[]{:S(2)}, u32[]{:S(2)}) collective-permute-start(f32[4,128,128]{2,1,0:T(8,128)} %get-tuple-element.34), channel_id=1, source_target_pairs={{0,4},{1,5},{2,6},{3,7},{4,0},{5,1},{6,2},{7,3},{8,12},{9,13},{10,... | collective-permute-start | bytes 786440 | tf_op jit(solution)/shard_map/ppermute | solution.py:298
  29.4 7.9 %copy-start.4 = (f32[4,128,128]{2,1,0:T(8,128)}, f32[4,128,128]{2,1,0:T(8,128)S(1)}, u32[]{:S(2)}) copy-start(f32[4,128,128]{2,1,0:T(8,128)S(1)} %collective-permute-done.5.refs_5_) | copy-start | bytes 786436
  29.4 20.3 %collective-permute-start.11 = (f32[4,128,128]{2,1,0:T(8,128)}, f32[4,128,128]{2,1,0:T(8,128)S(1)}, u32[]{:S(2)}, u32[]{:S(2)}) collective-permute-start(f32[4,128,128]{2,1,0:T(8,128)} %get-tuple-element.35), channel_id=1, source_target_pairs={{0,6},{1,7},{2,4},{3,5},{4,2},{5,3},{6,0},{7,1},{8,14},{9,15},{10,... | collective-permute-start | bytes 786440 | tf_op jit(solution)/shard_map/ppermute | solution.py:298
  65.1 2.1 %collective-permute-start.12 = (f32[4,264,128]{2,1,0:T(8,128)}, f32[4,264,128]{2,1,0:T(8,128)S(1)}, u32[]{:S(2)}, u32[]{:S(2)}) collective-permute-start(f32[4,264,128]{2,1,0:T(8,128)} %get-tuple-element.37), channel_id=1, source_target_pairs={{0,1},{1,0},{2,3},{3,2},{4,5},{5,4},{6,7},{7,6},{8,9},{9,8},{10,11... | collective-permute-start | bytes 1622024 | tf_op jit(solution)/shard_map/ppermute | solution.py:298
  68.4 6.5 %collective-permute-start.13 = (f32[264,128]{1,0:T(8,128)S(1)}, f32[264,128]{1,0:T(8,128)S(1)}, u32[]{:S(2)}, u32[]{:S(2)}) collective-permute-start(f32[264,128]{1,0:T(8,128)S(1)} %get-tuple-element.38), channel_id=1, source_target_pairs={{0,2},{1,3},{2,0},{3,1},{4,6},{5,7},{6,4},{7,5},{8,10},{9,11},{10,... | collective-permute-start | bytes 405512 | tf_op jit(solution)/shard_map/ppermute | solution.py:298
  69.4 8.7 %collective-permute-start.15 = (f32[264,128]{1,0:T(8,128)S(1)}, f32[264,128]{1,0:T(8,128)S(1)}, u32[]{:S(2)}, u32[]{:S(2)}) collective-permute-start(f32[264,128]{1,0:T(8,128)S(1)} %get-tuple-element.39), channel_id=1, source_target_pairs={{0,6},{1,7},{2,4},{3,5},{4,2},{5,3},{6,0},{7,1},{8,14},{9,15},{10,... | collective-permute-start | bytes 405512 | tf_op jit(solution)/shard_map/ppermute | solution.py:298
  71.5 8.0 %collective-permute-start.14 = (f32[264,128]{1,0:T(8,128)S(1)}, f32[264,128]{1,0:T(8,128)S(1)}, u32[]{:S(2)}, u32[]{:S(2)}) collective-permute-start(f32[264,128]{1,0:T(8,128)S(1)} %get-tuple-element.40), channel_id=1, source_target_pairs={{0,4},{1,5},{2,6},{3,7},{4,0},{5,1},{6,2},{7,3},{8,12},{9,13},{10,... | collective-permute-start | bytes 405512 | tf_op jit(solution)/shard_map/ppermute | solution.py:298
  79.5 5.0 %collective-permute-start.16 = (f32[2,128,128]{2,1,0:T(8,128)S(1)}, f32[2,128,128]{2,1,0:T(8,128)S(1)}, u32[]{:S(2)}, u32[]{:S(2)}) collective-permute-start(f32[2,128,128]{2,1,0:T(8,128)S(1)} %bitcast.24), channel_id=1, source_target_pairs={{0,8},{8,0},{16,24},{24,16},{1,9},{9,1},{17,25},{25,17},{2,10},{10... | collective-permute-start | bytes 393224 | tf_op jit(solution)/shard_map/ppermute | solution.py:298
  84.5 7.3 %collective-permute-start.17 = (f32[2,128,128]{2,1,0:T(8,128)S(1)}, f32[2,128,128]{2,1,0:T(8,128)S(1)}, u32[]{:S(2)}, u32[]{:S(2)}) collective-permute-start(f32[2,128,128]{2,1,0:T(8,128)S(1)} %add.32), channel_id=1, source_target_pairs={{0,16},{8,24},{16,0},{24,8},{1,17},{9,25},{17,1},{25,9},{2,18},{10... | collective-permute-start | bytes 393224 | tf_op jit(solution)/shard_map/ppermute | solution.py:298
  (6 other events, 4.6 us)

commit v2 on v0

--- a/solution.py
+++ b/solution.py
@@ -1,14 +1,441 @@
+import functools
 import math
 
 import jax
 import jax.numpy as jnp
 from jax import lax
+from jax.experimental import pallas as pl
+from jax.experimental.pallas import tpu as pltpu
 from jax.sharding import PartitionSpec as P
 
 ITERS = 2
 
 
 leakage = 0.05
+
+CORES = 2
+SPARE = 8
+ROWS = 256
+
+VMEM = pl.BlockSpec(memory_space=pltpu.VMEM)
+SMEM = pl.BlockSpec(memory_space=pltpu.SMEM)
+ANY = pl.BlockSpec(memory_space=pl.ANY)
+
+
+def call(body, out_shape, operands, in_specs, scratch=(), limit=8):
+    moved = sum(4 * a.size for a in operands) + sum(4 * o.size for o in out_shape)
+    return pl.pallas_call(
+        body,
+        out_shape=out_shape,
+        in_specs=in_specs,
+        out_specs=[VMEM] * len(out_shape),
+        scratch_shapes=list(scratch),
+        compiler_params=pltpu.CompilerParams(vmem_limit_bytes=limit << 20),
+        cost_estimate=pl.CostEstimate(flops=moved, bytes_accessed=moved, transcendentals=0),
+    )(*operands)
+
+
+def shape(*dims):
+    return jax.ShapeDtypeStruct(dims, jnp.float32)
+
+
+def total(acc):
+    return jnp.sum(acc, keepdims=True)
+
+
+def fold(rows):
+    return jnp.sum(rows.reshape(rows.shape[0] // 8, 8, rows.shape[1]), axis=0)
+
+
+def ahead(rows):
+    return pltpu.roll(rows, rows.shape[1] - 1, 1)
+
+
+def behind(rows):
+    return pltpu.roll(rows, 1, 1)
+
+
+def padded(planes, height, width):
+    return ((planes + 2) * height, width)
+
+
+def clear_edges(*refs, height):
+    for ref in refs:
+        zero = jnp.zeros((height, ref.shape[1]), ref.dtype)
+        ref[:height] = zero
+        ref[ref.shape[0] - height :] = zero
+
+
+def each_chunk(rows, height, body, start, size=ROWS):
+    size = math.gcd(size, rows)
+
+    def step(index, carry):
+        base = pl.multiple_of(height + index * size, math.gcd(size, height))
+
+        def at(ref, offset=0, value=None):
+            where = pl.ds(base + offset, size)
+            if value is None:
+                return ref[where, :]
+            ref[where, :] = value
+
+        return body(at, index * size, carry)
+
+    return lax.fori_loop(0, rows // size, step, start)
+
+
+def neighbours(at, field, depth, rows, columns, height):
+    here, column = at(field), at(columns)
+    result = at(depth) * at(field, height) + at(depth, -height) * at(field, -height)
+    result += at(rows) * at(field, 1)
+    result += at(rows, -1) * at(field, -1)
+    result += column * ahead(here) + behind(column * here)
+    return here, result
+
+
+def stage_kernel(place, forward, adjoint, *refs):
+    outs, sems = refs[:-1], refs[-1]
+    own, give = outs[-2], outs[-1]
+    sends = outs[:-2]
+    chip, core = place[0], place[1]
+    planes, chips = own.shape[:2]
+    copies = []
+    for step, out in enumerate(sends):
+        copies.append((forward.at[:, pl.ds(CORES * (chip ^ step), CORES)], out))
+    for plane in range(planes):
+        for other in range(chips):
+            copies.append((adjoint.at[plane, CORES * other + 1 - core], give.at[plane, other]))
+            copies.append((adjoint.at[plane, CORES * other + core], own.at[plane, other]))
+    started = [
+        pltpu.make_async_copy(source, target, sems.at[number])
+        for number, (source, target) in enumerate(copies)
+    ]
+    for copy in started:
+        copy.start()
+    for copy in started:
+        copy.wait()
+
+
+def pack_kernel(place, own, got, *outs):
+    planes = own.shape[0]
+    for step, out in enumerate(outs):
+        other = place[0] ^ step
+        for plane in range(planes):
+            out[0, plane] = own[plane, other]
+            out[1, plane] = got[plane, other]
+
+
+def sort_kernel(place, *refs):
+    blocks, keep, give = refs[:-2], refs[-2], refs[-1]
+    for step, block in enumerate(blocks):
+        for plane in range(block.shape[0]):
+            keep[step, plane] = block[plane, place[1]]
+            give[step, plane] = block[plane, 1 - place[1]]
+
+
+def plane_rows(place, step, relative, plane, planes, height):
+    level = ((place[0] ^ step) * CORES + (place[1] ^ relative)) * planes + plane
+    return pl.ds(pl.multiple_of((level + 1) * height, height), height)
+
+
+def coefficient_kernel(place, own, others, depth, rows, columns, scale, root, sigma):
+    chips, planes, height, width = own.shape
+    count = chips * CORES * planes
+    clear_edges(depth, rows, columns, scale, root, sigma, height=height)
+    for step in range(chips):
+        for relative, source in enumerate((own, others)):
+            for plane in range(planes):
+                sigma[plane_rows(place, step, relative, plane, planes, height), :] = source[
+                    step, plane
+                ]
+    row = lax.broadcasted_iota(jnp.int32, (height, width), 0)
+    lane = lax.broadcasted_iota(jnp.int32, (height, width), 1)
+    row_ahead, row_behind, lane_ahead = row < height - 1, row > 0, lane < width - 1
+
+    def diagonals(at, first, carry):
+        level = first // height
+        here = at(sigma)
+        along_depth = jnp.where(level > 0, 0.5, 0.0) * (here + at(sigma, -height))
+        along_depth += jnp.where(level < count - 1, 0.5, 0.0) * (here + at(sigma, height))
+        along_row = jnp.where(row_behind, 0.5 * (here + at(sigma, -1)), 0.0)
+        along_row += jnp.where(row_ahead, 0.5 * (here + at(sigma, 1)), 0.0)
+        face = jnp.where(lane_ahead, 0.5 * (here + ahead(here)), 0.0)
+        diagonal = leakage + along_depth + along_row + (behind(face) + face)
+        inverse = lax.rsqrt(diagonal)
+        inverse = inverse * (1.5 - 0.5 * diagonal * inverse * inverse)
+        at(scale, value=inverse)
+        at(root, value=diagonal * inverse)
+        return carry
+
+    each_chunk(count * height, height, diagonals, 0, height)
+
+    def couplings(at, first, carry):
+        here, size = at(sigma), at(scale)
+        half = 0.5 * size
+        upper = jnp.where(first // height < count - 1, half, 0.0)
+        at(depth, value=upper * ((here + at(sigma, height)) * at(scale, height)))
+        face = half * ((here + at(sigma, 1)) * at(scale, 1))
+        at(rows, value=jnp.where(row_ahead, face, 0.0))
+        face = half * ((here + ahead(here)) * ahead(size))
+        at(columns, value=jnp.where(lane_ahead, face, 0.0))
+        return carry
+
+    each_chunk(count * height, height, couplings, 0, height)
+
+
+def spot(ref, cell, height):
+    width = ref.shape[1]
+    lane = lax.broadcasted_iota(jnp.int32, (1, width), 1)
+    return pl.ds(height + cell // width, 1), lane == cell % width
+
+
+def add_at(ref, scale, cell, value, height):
+    row, hit = spot(ref, cell, height)
+    ref[row, :] += jnp.where(hit, value * scale[row, :], 0.0)
+
+
+def value_at(ref, cell, height):
+    row, hit = spot(ref, cell, height)
+    return total(jnp.where(hit, ref[row, :], 0.0))
+
+
+def solve_in_place(coefficients, sources, field, residue, applied, later, end, height):
+    depth, rows, columns, scale = coefficients
+    width = field.shape[1]
+    size = field.shape[0] - 2 * height
+    nothing = jnp.zeros((8, width), jnp.float32)
+    clear_edges(field, residue, later, height=height)
+
+    def first(at, index, carry):
+        here, sums = neighbours(at, field, depth, rows, columns, height)
+        at(residue, value=sums - here)
+        return carry
+
+    each_chunk(size, height, first, 0)
+    for cell, value in sources:
+        add_at(residue, scale, cell, value, height)
+
+    def second(at, index, carry):
+        squares, products = carry
+        here, sums = neighbours(at, residue, depth, rows, columns, height)
+        product = here - sums
+        at(applied, value=product)
+        return squares + fold(here * here), products + fold(here * product)
+
+    squares, products = each_chunk(size, height, second, (nothing, nothing))
+    current, energy = total(squares), total(products)
+    step_size = current / energy
+
+    def third(at, index, carry):
+        squares, products = carry
+        product = at(applied)
+        left = at(residue) - step_size * product
+        at(later, value=left)
+        return squares + fold(left * left), products + fold(left * product)
+
+    squares, products = each_chunk(size, height, third, (nothing, nothing))
+    following, cross = total(squares), total(products)
+    ratio = following / current
+
+    def fourth(at, index, acc):
+        here = at(later)
+        sums = at(depth, -height) * at(later, -height) + at(rows, -1) * at(later, -1)
+        sums += behind(at(columns) * here)
+        return acc + fold(here * (here - 2.0 * sums))
+
+    own = total(each_chunk(size, height, fourth, nothing))
+    last_size = following / (own + ratio * (2.0 * cross + ratio * energy))
+    first_size = step_size + last_size * ratio
+
+    def fifth(at, index, carry):
+        moved = at(field) + first_size * at(residue) + last_size * at(later)
+        end(at, at(scale) * moved)
+        return carry
+
+    each_chunk(size, height, fifth, 0)
+
+
+def electrode(place, electrodes, patterns, which):
+    return electrodes[patterns[place[2], which]]
+
+
+def forward_kernel(strength, place, electrodes, patterns, *refs):
+    depth, rows, columns, scale, root, own, others = refs[:7]
+    result, slopes, voltage, field, residue, applied, later = refs[7:]
+    chips, planes, height, width = own.shape
+    for step in range(chips):
+        for relative, source in enumerate((own, others)):
+            for plane in range(planes):
+                where = plane_rows(place, step, relative, plane, planes, height)
+                field[where, :] = source[step, plane] * root[where, :]
+    plus, minus, high, low = (
+        electrode(place, electrodes, patterns, which) for which in range(4)
+    )
+    lane = lax.broadcasted_iota(jnp.int32, (1, width), 1)
+    weight = jnp.where(lane < width - 1, -0.5, 0.0)
+
+    def end(at, potential):
+        at(result, value=potential)
+        at(slopes, value=weight * (ahead(potential) - potential))
+
+    solve_in_place(
+        (depth, rows, columns, scale),
+        ((plus, strength), (minus, -strength)),
+        field, residue, applied, later, end, height,
+    )
+    clear_edges(result, height=height)
+    seen = value_at(result, high, height) - value_at(result, low, height)
+    voltage[...] = jnp.broadcast_to(seen, voltage.shape)
+
+
+def adjoint_kernel(weight, place, electrodes, patterns, observed, *refs):
+    depth, rows, columns, scale, root, forward, slopes, voltage = refs[:8]
+    *blocks, kept, given, field, residue, applied, later, adjoint = refs[8:]
+    chips = len(blocks)
+    planes, height, width = blocks[0].shape[1:]
+    count = chips * CORES * planes
+    for step, block in enumerate(blocks):
+        for relative in range(CORES):
+            for plane in range(planes):
+                where = plane_rows(place, step, relative, plane, planes, height)
+                field[where, :] = block[relative, plane] * root[where, :]
+    weighted = weight * (voltage[0:1, :] - observed[place[2]])
+    high = electrode(place, electrodes, patterns, 2)
+    low = electrode(place, electrodes, patterns, 3)
+
+    def end(at, potential):
+        at(adjoint, value=potential)
+
+    solve_in_place(
+        (depth, rows, columns, scale),
+        ((high, weighted), (low, -weighted)),
+        field, residue, applied, later, end, height,
+    )
+    clear_edges(adjoint, height=height)
+    row = lax.broadcasted_iota(jnp.int32, (height, 1), 0)
+    row_ahead = jnp.where(row < height - 1, -0.5, 0.0)
+    row_behind = jnp.where(row > 0, -0.5, 0.0)
+
+    def step(at, first, carry):
+        level = first // height
+        left, right = at(forward), at(adjoint)
+
+        def product(offset):
+            return (at(forward, offset) - left) * (at(adjoint, offset) - right)
+
+        plane = jnp.where(level < count - 1, -0.5, 0.0) * product(height)
+        plane += jnp.where(level > 0, -0.5, 0.0) * product(-height)
+        plane += row_ahead * product(1) + row_behind * product(-1)
+        face = at(slopes) * (ahead(right) - right)
+        plane += face + behind(face)
+        block = (level // (CORES * planes)) ^ place[0]
+        owner = (level // planes) % CORES
+        start = pl.multiple_of((level % planes) * height, height)
+
+        @pl.when(owner == place[1])
+        def _():
+            kept[block, pl.ds(start, height), :] = plane
+
+        @pl.when(owner != place[1])
+        def _():
+            given[block, pl.ds(start, height), :] = plane
+
+        return carry
+
+    each_chunk(count * height, height, step, 0, height)
+    lane = lax.broadcasted_iota(jnp.int32, (SPARE, width), 1)
+    note = jnp.where(lane == place[2], voltage[...], 0.0)
+    for block in range(chips):
+        kept[block, planes * height :, :] = note
+        given[block, planes * height :, :] = note
+
+
+def swap(values, axis, size, bit):
+    return lax.ppermute(values, axis, [(i, i ^ bit) for i in range(size)])
+
+
+def per_device_exchanged(
+    conductivity, warm_forward, warm_adjoint, electrodes, patterns, observed
+):
+    plane_count, pattern_count, row_count, column_count = warm_forward.shape
+    layers = lax.axis_size("vox")
+    groups = lax.axis_size("pat")
+    chips = layers // CORES
+    strength = 2.0 * math.sqrt(layers * plane_count * row_count * column_count)
+    position = lax.axis_index("vox")
+    chip, core = position // CORES, position % CORES
+    place = jnp.stack([chip, core, position]).astype(jnp.int32)
+    plane = (row_count, column_count)
+    whole = shape(*padded(layers * plane_count, *plane))
+    room = pltpu.VMEM(whole.shape, jnp.float32)
+
+    def chip_swap(values, step):
+        return swap(values, "vox", layers, CORES * step)
+
+    def core_swap(values):
+        return swap(values, "vox", layers, 1)
+
+    sigma = [conductivity] + [chip_swap(conductivity, step) for step in range(1, chips)]
+    *sends, own, give = call(
+        stage_kernel,
+        [shape(plane_count, CORES, *plane)] * chips
+        + [shape(plane_count, chips, *plane)] * 2,
+        (place, warm_forward, warm_adjoint),
+        [SMEM, ANY, ANY],
+        scratch=[pltpu.SemaphoreType.DMA((chips + 2 * chips * plane_count,))],
+    )
+    blocks = [sends[0]] + [chip_swap(sends[step], step) for step in range(1, chips)]
+    got = core_swap(give)
+    packed = call(
+        pack_kernel,
+        [shape(CORES, plane_count, *plane)] * chips,
+        (place, own, got),
+        [SMEM, VMEM, VMEM],
+    )
+    adjoint_blocks = [packed[0]] + [chip_swap(packed[step], step) for step in range(1, chips)]
+    own_sigma = jnp.stack(sigma)
+    other_sigma = core_swap(own_sigma)
+    coefficients = call(
+        coefficient_kernel,
+        [whole] * 5,
+        (place, own_sigma, other_sigma),
+        [SMEM, VMEM, VMEM],
+        scratch=[room],
+        limit=16,
+    )
+    half = shape(chips, plane_count, *plane)
+    keep, pass_on = call(sort_kernel, [half] * 2, (place, *blocks), [SMEM] + [VMEM] * chips)
+    received = core_swap(pass_on)
+    forward, slopes, voltage = call(
+        functools.partial(forward_kernel, strength),
+        [whole, whole, shape(SPARE, column_count)],
+        (place, electrodes, patterns, *coefficients, keep, received),
+        [SMEM] * 3 + [VMEM] * 7,
+        scratch=[room] * 4,
+        limit=20,
+    )
+    block = shape(chips, plane_count * row_count + SPARE, column_count)
+    kept, given = call(
+        functools.partial(adjoint_kernel, 0.1 * strength),
+        [block] * 2,
+        (
+            place, electrodes, patterns, observed,
+            *coefficients, forward, slopes, voltage, *adjoint_blocks,
+        ),
+        [SMEM] * 4 + [VMEM] * (8 + chips),
+        scratch=[room] * 5,
+        limit=24,
+    )
+    summed = kept + core_swap(given)
+    mine = summed[0]
+    for step in range(1, chips):
+        mine = mine + chip_swap(summed[step], step)
+    predicted = mine[plane_count * row_count, :pattern_count]
+    gradient = mine[: plane_count * row_count].reshape(plane_count, *plane)
+    bit = 1
+    while bit < groups:
+        gradient = gradient + swap(gradient, "pat", groups, bit)
+        bit *= 2
+    return gradient, predicted
 
 
 def extended(block, sides, width):
@@ -83,7 +510,7 @@
     return solution
 
 
-def per_device(conductivity, warm_forward, warm_adjoint, electrodes, patterns, observed):
+def per_device_in_place(conductivity, warm_forward, warm_adjoint, electrodes, patterns, observed):
     plane_count, pattern_count, row_count, column_count = warm_forward.shape
     position = lax.axis_index("vox")
     layers = lax.axis_size("vox")
@@ -156,6 +583,15 @@
     return (gradient, predicted)
 
 
+def per_device(conductivity, warm_forward, *rest):
+    size = lax.axis_size("vox")
+    groups = lax.axis_size("pat")
+    exchange = warm_forward.shape[1] == size and size % CORES == 0
+    exchange = exchange and size & (size - 1) == 0 and groups & (groups - 1) == 0
+    form = per_device_exchanged if exchange else per_device_in_place
+    return form(conductivity, warm_forward, *rest)
+
+
 def solution(mesh):
     in_specs = (
         P("vox", None, None),

time: 283 us -> 79.2 us (0.28)
  blocking collectives: 130 us -> 0 us
  waiting for transfers between devices: 60.6 us -> 29.6 us
  other arithmetic: 31.2 us -> 0.9 us
  Pallas kernels: 0 us -> 24.4 us
  starting transfers between devices: 39.3 us -> 20.1 us
  between operations: 14.7 us -> 0.82 us
  local copies, waits for them, and re-layouts: 7.01 us -> 3.1 us
    psum x7 -> x0, blocking collectives: 130 us -> none  [the longest x6 117 us: pattern_sum(): return lax.psum(local_terms, 'vox')]
    psum x1 -> x0, waiting for transfers between devices: 56.4 us -> none  [per_device(): gradient = lax.psum(local_gradient, 'pat')]
    ppermute x16 -> x18, waiting for transfers between devices: 4.17 us -> 29.6 us  [swap(): return lax.ppermute(values, axis, [(i, i ^ bit) for i in range(size)])]
    pallas_call x0 -> x6, Pallas kernels: none -> 24.4 us  [call(): pl.pallas_call(body, out_shape=out_shape, in_specs=in_specs, out_specs=[V...]
    ppermute x16 -> x18, starting transfers between devices: 39.2 us -> 20.1 us  [swap(): return lax.ppermute(values, axis, [(i, i ^ bit) for i in range(size)])]
    mul x23 -> x0, other arithmetic: 10.6 us -> none  [the longest x5 4.72 us: operate(): flux_depth = depth_faces[:, None] * (padded[1:] - padded[:-1])]
    reduce_sum x11 -> x0, other arithmetic: 10.4 us -> none  [the longest x7 8.68 us: inner(): return jnp.sum(left_factor * right_factor, axis=(0, 2, 3))]
    div x8 -> x0, other arithmetic: 4.6 us -> none  [the longest x2 4.56 us: solve_pattern(): precond = residue / diagonal]
  transfers between devices with their start and end apart: 17 -> 18, of which waited for: 5 -> 7; matrix products, arithmetic and copies ran while one was open for 6% -> 1% of each run, Pallas kernels for 0% -> 21%
where the time goes in v2:
time: 79.2 us; the launch traced here: 79 us
  waiting for transfers between devices  29.6 us (37%)
  Pallas kernels  24.4 us (31%)
  starting transfers between devices  20.1 us (25%)
  local copies, waits for them, and re-layouts  3.1 us (4%)
  other arithmetic  0.9 us (1%)
  between operations  0.82 us (1%)
    ppermute x18, waiting for transfers between devices, swap(): return lax.ppermute(values, axis, [(i, i ^ bit) for i in range(size)])  29.6 us
    pallas_call x6, Pallas kernels, call(): pl.pallas_call(body, out_shape=out_shape, in_specs=in_specs, out_specs=[V...  24.4 us
    ppermute x18, starting transfers between devices, swap(): return lax.ppermute(values, axis, [(i, i ^ bit) for i in range(size)])  20.1 us
    unnamed x13, local copies, waits for them, and re-layouts  2.55 us
  transfers between devices with their start and end apart: 18, of which 7 were waited for; matrix products, arithmetic and copies ran while one was open for 1% of the time, Pallas kernels for 21%

profile of v2, /device:TPU:0, one launch (start us, length us, event | category | flops | bytes accessed | tf_op | source)
XLA Modules:
  0.0 79.0 jit_solution(13638019734258251115)
XLA Ops:
  0.6 3.0 %collective-permute-start = (f32[2,128,128]{2,1,0:T(8,128)}, f32[2,128,128]{2,1,0:T(8,128)S(1)}, u32[]{:S(2)}, u32[]{:S(2)}) collective-permute-start(f32[2,128,128]{2,1,0:T(8,128)} %param.6), channel_id=1, source_target_pairs={{0,2},{1,3},{2,0},{3,1},{4,6},{5,7},{6,4},{7,5},{8,10},{9,11},{10,... | collective-permute-start | bytes 393224 | tf_op jit(solution)/shard_map/ppermute | solution.py:353
  3.7 1.5 %collective-permute-start.2 = (f32[2,128,128]{2,1,0:T(8,128)}, f32[2,128,128]{2,1,0:T(8,128)S(1)}, u32[]{:S(2)}, u32[]{:S(2)}) collective-permute-start(f32[2,128,128]{2,1,0:T(8,128)} %param.6), channel_id=1, source_target_pairs={{0,6},{1,7},{2,4},{3,5},{4,2},{5,3},{6,0},{7,1},{8,14},{9,15},{10,... | collective-permute-start | bytes 393224 | tf_op jit(solution)/shard_map/ppermute | solution.py:353
  5.2 1.2 %copy-done = f32[2,8,128,128]{3,2,1,0:T(8,128)S(1)} copy-done((f32[2,8,128,128]{3,2,1,0:T(8,128)S(1)}, f32[2,8,128,128]{3,2,1,0:T(8,128)}, u32[]{:S(2)}) %copy-start) | copy-done | bytes 1048600
  6.5 1.2 %copy-done.1 = f32[2,8,128,128]{3,2,1,0:T(8,128)S(1)} copy-done((f32[2,8,128,128]{3,2,1,0:T(8,128)S(1)}, f32[2,8,128,128]{3,2,1,0:T(8,128)}, u32[]{:S(2)}) %copy-start.1) | copy-done | bytes 1048600
  7.7 2.2 %shard_map.78 = (f32[2,2,128,128]{3,2,1,0:T(8,128)S(1)}, f32[2,2,128,128]{3,2,1,0:T(8,128)S(1)}, f32[2,2,128,128]{3,2,1,0:T(8,128)S(1)}, f32[2,2,128,128]{3,2,1,...) custom-call(s32[3]{0:T(128)S(1)} %pad_add_fusion.place, f32[2,8,128,128]{3,2,1,0:T(8,128)S(1)} %copy-done, ...), custom_call_target="tpu_custom_call" | custom-call | flops 4194316 | bytes 4194316 | tf_op jit(solution)/shard_map/pallas_call | solution.py:27
  9.9 1.6 %collective-permute-start.4 = (f32[2,2,128,128]{3,2,1,0:T(8,128)S(1)}, f32[2,2,128,128]{3,2,1,0:T(8,128)S(1)}, u32[]{:S(2)}, u32[]{:S(2)}) collective-permute-start(f32[2,2,128,128]{3,2,1,0:T(8,128)S(1)} %get-tuple-element.30), channel_id=1, source_target_pairs={{0,2},{1,3},{2,0},{3,1},{4,6},{5,7},{6,4},{7,5},{8,10},{9,11},{10,... | collective-permute-start | bytes 786440 | tf_op jit(solution)/shard_map/ppermute | solution.py:353
  11.9 1.5 %collective-permute-start.6 = (f32[2,2,128,128]{3,2,1,0:T(8,128)S(1)}, f32[2,2,128,128]{3,2,1,0:T(8,128)S(1)}, u32[]{:S(2)}, u32[]{:S(2)}) collective-permute-start(f32[2,2,128,128]{3,2,1,0:T(8,128)S(1)} %get-tuple-element.32), channel_id=1, source_target_pairs={{0,6},{1,7},{2,4},{3,5},{4,2},{5,3},{6,0},{7,1},{8,14},{9,15},{10,... | collective-permute-start | bytes 786440 | tf_op jit(solution)/shard_map/ppermute | solution.py:353
  13.6 13.5 %collective-permute-done.1 = f32[2,128,128]{2,1,0:T(8,128)S(1)} collective-permute-done((f32[2,128,128]{2,1,0:T(8,128)S(1)}, f32[2,128,128]{2,1,0:T(8,128)S(1)}, u32[]{:S(2)}, u32[]{:S(2)}) %collective-permute-start.1) | collective-permute-done | bytes 131104 | tf_op jit(solution)/shard_map/ppermute | solution.py:353
  27.2 1.4 %shard_map.79 = (f32[4,2,128,128]{3,2,1,0:T(8,128)S(1)}, f32[4,2,128,128]{3,2,1,0:T(8,128)}) custom-call(s32[3]{0:T(128)S(1)} %pad_add_fusion.place, f32[2,2,128,128]{3,2,1,0:T(8,128)S(1)} %get-tuple-element.29.refs_0_, f32[2,2,128,128]{3,2,1,0:T(8,128)S(1)} %collective-permute-done.4.refs_1_, f32[2,2,128,128]{3,2,1,0:T(8,128)S(1)} %collective-permute-done.5.refs_2_, ...), custom_call_target="tpu_custom_call" | custom-call | flops 2097164 | bytes 2097164 | tf_op jit(solution)/shard_map/pallas_call | solution.py:27
  29.2 1.4 %shard_map.81 = (f32[2,2,128,128]{3,2,1,0:T(8,128)S(1)}, f32[2,2,128,128]{3,2,1,0:T(8,128)}, f32[2,2,128,128]{3,2,1,0:T(8,128)}, f32[2,2,128,128]{3,2,1,0:T(8,128)S(1)}) custom-call(s32[3]{0:T(128)S(1)} %pad_add_fusion.place, f32[2,4,128,128]{3,2,1,0:T(8,128)S(1)} %get-tuple-element.38.own, f32[2,4,128,128]{3,2,1,0:T(8,128)S(1)} %collective-permute-done.8.got), custom_call_target="tpu_custom_call" | custom-call | flops 2097164 | bytes 2097164 | tf_op jit(solution)/shard_map/pallas_call | solution.py:27
  31.4 2.6 %collective-permute-start.11 = (f32[2,2,128,128]{3,2,1,0:T(8,128)S(1)}, f32[2,2,128,128]{3,2,1,0:T(8,128)S(1)}, u32[]{:S(2)}, u32[]{:S(2)}) collective-permute-start(f32[2,2,128,128]{3,2,1,0:T(8,128)S(1)} %get-tuple-element.43), channel_id=1, source_target_pairs={{0,6},{1,7},{2,4},{3,5},{4,2},{5,3},{6,0},{7,1},{8,14},{9,15},{10,... | collective-permute-start | bytes 786440 | tf_op jit(solution)/shard_map/ppermute | solution.py:353
  34.1 5.1 %shard_map.77 = (f32[2304,128]{1,0:T(8,128)S(1)}, f32[2304,128]{1,0:T(8,128)S(1)}, f32[2304,128]{1,0:T(8,128)S(1)}, f32[2304,128]{1,0:T(8,128)S(1)}, f32[2304,128]{1,0:T(8,128)S(1)}) custom-call(s32[3]{0:T(128)S(1)} %pad_add_fusion.place, f32[4,2,128,128]{3,2,1,0:T(8,128)S(1)} %pad_maximum_fusion.own, f32[4,2,128,128]{3,2,1,0:T(8,128)S(1)} %collective-permute-done.3.others), custom_call_target="tpu_custom_call" | custom-call | flops 6946828 | bytes 6946828 | tf_op jit(solution)/shard_map/pallas_call | solution.py:27
  39.3 6.1 %shard_map.80 = (f32[2304,128]{1,0:T(8,128)S(1)}, f32[2304,128]{1,0:T(8,128)S(1)}, f32[8,128]{1,0:T(8,128)S(1)}) custom-call(s32[3]{0:T(128)S(1)} %pad_add_fusion.place, s32[128]{0:T(128)S(1)} %copy-done.2, s32[8,4]{1,0:T(8,128)S(1)} %copy.9.patterns, f32[2304,128]{1,0:T(8,128)S(1)} %get-tuple-element.24.refs_0_, f32[2304,128]{1,0:T(8,128)S(1)} %get-tuple-element.25.refs_1_, ...), custom_call_target="tpu_custom_call" | custom-call | flops 9310860 | bytes 9310860 | tf_op jit(solution)/shard_map/pallas_call | solution.py:27
  45.5 8.2 %shard_map.82 = (f32[4,264,128]{2,1,0:T(8,128)S(1)}, f32[4,264,128]{2,1,0:T(8,128)S(1)}) custom-call(s32[3]{0:T(128)S(1)} %pad_add_fusion.place, s32[128]{0:T(128)S(1)} %copy-done.2, s32[8,4]{1,0:T(8,128)S(1)} %copy.9.patterns, f32[8]{0:T(128)S(1)} %copy-done.3, f32[2304,128]{1,0:T(8,128)S(1)} %get-tuple-element.24.refs_0_, ...), custom_call_target="tpu_custom_call" | custom-call | flops 10392236 | bytes 10392236 | tf_op jit(solution)/shard_map/pallas_call | solution.py:27
  53.7 1.9 %collective-permute-done.12 = f32[4,264,128]{2,1,0:T(8,128)S(1)} collective-permute-done((f32[4,264,128]{2,1,0:T(8,128)S(1)}, f32[4,264,128]{2,1,0:T(8,128)S(1)}, u32[]{:S(2)}, u32[]{:S(2)}) %collective-permute-start.12) | collective-permute-done | bytes 540704 | tf_op jit(solution)/shard_map/ppermute | solution.py:353
  56.7 1.2 %collective-permute-start.15 = (f32[264,128]{1,0:T(8,128)S(1)}, f32[264,128]{1,0:T(8,128)S(1)}, u32[]{:S(2)}, u32[]{:S(2)}) collective-permute-start(f32[264,128]{1,0:T(8,128)S(1)} %get-tuple-element.47), channel_id=1, source_target_pairs={{0,6},{1,7},{2,4},{3,5},{4,2},{5,3},{6,0},{7,1},{8,14},{9,15},{10,... | collective-permute-start | bytes 405512 | tf_op jit(solution)/shard_map/ppermute | solution.py:353
  57.9 1.4 %collective-permute-start.14 = (f32[264,128]{1,0:T(8,128)S(1)}, f32[264,128]{1,0:T(8,128)S(1)}, u32[]{:S(2)}, u32[]{:S(2)}) collective-permute-start(f32[264,128]{1,0:T(8,128)S(1)} %get-tuple-element.48), channel_id=1, source_target_pairs={{0,4},{1,5},{2,6},{3,7},{4,0},{5,1},{6,2},{7,3},{8,12},{9,13},{10,... | collective-permute-start | bytes 405512 | tf_op jit(solution)/shard_map/ppermute | solution.py:353
  59.3 3.0 %collective-permute-done.13 = f32[264,128]{1,0:T(8,128)S(1)} collective-permute-done((f32[264,128]{1,0:T(8,128)S(1)}, f32[264,128]{1,0:T(8,128)S(1)}, u32[]{:S(2)}, u32[]{:S(2)}) %collective-permute-start.13) | collective-permute-done | bytes 135200 | tf_op jit(solution)/shard_map/ppermute | solution.py:353
  62.3 2.3 %collective-permute-done.15 = f32[264,128]{1,0:T(8,128)S(1)} collective-permute-done((f32[264,128]{1,0:T(8,128)S(1)}, f32[264,128]{1,0:T(8,128)S(1)}, u32[]{:S(2)}, u32[]{:S(2)}) %collective-permute-start.15) | collective-permute-done | bytes 135200 | tf_op jit(solution)/shard_map/ppermute | solution.py:353
  64.5 1.4 %collective-permute-done.14 = f32[264,128]{1,0:T(8,128)S(1)} collective-permute-done((f32[264,128]{1,0:T(8,128)S(1)}, f32[264,128]{1,0:T(8,128)S(1)}, u32[]{:S(2)}, u32[]{:S(2)}) %collective-permute-start.14) | collective-permute-done | bytes 135200 | tf_op jit(solution)/shard_map/ppermute | solution.py:353
  65.9 1.6 %collective-permute-start.16 = (f32[2,128,128]{2,1,0:T(8,128)S(1)}, f32[2,128,128]{2,1,0:T(8,128)S(1)}, u32[]{:S(2)}, u32[]{:S(2)}) collective-permute-start(f32[2,128,128]{2,1,0:T(8,128)S(1)} %bitcast.24), channel_id=1, source_target_pairs={{0,8},{8,0},{16,24},{24,16},{1,9},{9,1},{17,25},{25,17},{2,10},{10... | collective-permute-start | bytes 393224 | tf_op jit(solution)/shard_map/ppermute | solution.py:353
  67.6 3.4 %collective-permute-done.16 = f32[2,128,128]{2,1,0:T(8,128)S(1)} collective-permute-done((f32[2,128,128]{2,1,0:T(8,128)S(1)}, f32[2,128,128]{2,1,0:T(8,128)S(1)}, u32[]{:S(2)}, u32[]{:S(2)}) %collective-permute-start.16) | collective-permute-done | bytes 131104 | tf_op jit(solution)/shard_map/ppermute | solution.py:353
  71.0 2.7 %collective-permute-start.17 = (f32[2,128,128]{2,1,0:T(8,128)S(1)}, f32[2,128,128]{2,1,0:T(8,128)S(1)}, u32[]{:S(2)}, u32[]{:S(2)}) collective-permute-start(f32[2,128,128]{2,1,0:T(8,128)S(1)} %add.28), channel_id=1, source_target_pairs={{0,16},{8,24},{16,0},{24,8},{1,17},{9,25},{17,1},{25,9},{2,18},{10... | collective-permute-start | bytes 393224 | tf_op jit(solution)/shard_map/ppermute | solution.py:353
  74.2 4.2 %collective-permute-done.17 = f32[2,128,128]{2,1,0:T(8,128)S(1)} collective-permute-done((f32[2,128,128]{2,1,0:T(8,128)S(1)}, f32[2,128,128]{2,1,0:T(8,128)S(1)}, u32[]{:S(2)}, u32[]{:S(2)}) %collective-permute-start.17) | collective-permute-done | bytes 131104 | tf_op jit(solution)/shard_map/ppermute | solution.py:353
  (40 shorter events, 4.7 us)
Async XLA Ops:
  0.6 12.8 %collective-permute-start = (f32[2,128,128]{2,1,0:T(8,128)}, f32[2,128,128]{2,1,0:T(8,128)S(1)}, u32[]{:S(2)}, u32[]{:S(2)}) collective-permute-start(f32[2,128,128]{2,1,0:T(8,128)} %param.6), channel_id=1, source_target_pairs={{0,2},{1,3},{2,0},{3,1},{4,6},{5,7},{6,4},{7,5},{8,10},{9,11},{10,... | collective-permute-start | bytes 393224 | tf_op jit(solution)/shard_map/ppermute | solution.py:353
  3.7 9.8 %collective-permute-start.2 = (f32[2,128,128]{2,1,0:T(8,128)}, f32[2,128,128]{2,1,0:T(8,128)S(1)}, u32[]{:S(2)}, u32[]{:S(2)}) collective-permute-start(f32[2,128,128]{2,1,0:T(8,128)} %param.6), channel_id=1, source_target_pairs={{0,6},{1,7},{2,4},{3,5},{4,2},{5,3},{6,0},{7,1},{8,14},{9,15},{10,... | collective-permute-start | bytes 393224 | tf_op jit(solution)/shard_map/ppermute | solution.py:353
  5.2 1.2 %copy-start = (f32[2,8,128,128]{3,2,1,0:T(8,128)S(1)}, f32[2,8,128,128]{3,2,1,0:T(8,128)}, u32[]{:S(2)}) copy-start(f32[2,8,128,128]{3,2,1,0:T(8,128)} %forward.1) | copy-start | bytes 3145732
  6.5 1.2 %copy-start.1 = (f32[2,8,128,128]{3,2,1,0:T(8,128)S(1)}, f32[2,8,128,128]{3,2,1,0:T(8,128)}, u32[]{:S(2)}) copy-start(f32[2,8,128,128]{3,2,1,0:T(8,128)} %adjoint.1) | copy-start | bytes 3145732
  7.7 5.8 %copy-start.4 = (f32[2,128,128]{2,1,0:T(8,128)S(1)}, f32[2,128,128]{2,1,0:T(8,128)}, u32[]{:S(2)}) copy-start(f32[2,128,128]{2,1,0:T(8,128)} %param.6) | copy-start | bytes 393220
  9.9 17.3 %collective-permute-start.4 = (f32[2,2,128,128]{3,2,1,0:T(8,128)S(1)}, f32[2,2,128,128]{3,2,1,0:T(8,128)S(1)}, u32[]{:S(2)}, u32[]{:S(2)}) collective-permute-start(f32[2,2,128,128]{3,2,1,0:T(8,128)S(1)} %get-tuple-element.30), channel_id=1, source_target_pairs={{0,2},{1,3},{2,0},{3,1},{4,6},{5,7},{6,4},{7,5},{8,10},{9,11},{10,... | collective-permute-start | bytes 786440 | tf_op jit(solution)/shard_map/ppermute | solution.py:353
  11.4 15.8 %collective-permute-start.5 = (f32[2,2,128,128]{3,2,1,0:T(8,128)S(1)}, f32[2,2,128,128]{3,2,1,0:T(8,128)S(1)}, u32[]{:S(2)}, u32[]{:S(2)}) collective-permute-start(f32[2,2,128,128]{3,2,1,0:T(8,128)S(1)} %get-tuple-element.31), channel_id=1, source_target_pairs={{0,4},{1,5},{2,6},{3,7},{4,0},{5,1},{6,2},{7,3},{8,12},{9,13},{10,... | collective-permute-start | bytes 786440 | tf_op jit(solution)/shard_map/ppermute | solution.py:353
  11.9 15.3 %collective-permute-start.6 = (f32[2,2,128,128]{3,2,1,0:T(8,128)S(1)}, f32[2,2,128,128]{3,2,1,0:T(8,128)S(1)}, u32[]{:S(2)}, u32[]{:S(2)}) collective-permute-start(f32[2,2,128,128]{3,2,1,0:T(8,128)S(1)} %get-tuple-element.32), channel_id=1, source_target_pairs={{0,6},{1,7},{2,4},{3,5},{4,2},{5,3},{6,0},{7,1},{8,14},{9,15},{10,... | collective-permute-start | bytes 786440 | tf_op jit(solution)/shard_map/ppermute | solution.py:353
  13.4 15.7 %collective-permute-start.8 = (f32[2,4,128,128]{3,2,1,0:T(8,128)S(1)}, f32[2,4,128,128]{3,2,1,0:T(8,128)S(1)}, u32[]{:S(2)}, u32[]{:S(2)}) collective-permute-start(f32[2,4,128,128]{3,2,1,0:T(8,128)S(1)} %get-tuple-element.39), channel_id=1, source_target_pairs={{0,1},{1,0},{2,3},{3,2},{4,5},{5,4},{6,7},{7,6},{8,9},{9,8},{10,11... | collective-permute-start | bytes 1572872 | tf_op jit(solution)/shard_map/ppermute | solution.py:353
  13.5 13.6 %collective-permute-start.1 = (f32[2,128,128]{2,1,0:T(8,128)S(1)}, f32[2,128,128]{2,1,0:T(8,128)S(1)}, u32[]{:S(2)}, u32[]{:S(2)}) collective-permute-start(f32[2,128,128]{2,1,0:T(8,128)S(1)} %copy-done.4), channel_id=1, source_target_pairs={{0,4},{1,5},{2,6},{3,7},{4,0},{5,1},{6,2},{7,3},{8,12},{9,13},{10,... | collective-permute-start | bytes 393224 | tf_op jit(solution)/shard_map/ppermute | solution.py:353
  27.1 7.0 %copy-start.5 = (s32[8,4]{0,1:T(4,128)S(1)}, s32[8,4]{0,1:T(4,128)}, u32[]{:S(2)}) copy-start(s32[8,4]{0,1:T(4,128)} %param.10) | copy-start | bytes 388
  27.1 7.0 %collective-permute-start.3 = (f32[4,2,128,128]{3,2,1,0:T(8,128)S(1)}, f32[4,2,128,128]{3,2,1,0:T(8,128)S(1)}, u32[]{:S(2)}, u32[]{:S(2)}) collective-permute-start(f32[4,2,128,128]{3,2,1,0:T(8,128)S(1)} %pad_maximum_fusion.own), channel_id=1, source_target_pairs={{0,1},{1,0},{2,3},{3,2},{4,5},{5,4},{6,7},{7,6},{8,9},{9,8},{10,11... | collective-permute-start | bytes 1572872 | tf_op jit(solution)/shard_map/ppermute | solution.py:353
  28.7 10.6 %copy-start.2 = (s32[128]{0:T(128)S(1)}, s32[128]{0:T(128)}, u32[]{:S(2)}) copy-start(s32[128]{0:T(128)} %electrodes.3) | copy-start | bytes 1540
  28.7 10.6 %collective-permute-start.7 = (f32[4,2,128,128]{3,2,1,0:T(8,128)}, f32[4,2,128,128]{3,2,1,0:T(8,128)S(1)}, u32[]{:S(2)}, u32[]{:S(2)}) collective-permute-start(f32[4,2,128,128]{3,2,1,0:T(8,128)} %get-tuple-element.34), channel_id=1, source_target_pairs={{0,1},{1,0},{2,3},{3,2},{4,5},{5,4},{6,7},{7,6},{8,9},{9,8},{10,11... | collective-permute-start | bytes 1572872 | tf_op jit(solution)/shard_map/ppermute | solution.py:353
  30.6 14.8 %collective-permute-start.9 = (f32[2,2,128,128]{3,2,1,0:T(8,128)}, f32[2,2,128,128]{3,2,1,0:T(8,128)S(1)}, u32[]{:S(2)}, u32[]{:S(2)}) collective-permute-start(f32[2,2,128,128]{3,2,1,0:T(8,128)} %get-tuple-element.41), channel_id=1, source_target_pairs={{0,2},{1,3},{2,0},{3,1},{4,6},{5,7},{6,4},{7,5},{8,10},{9,11},{10,... | collective-permute-start | bytes 786440 | tf_op jit(solution)/shard_map/ppermute | solution.py:353
  31.1 14.3 %collective-permute-start.10 = (f32[2,2,128,128]{3,2,1,0:T(8,128)}, f32[2,2,128,128]{3,2,1,0:T(8,128)S(1)}, u32[]{:S(2)}, u32[]{:S(2)}) collective-permute-start(f32[2,2,128,128]{3,2,1,0:T(8,128)} %get-tuple-element.42), channel_id=1, source_target_pairs={{0,4},{1,5},{2,6},{3,7},{4,0},{5,1},{6,2},{7,3},{8,12},{9,13},{10,... | collective-permute-start | bytes 786440 | tf_op jit(solution)/shard_map/ppermute | solution.py:353
  31.4 14.0 %collective-permute-start.11 = (f32[2,2,128,128]{3,2,1,0:T(8,128)S(1)}, f32[2,2,128,128]{3,2,1,0:T(8,128)S(1)}, u32[]{:S(2)}, u32[]{:S(2)}) collective-permute-start(f32[2,2,128,128]{3,2,1,0:T(8,128)S(1)} %get-tuple-element.43), channel_id=1, source_target_pairs={{0,6},{1,7},{2,4},{3,5},{4,2},{5,3},{6,0},{7,1},{8,14},{9,15},{10,... | collective-permute-start | bytes 786440 | tf_op jit(solution)/shard_map/ppermute | solution.py:353
  39.3 6.1 %copy-start.3 = (f32[8]{0:T(128)S(1)}, f32[8]{0:T(128)}, u32[]{:S(2)}) copy-start(f32[8]{0:T(128)} %observed.1) | copy-start | bytes 100
  53.6 2.0 %collective-permute-start.12 = (f32[4,264,128]{2,1,0:T(8,128)S(1)}, f32[4,264,128]{2,1,0:T(8,128)S(1)}, u32[]{:S(2)}, u32[]{:S(2)}) collective-permute-start(f32[4,264,128]{2,1,0:T(8,128)S(1)} %get-tuple-element.45), channel_id=1, source_target_pairs={{0,1},{1,0},{2,3},{3,2},{4,5},{5,4},{6,7},{7,6},{8,9},{9,8},{10,11... | collective-permute-start | bytes 1622024 | tf_op jit(solution)/shard_map/ppermute | solution.py:353
  55.7 6.5 %collective-permute-start.13 = (f32[264,128]{1,0:T(8,128)S(1)}, f32[264,128]{1,0:T(8,128)S(1)}, u32[]{:S(2)}, u32[]{:S(2)}) collective-permute-start(f32[264,128]{1,0:T(8,128)S(1)} %get-tuple-element.46), channel_id=1, source_target_pairs={{0,2},{1,3},{2,0},{3,1},{4,6},{5,7},{6,4},{7,5},{8,10},{9,11},{10,... | collective-permute-start | bytes 405512 | tf_op jit(solution)/shard_map/ppermute | solution.py:353
  56.7 7.8 %collective-permute-start.15 = (f32[264,128]{1,0:T(8,128)S(1)}, f32[264,128]{1,0:T(8,128)S(1)}, u32[]{:S(2)}, u32[]{:S(2)}) collective-permute-start(f32[264,128]{1,0:T(8,128)S(1)} %get-tuple-element.47), channel_id=1, source_target_pairs={{0,6},{1,7},{2,4},{3,5},{4,2},{5,3},{6,0},{7,1},{8,14},{9,15},{10,... | collective-permute-start | bytes 405512 | tf_op jit(solution)/shard_map/ppermute | solution.py:353
  57.9 8.0 %collective-permute-start.14 = (f32[264,128]{1,0:T(8,128)S(1)}, f32[264,128]{1,0:T(8,128)S(1)}, u32[]{:S(2)}, u32[]{:S(2)}) collective-permute-start(f32[264,128]{1,0:T(8,128)S(1)} %get-tuple-element.48), channel_id=1, source_target_pairs={{0,4},{1,5},{2,6},{3,7},{4,0},{5,1},{6,2},{7,3},{8,12},{9,13},{10,... | collective-permute-start | bytes 405512 | tf_op jit(solution)/shard_map/ppermute | solution.py:353
  65.9 5.0 %collective-permute-start.16 = (f32[2,128,128]{2,1,0:T(8,128)S(1)}, f32[2,128,128]{2,1,0:T(8,128)S(1)}, u32[]{:S(2)}, u32[]{:S(2)}) collective-permute-start(f32[2,128,128]{2,1,0:T(8,128)S(1)} %bitcast.24), channel_id=1, source_target_pairs={{0,8},{8,0},{16,24},{24,16},{1,9},{9,1},{17,25},{25,17},{2,10},{10... | collective-permute-start | bytes 393224 | tf_op jit(solution)/shard_map/ppermute | solution.py:353
  71.0 7.3 %collective-permute-start.17 = (f32[2,128,128]{2,1,0:T(8,128)S(1)}, f32[2,128,128]{2,1,0:T(8,128)S(1)}, u32[]{:S(2)}, u32[]{:S(2)}) collective-permute-start(f32[2,128,128]{2,1,0:T(8,128)S(1)} %add.28), channel_id=1, source_target_pairs={{0,16},{8,24},{16,0},{24,8},{1,17},{9,25},{17,1},{25,9},{2,18},{10... | collective-permute-start | bytes 393224 | tf_op jit(solution)/shard_map/ppermute | solution.py:353

commit v3 on v2

--- a/solution.py
+++ b/solution.py
@@ -8,6 +8,7 @@
 from jax.experimental.pallas import tpu as pltpu
 from jax.sharding import PartitionSpec as P
 
+
 ITERS = 2
 
 
@@ -17,12 +18,13 @@
 SPARE = 8
 ROWS = 256
 
+
 VMEM = pl.BlockSpec(memory_space=pltpu.VMEM)
 SMEM = pl.BlockSpec(memory_space=pltpu.SMEM)
-ANY = pl.BlockSpec(memory_space=pl.ANY)
-
-
-def call(body, out_shape, operands, in_specs, scratch=(), limit=8):
+HBM = pl.BlockSpec(memory_space=pltpu.HBM)
+
+
+def call(body, out_shape, operands, in_specs, scratch=(), limit=1):
     moved = sum(4 * a.size for a in operands) + sum(4 * o.size for o in out_shape)
     return pl.pallas_call(
         body,
@@ -92,7 +94,13 @@
     return here, result
 
 
-def stage_kernel(place, forward, adjoint, *refs):
+def my_place():
+    position = lax.axis_index("vox")
+    return lax.div(position, CORES), lax.rem(position, CORES), position
+
+
+def stage_kernel(forward, adjoint, *refs):
+    place = my_place()
     outs, sems = refs[:-1], refs[-1]
     own, give = outs[-2], outs[-1]
     sends = outs[:-2]
@@ -115,7 +123,8 @@
         copy.wait()
 
 
-def pack_kernel(place, own, got, *outs):
+def pack_kernel(own, got, *outs):
+    place = my_place()
     planes = own.shape[0]
     for step, out in enumerate(outs):
         other = place[0] ^ step
@@ -124,7 +133,8 @@
             out[1, plane] = got[plane, other]
 
 
-def sort_kernel(place, *refs):
+def sort_kernel(*refs):
+    place = my_place()
     blocks, keep, give = refs[:-2], refs[-2], refs[-1]
     for step, block in enumerate(blocks):
         for plane in range(block.shape[0]):
@@ -137,7 +147,8 @@
     return pl.ds(pl.multiple_of((level + 1) * height, height), height)
 
 
-def coefficient_kernel(place, own, others, depth, rows, columns, scale, root, sigma):
+def coefficient_kernel(own, others, depth, rows, columns, scale, root, sigma):
+    place = my_place()
     chips, planes, height, width = own.shape
     count = chips * CORES * planes
     clear_edges(depth, rows, columns, scale, root, sigma, height=height)
@@ -203,7 +214,7 @@
     width = field.shape[1]
     size = field.shape[0] - 2 * height
     nothing = jnp.zeros((8, width), jnp.float32)
-    clear_edges(field, residue, later, height=height)
+    clear_edges(field, residue, applied, height=height)
 
     def first(at, index, carry):
         here, sums = neighbours(at, field, depth, rows, columns, height)
@@ -226,23 +237,22 @@
     step_size = current / energy
 
     def third(at, index, carry):
-        squares, products = carry
-        product = at(applied)
-        left = at(residue) - step_size * product
-        at(later, value=left)
-        return squares + fold(left * left), products + fold(left * product)
-
-    squares, products = each_chunk(size, height, third, (nothing, nothing))
-    following, cross = total(squares), total(products)
+        squares, products, energies = carry
+
+        def left(offset=0):
+            return at(residue, offset) - step_size * at(applied, offset)
+
+        here = left()
+        at(later, value=here)
+        sums = at(depth, -height) * left(-height) + at(rows, -1) * left(-1)
+        sums += behind(at(columns) * here)
+        squares = squares + fold(here * here)
+        products = products + fold(here * at(applied))
+        return squares, products, energies + fold(here * (here - 2.0 * sums))
+
+    squares, products, energies = each_chunk(size, height, third, (nothing,) * 3)
+    following, cross, own = total(squares), total(products), total(energies)
     ratio = following / current
-
-    def fourth(at, index, acc):
-        here = at(later)
-        sums = at(depth, -height) * at(later, -height) + at(rows, -1) * at(later, -1)
-        sums += behind(at(columns) * here)
-        return acc + fold(here * (here - 2.0 * sums))
-
-    own = total(each_chunk(size, height, fourth, nothing))
     last_size = following / (own + ratio * (2.0 * cross + ratio * energy))
     first_size = step_size + last_size * ratio
 
@@ -255,12 +265,13 @@
 
 
 def electrode(place, electrodes, patterns, which):
-    return electrodes[patterns[place[2], which]]
-
-
-def forward_kernel(strength, place, electrodes, patterns, *refs):
+    return electrodes[patterns[which, place[2]]]
+
+
+def forward_kernel(strength, electrodes, patterns, *refs):
+    place = my_place()
     depth, rows, columns, scale, root, own, others = refs[:7]
-    result, slopes, voltage, field, residue, applied, later = refs[7:]
+    *slopes, voltage, field, residue, applied, later, result = refs[7:]
     chips, planes, height, width = own.shape
     for step in range(chips):
         for relative, source in enumerate((own, others)):
@@ -270,29 +281,41 @@
     plus, minus, high, low = (
         electrode(place, electrodes, patterns, which) for which in range(4)
     )
-    lane = lax.broadcasted_iota(jnp.int32, (1, width), 1)
-    weight = jnp.where(lane < width - 1, -0.5, 0.0)
 
     def end(at, potential):
         at(result, value=potential)
-        at(slopes, value=weight * (ahead(potential) - potential))
 
     solve_in_place(
         (depth, rows, columns, scale),
         ((plus, strength), (minus, -strength)),
         field, residue, applied, later, end, height,
     )
-    clear_edges(result, height=height)
+    clear_edges(result, *slopes, height=height)
+    count = chips * CORES * planes
+    row = lax.broadcasted_iota(jnp.int32, (height, 1), 0)
+    lane = lax.broadcasted_iota(jnp.int32, (1, width), 1)
+    row_weight = jnp.where(row < height - 1, -0.5, 0.0)
+    lane_weight = jnp.where(lane < width - 1, -0.5, 0.0)
+    along_depth, along_row, along_column = slopes
+
+    def slope(at, first, carry):
+        here = at(result)
+        depth_weight = jnp.where(first // height < count - 1, -0.5, 0.0)
+        at(along_depth, value=depth_weight * (at(result, height) - here))
+        at(along_row, value=row_weight * (at(result, 1) - here))
+        at(along_column, value=lane_weight * (ahead(here) - here))
+        return carry
+
+    each_chunk(count * height, height, slope, 0, height)
     seen = value_at(result, high, height) - value_at(result, low, height)
     voltage[...] = jnp.broadcast_to(seen, voltage.shape)
 
 
-def adjoint_kernel(weight, place, electrodes, patterns, observed, *refs):
-    depth, rows, columns, scale, root, forward, slopes, voltage = refs[:8]
-    *blocks, kept, given, field, residue, applied, later, adjoint = refs[8:]
-    chips = len(blocks)
-    planes, height, width = blocks[0].shape[1:]
-    count = chips * CORES * planes
+def adjoint_kernel(weight, electrodes, patterns, observed, *refs):
+    place = my_place()
+    depth, rows, columns, scale, root, *slopes, voltage = refs[:9]
+    *blocks, adjoint, given, field, residue, applied, later = refs[9:]
+    planes, height, _ = blocks[0].shape[1:]
     for step, block in enumerate(blocks):
         for relative in range(CORES):
             for plane in range(planes):
@@ -311,42 +334,40 @@
         field, residue, applied, later, end, height,
     )
     clear_edges(adjoint, height=height)
-    row = lax.broadcasted_iota(jnp.int32, (height, 1), 0)
-    row_ahead = jnp.where(row < height - 1, -0.5, 0.0)
-    row_behind = jnp.where(row > 0, -0.5, 0.0)
-
-    def step(at, first, carry):
-        level = first // height
-        left, right = at(forward), at(adjoint)
-
-        def product(offset):
-            return (at(forward, offset) - left) * (at(adjoint, offset) - right)
-
-        plane = jnp.where(level < count - 1, -0.5, 0.0) * product(height)
-        plane += jnp.where(level > 0, -0.5, 0.0) * product(-height)
-        plane += row_ahead * product(1) + row_behind * product(-1)
-        face = at(slopes) * (ahead(right) - right)
-        plane += face + behind(face)
-        block = (level // (CORES * planes)) ^ place[0]
-        owner = (level // planes) % CORES
-        start = pl.multiple_of((level % planes) * height, height)
-
-        @pl.when(owner == place[1])
-        def _():
-            kept[block, pl.ds(start, height), :] = plane
-
-        @pl.when(owner != place[1])
-        def _():
-            given[block, pl.ds(start, height), :] = plane
-
+    gradient_blocks(place, 1, slopes, voltage, adjoint, given, planes, height)
+
+
+def gradient_kernel(planes, height, *refs):
+    place = my_place()
+    *slopes, voltage, adjoint, kept = refs
+    gradient_blocks(place, 0, slopes, voltage, adjoint, kept, planes, height)
+
+
+def gradient_blocks(place, relative, slopes, voltage, adjoint, out, planes, height):
+    along_depth, along_row, along_column = slopes
+    chips, width = out.shape[0], out.shape[2]
+    size = planes * height
+
+    def step(block, carry):
+        start = plane_rows(place, block, relative, 0, planes, height).start
+
+        def at(ref, offset=0):
+            return ref[pl.ds(start + offset, size), :]
+
+        here = at(adjoint)
+        result = at(along_depth) * (at(adjoint, height) - here)
+        result += at(along_depth, -height) * (here - at(adjoint, -height))
+        result += at(along_row) * (at(adjoint, 1) - here)
+        result += at(along_row, -1) * (here - at(adjoint, -1))
+        face = at(along_column) * (ahead(here) - here)
+        out[block, :size, :] = result + (face + behind(face))
         return carry
 
-    each_chunk(count * height, height, step, 0, height)
+    lax.fori_loop(0, chips, step, 0)
     lane = lax.broadcasted_iota(jnp.int32, (SPARE, width), 1)
     note = jnp.where(lane == place[2], voltage[...], 0.0)
     for block in range(chips):
-        kept[block, planes * height :, :] = note
-        given[block, planes * height :, :] = note
+        out[block, size:, :] = note
 
 
 def swap(values, axis, size, bit):
@@ -361,9 +382,6 @@
     groups = lax.axis_size("pat")
     chips = layers // CORES
     strength = 2.0 * math.sqrt(layers * plane_count * row_count * column_count)
-    position = lax.axis_index("vox")
-    chip, core = position // CORES, position % CORES
-    place = jnp.stack([chip, core, position]).astype(jnp.int32)
     plane = (row_count, column_count)
     whole = shape(*padded(layers * plane_count, *plane))
     room = pltpu.VMEM(whole.shape, jnp.float32)
@@ -379,17 +397,17 @@
         stage_kernel,
         [shape(plane_count, CORES, *plane)] * chips
         + [shape(plane_count, chips, *plane)] * 2,
-        (place, warm_forward, warm_adjoint),
-        [SMEM, ANY, ANY],
+        (
+            pltpu.with_memory_space_constraint(warm_forward, pltpu.HBM),
+            pltpu.with_memory_space_constraint(warm_adjoint, pltpu.HBM),
+        ),
+        [HBM, HBM],
         scratch=[pltpu.SemaphoreType.DMA((chips + 2 * chips * plane_count,))],
     )
     blocks = [sends[0]] + [chip_swap(sends[step], step) for step in range(1, chips)]
     got = core_swap(give)
     packed = call(
-        pack_kernel,
-        [shape(CORES, plane_count, *plane)] * chips,
-        (place, own, got),
-        [SMEM, VMEM, VMEM],
+        pack_kernel, [shape(CORES, plane_count, *plane)] * chips, (own, got), [VMEM, VMEM]
     )
     adjoint_blocks = [packed[0]] + [chip_swap(packed[step], step) for step in range(1, chips)]
     own_sigma = jnp.stack(sigma)
@@ -397,33 +415,39 @@
     coefficients = call(
         coefficient_kernel,
         [whole] * 5,
-        (place, own_sigma, other_sigma),
-        [SMEM, VMEM, VMEM],
+        (own_sigma, other_sigma),
+        [VMEM, VMEM],
         scratch=[room],
-        limit=16,
+        limit=3,
     )
     half = shape(chips, plane_count, *plane)
-    keep, pass_on = call(sort_kernel, [half] * 2, (place, *blocks), [SMEM] + [VMEM] * chips)
+    keep, pass_on = call(sort_kernel, [half] * 2, tuple(blocks), [VMEM] * chips)
     received = core_swap(pass_on)
-    forward, slopes, voltage = call(
+    *slopes, voltage = call(
         functools.partial(forward_kernel, strength),
-        [whole, whole, shape(SPARE, column_count)],
-        (place, electrodes, patterns, *coefficients, keep, received),
-        [SMEM] * 3 + [VMEM] * 7,
+        [whole] * 3 + [shape(SPARE, column_count)],
+        (electrodes, patterns.T, *coefficients, keep, received),
+        [SMEM] * 2 + [VMEM] * 7,
+        scratch=[room] * 5,
+        limit=8,
+    )
+    block = shape(chips, plane_count * row_count + SPARE, column_count)
+    adjoint, given = call(
+        functools.partial(adjoint_kernel, 0.1 * strength),
+        [whole, block],
+        (
+            electrodes, patterns.T, observed,
+            *coefficients, *slopes, voltage, *adjoint_blocks,
+        ),
+        [SMEM] * 3 + [VMEM] * (9 + chips),
         scratch=[room] * 4,
-        limit=20,
-    )
-    block = shape(chips, plane_count * row_count + SPARE, column_count)
-    kept, given = call(
-        functools.partial(adjoint_kernel, 0.1 * strength),
-        [block] * 2,
-        (
-            place, electrodes, patterns, observed,
-            *coefficients, forward, slopes, voltage, *adjoint_blocks,
-        ),
-        [SMEM] * 4 + [VMEM] * (8 + chips),
-        scratch=[room] * 5,
-        limit=24,
+        limit=8,
+    )
+    (kept,) = call(
+        functools.partial(gradient_kernel, plane_count, row_count),
+        [block],
+        (*slopes, voltage, adjoint),
+        [VMEM] * 5,
     )
     summed = kept + core_swap(given)
     mine = summed[0]

time: 79.2 us -> 71.7 us (0.905)
  Pallas kernels: 24.4 us -> 18.1 us
  local copies, waits for them, and re-layouts: 3.1 us -> 0.57 us
  waiting for transfers between devices: 29.6 us -> 30.9 us
    pallas_call x6 -> x7, Pallas kernels: 24.4 us -> 18.1 us  [call(): pl.pallas_call(body, out_shape=out_shape, in_specs=in_specs, out_specs=[V...]
    unnamed x13 -> x8, local copies, waits for them, and re-layouts: 2.55 us -> 0.02 us
    ppermute x18, waiting for transfers between devices: 29.6 us -> 30.9 us  [swap(): return lax.ppermute(values, axis, [(i, i ^ bit) for i in range(size)])]
  transfers between devices with their start and end apart: 18 -> 18, of which waited for: 7 -> 9; matrix products, arithmetic and copies ran while one was open for 1% -> 1% of each run, Pallas kernels for 21% -> 18%
where the time goes in v3:
time: 71.7 us; the launch traced here: 71.6 us
  waiting for transfers between devices  30.9 us (43%)
  starting transfers between devices  20.3 us (28%)
  Pallas kernels  18.1 us (25%)
  other arithmetic  0.82 us (1%)
  between operations  0.82 us (1%)
    ppermute x18, waiting for transfers between devices, swap(): return lax.ppermute(values, axis, [(i, i ^ bit) for i in range(size)])  30.9 us
    ppermute x18, starting transfers between devices, swap(): return lax.ppermute(values, axis, [(i, i ^ bit) for i in range(size)])  20.3 us
    pallas_call x7, Pallas kernels, call(): pl.pallas_call(body, out_shape=out_shape, in_specs=in_specs, out_specs=[V...  18.1 us
  transfers between devices with their start and end apart: 18, of which 9 were waited for; matrix products, arithmetic and copies ran while one was open for 1% of the time, Pallas kernels for 18%

profile of v3, /device:TPU:0, one launch (start us, length us, event | category | flops | bytes accessed | tf_op | source)
XLA Modules:
  0.0 71.6 jit_solution(16245237462048443649)
XLA Ops:
  0.6 3.0 %collective-permute-start = (f32[2,128,128]{2,1,0:T(8,128)}, f32[2,128,128]{2,1,0:T(8,128)S(1)}, u32[]{:S(2)}, u32[]{:S(2)}) collective-permute-start(f32[2,128,128]{2,1,0:T(8,128)} %param.6), channel_id=1, source_target_pairs={{0,2},{1,3},{2,0},{3,1},{4,6},{5,7},{6,4},{7,5},{8,10},{9,11},{10,... | collective-permute-start | bytes 393224 | tf_op jit(solution)/shard_map/ppermute | solution.py:374
  3.7 1.5 %collective-permute-start.2 = (f32[2,128,128]{2,1,0:T(8,128)}, f32[2,128,128]{2,1,0:T(8,128)S(1)}, u32[]{:S(2)}, u32[]{:S(2)}) collective-permute-start(f32[2,128,128]{2,1,0:T(8,128)} %param.6), channel_id=1, source_target_pairs={{0,6},{1,7},{2,4},{3,5},{4,2},{5,3},{6,0},{7,1},{8,14},{9,15},{10,... | collective-permute-start | bytes 393224 | tf_op jit(solution)/shard_map/ppermute | solution.py:374
  5.2 1.6 %shard_map.78 = (f32[2,2,128,128]{3,2,1,0:T(8,128)S(1)}, f32[2,2,128,128]{3,2,1,0:T(8,128)S(1)}, f32[2,2,128,128]{3,2,1,0:T(8,128)S(1)}, f32[2,2,128,128]{3,2,1,...) custom-call(f32[2,8,128,128]{3,2,1,0:T(8,128)} %forward.1, f32[2,8,128,128]{3,2,1,0:T(8,128)} %adjoint.1), custom_call_target="tpu_custom_call" | custom-call | flops 4194304 | bytes 4194304 | tf_op jit(solution)/shard_map/pallas_call | solution.py:29
  6.8 1.6 %collective-permute-start.4 = (f32[2,2,128,128]{3,2,1,0:T(8,128)S(1)}, f32[2,2,128,128]{3,2,1,0:T(8,128)S(1)}, u32[]{:S(2)}, u32[]{:S(2)}) collective-permute-start(f32[2,2,128,128]{3,2,1,0:T(8,128)S(1)} %get-tuple-element.31), channel_id=1, source_target_pairs={{0,2},{1,3},{2,0},{3,1},{4,6},{5,7},{6,4},{7,5},{8,10},{9,11},{10,... | collective-permute-start | bytes 786440 | tf_op jit(solution)/shard_map/ppermute | solution.py:374
  8.9 1.5 %collective-permute-start.6 = (f32[2,2,128,128]{3,2,1,0:T(8,128)S(1)}, f32[2,2,128,128]{3,2,1,0:T(8,128)S(1)}, u32[]{:S(2)}, u32[]{:S(2)}) collective-permute-start(f32[2,2,128,128]{3,2,1,0:T(8,128)S(1)} %get-tuple-element.33), channel_id=1, source_target_pairs={{0,6},{1,7},{2,4},{3,5},{4,2},{5,3},{6,0},{7,1},{8,14},{9,15},{10,... | collective-permute-start | bytes 786440 | tf_op jit(solution)/shard_map/ppermute | solution.py:374
  10.4 2.2 %collective-permute-done.2 = f32[2,128,128]{2,1,0:T(8,128)S(1)} collective-permute-done((f32[2,128,128]{2,1,0:T(8,128)}, f32[2,128,128]{2,1,0:T(8,128)S(1)}, u32[]{:S(2)}, u32[]{:S(2)}) %collective-permute-start.2) | collective-permute-done | bytes 131104 | tf_op jit(solution)/shard_map/ppermute | solution.py:374
  12.7 12.8 %collective-permute-done.1 = f32[2,128,128]{2,1,0:T(8,128)S(1)} collective-permute-done((f32[2,128,128]{2,1,0:T(8,128)S(1)}, f32[2,128,128]{2,1,0:T(8,128)S(1)}, u32[]{:S(2)}, u32[]{:S(2)}) %collective-permute-start.1) | collective-permute-done | bytes 131104 | tf_op jit(solution)/shard_map/ppermute | solution.py:374
  26.3 1.2 %collective-permute-start.9 = (f32[2,2,128,128]{3,2,1,0:T(8,128)S(1)}, f32[2,2,128,128]{3,2,1,0:T(8,128)S(1)}, u32[]{:S(2)}, u32[]{:S(2)}) collective-permute-start(f32[2,2,128,128]{3,2,1,0:T(8,128)S(1)} %get-tuple-element.43), channel_id=1, source_target_pairs={{0,2},{1,3},{2,0},{3,1},{4,6},{5,7},{6,4},{7,5},{8,10},{9,11},{10,... | collective-permute-start | bytes 786440 | tf_op jit(solution)/shard_map/ppermute | solution.py:374
  27.9 1.9 %collective-permute-start.11 = (f32[2,2,128,128]{3,2,1,0:T(8,128)S(1)}, f32[2,2,128,128]{3,2,1,0:T(8,128)S(1)}, u32[]{:S(2)}, u32[]{:S(2)}) collective-permute-start(f32[2,2,128,128]{3,2,1,0:T(8,128)S(1)} %get-tuple-element.45), channel_id=1, source_target_pairs={{0,6},{1,7},{2,4},{3,5},{4,2},{5,3},{6,0},{7,1},{8,14},{9,15},{10,... | collective-permute-start | bytes 786440 | tf_op jit(solution)/shard_map/ppermute | solution.py:374
  29.9 4.5 %shard_map.77 = (f32[2304,128]{1,0:T(8,128)S(1)}, f32[2304,128]{1,0:T(8,128)S(1)}, f32[2304,128]{1,0:T(8,128)S(1)}, f32[2304,128]{1,0:T(8,128)S(1)}, f32[2304,128]{1,0:T(8,128)S(1)}) custom-call(f32[4,2,128,128]{3,2,1,0:T(8,128)S(1)} %pad_maximum_fusion.own, f32[4,2,128,128]{3,2,1,0:T(8,128)S(1)} %collective-permute-done.3.others), custom_call_target="tpu_custom_call" | custom-call | flops 6946816 | bytes 6946816 | tf_op jit(solution)/shard_map/pallas_call | solution.py:29
  34.4 5.9 %shard_map.80 = (f32[2304,128]{1,0:T(8,128)S(1)}, f32[2304,128]{1,0:T(8,128)S(1)}, f32[2304,128]{1,0:T(8,128)S(1)}, f32[8,128]{1,0:T(8,128)S(1)}) custom-call(s32[128]{0:T(128)S(1)} %copy-done.1, s32[4,8]{1,0:T(4,128)S(1)} %bitcast.22, f32[2304,128]{1,0:T(8,128)S(1)} %get-tuple-element.25.refs_0_, f32[2304,128]{1,0:T(8,128)S(1)} %get-tuple-element.26.refs_1_, ...), custom_call_target="tpu_custom_call" | custom-call | flops 10490496 | bytes 10490496 | tf_op jit(solution)/shard_map/pallas_call | solution.py:29
  41.1 5.2 %shard_map.82 = (f32[2304,128]{1,0:T(8,128)S(1)}, f32[4,264,128]{2,1,0:T(8,128)S(1)}) custom-call(s32[128]{0:T(128)S(1)} %copy-done.1, s32[4,8]{1,0:T(4,128)S(1)} %bitcast.23, f32[8]{0:T(128)S(1)} %copy-done.2, f32[2304,128]{1,0:T(8,128)S(1)} %get-tuple-element.25.refs_0_, f32[2304,128]{1,0:T(8,128)S(1)} %get-tuple-element.26.refs_1_, ...), custom_call_target="tpu_custom_call" | custom-call | flops 12210848 | bytes 12210848 | tf_op jit(solution)/shard_map/pallas_call | solution.py:29
  46.3 0.8 %shard_map.83 = f32[4,264,128]{2,1,0:T(8,128)S(1)} custom-call(f32[2304,128]{1,0:T(8,128)S(1)} %get-tuple-element.36.refs_5_.refs_0_, f32[2304,128]{1,0:T(8,128)S(1)} %get-tuple-element.37.refs_6_.refs_1_, f32[2304,128]{1,0:T(8,128)S(1)} %get-tuple-element.38.refs_7_.refs_2_, f32[8,128]{1,0:T(8,128)S(1)} %get-tuple-element.39.refs_8_.refs_3_, ...), custom_call_target="tpu_custom_call" | custom-call | flops 5263360 | bytes 5263360 | tf_op jit(solution)/shard_map/pallas_call | solution.py:29
  47.1 1.2 %collective-permute-done.12 = f32[4,264,128]{2,1,0:T(8,128)S(1)} collective-permute-done((f32[4,264,128]{2,1,0:T(8,128)S(1)}, f32[4,264,128]{2,1,0:T(8,128)S(1)}, u32[]{:S(2)}, u32[]{:S(2)}) %collective-permute-start.12) | collective-permute-done | bytes 540704 | tf_op jit(solution)/shard_map/ppermute | solution.py:374
  48.4 1.0 %collective-permute-start.13 = (f32[264,128]{1,0:T(8,128)S(1)}, f32[264,128]{1,0:T(8,128)S(1)}, u32[]{:S(2)}, u32[]{:S(2)}) collective-permute-start(f32[264,128]{1,0:T(8,128)S(1)} %get-tuple-element.48), channel_id=1, source_target_pairs={{0,2},{1,3},{2,0},{3,1},{4,6},{5,7},{6,4},{7,5},{8,10},{9,11},{10,... | collective-permute-start | bytes 405512 | tf_op jit(solution)/shard_map/ppermute | solution.py:374
  49.3 1.2 %collective-permute-start.15 = (f32[264,128]{1,0:T(8,128)S(1)}, f32[264,128]{1,0:T(8,128)S(1)}, u32[]{:S(2)}, u32[]{:S(2)}) collective-permute-start(f32[264,128]{1,0:T(8,128)S(1)} %get-tuple-element.49), channel_id=1, source_target_pairs={{0,6},{1,7},{2,4},{3,5},{4,2},{5,3},{6,0},{7,1},{8,14},{9,15},{10,... | collective-permute-start | bytes 405512 | tf_op jit(solution)/shard_map/ppermute | solution.py:374
  50.5 1.4 %collective-permute-start.14 = (f32[264,128]{1,0:T(8,128)S(1)}, f32[264,128]{1,0:T(8,128)S(1)}, u32[]{:S(2)}, u32[]{:S(2)}) collective-permute-start(f32[264,128]{1,0:T(8,128)S(1)} %get-tuple-element.50), channel_id=1, source_target_pairs={{0,4},{1,5},{2,6},{3,7},{4,0},{5,1},{6,2},{7,3},{8,12},{9,13},{10,... | collective-permute-start | bytes 405512 | tf_op jit(solution)/shard_map/ppermute | solution.py:374
  51.9 3.0 %collective-permute-done.13 = f32[264,128]{1,0:T(8,128)S(1)} collective-permute-done((f32[264,128]{1,0:T(8,128)S(1)}, f32[264,128]{1,0:T(8,128)S(1)}, u32[]{:S(2)}, u32[]{:S(2)}) %collective-permute-start.13) | collective-permute-done | bytes 135200 | tf_op jit(solution)/shard_map/ppermute | solution.py:374
  54.9 2.2 %collective-permute-done.15 = f32[264,128]{1,0:T(8,128)S(1)} collective-permute-done((f32[264,128]{1,0:T(8,128)S(1)}, f32[264,128]{1,0:T(8,128)S(1)}, u32[]{:S(2)}, u32[]{:S(2)}) %collective-permute-start.15) | collective-permute-done | bytes 135200 | tf_op jit(solution)/shard_map/ppermute | solution.py:374
  57.1 1.4 %collective-permute-done.14 = f32[264,128]{1,0:T(8,128)S(1)} collective-permute-done((f32[264,128]{1,0:T(8,128)S(1)}, f32[264,128]{1,0:T(8,128)S(1)}, u32[]{:S(2)}, u32[]{:S(2)}) %collective-permute-start.14) | collective-permute-done | bytes 135200 | tf_op jit(solution)/shard_map/ppermute | solution.py:374
  58.5 1.6 %collective-permute-start.16 = (f32[2,128,128]{2,1,0:T(8,128)S(1)}, f32[2,128,128]{2,1,0:T(8,128)S(1)}, u32[]{:S(2)}, u32[]{:S(2)}) collective-permute-start(f32[2,128,128]{2,1,0:T(8,128)S(1)} %bitcast.24), channel_id=1, source_target_pairs={{0,8},{8,0},{16,24},{24,16},{1,9},{9,1},{17,25},{25,17},{2,10},{10... | collective-permute-start | bytes 393224 | tf_op jit(solution)/shard_map/ppermute | solution.py:374
  60.2 3.4 %collective-permute-done.16 = f32[2,128,128]{2,1,0:T(8,128)S(1)} collective-permute-done((f32[2,128,128]{2,1,0:T(8,128)S(1)}, f32[2,128,128]{2,1,0:T(8,128)S(1)}, u32[]{:S(2)}, u32[]{:S(2)}) %collective-permute-start.16) | collective-permute-done | bytes 131104 | tf_op jit(solution)/shard_map/ppermute | solution.py:374
  63.6 2.7 %collective-permute-start.17 = (f32[2,128,128]{2,1,0:T(8,128)S(1)}, f32[2,128,128]{2,1,0:T(8,128)S(1)}, u32[]{:S(2)}, u32[]{:S(2)}) collective-permute-start(f32[2,128,128]{2,1,0:T(8,128)S(1)} %add.22), channel_id=1, source_target_pairs={{0,16},{8,24},{16,0},{24,8},{1,17},{9,25},{17,1},{25,9},{2,18},{10... | collective-permute-start | bytes 393224 | tf_op jit(solution)/shard_map/ppermute | solution.py:374
  66.7 4.2 %collective-permute-done.17 = f32[2,128,128]{2,1,0:T(8,128)S(1)} collective-permute-done((f32[2,128,128]{2,1,0:T(8,128)S(1)}, f32[2,128,128]{2,1,0:T(8,128)S(1)}, u32[]{:S(2)}, u32[]{:S(2)}) %collective-permute-start.17) | collective-permute-done | bytes 131104 | tf_op jit(solution)/shard_map/ppermute | solution.py:374
  (35 shorter events, 4.1 us)
Async XLA Ops:
  0.6 11.9 %copy-start.3 = (f32[2,128,128]{2,1,0:T(8,128)S(1)}, f32[2,128,128]{2,1,0:T(8,128)}, u32[]{:S(2)}) copy-start(f32[2,128,128]{2,1,0:T(8,128)} %param.6) | copy-start | bytes 393220
  0.6 9.7 %collective-permute-start = (f32[2,128,128]{2,1,0:T(8,128)}, f32[2,128,128]{2,1,0:T(8,128)S(1)}, u32[]{:S(2)}, u32[]{:S(2)}) collective-permute-start(f32[2,128,128]{2,1,0:T(8,128)} %param.6), channel_id=1, source_target_pairs={{0,2},{1,3},{2,0},{3,1},{4,6},{5,7},{6,4},{7,5},{8,10},{9,11},{10,... | collective-permute-start | bytes 393224 | tf_op jit(solution)/shard_map/ppermute | solution.py:374
  3.7 8.9 %collective-permute-start.2 = (f32[2,128,128]{2,1,0:T(8,128)}, f32[2,128,128]{2,1,0:T(8,128)S(1)}, u32[]{:S(2)}, u32[]{:S(2)}) collective-permute-start(f32[2,128,128]{2,1,0:T(8,128)} %param.6), channel_id=1, source_target_pairs={{0,6},{1,7},{2,4},{3,5},{4,2},{5,3},{6,0},{7,1},{8,14},{9,15},{10,... | collective-permute-start | bytes 393224 | tf_op jit(solution)/shard_map/ppermute | solution.py:374
  6.8 18.7 %collective-permute-start.4 = (f32[2,2,128,128]{3,2,1,0:T(8,128)S(1)}, f32[2,2,128,128]{3,2,1,0:T(8,128)S(1)}, u32[]{:S(2)}, u32[]{:S(2)}) collective-permute-start(f32[2,2,128,128]{3,2,1,0:T(8,128)S(1)} %get-tuple-element.31), channel_id=1, source_target_pairs={{0,2},{1,3},{2,0},{3,1},{4,6},{5,7},{6,4},{7,5},{8,10},{9,11},{10,... | collective-permute-start | bytes 786440 | tf_op jit(solution)/shard_map/ppermute | solution.py:374
  8.4 17.2 %collective-permute-start.5 = (f32[2,2,128,128]{3,2,1,0:T(8,128)S(1)}, f32[2,2,128,128]{3,2,1,0:T(8,128)S(1)}, u32[]{:S(2)}, u32[]{:S(2)}) collective-permute-start(f32[2,2,128,128]{3,2,1,0:T(8,128)S(1)} %get-tuple-element.32), channel_id=1, source_target_pairs={{0,4},{1,5},{2,6},{3,7},{4,0},{5,1},{6,2},{7,3},{8,12},{9,13},{10,... | collective-permute-start | bytes 786440 | tf_op jit(solution)/shard_map/ppermute | solution.py:374
  8.9 16.7 %collective-permute-start.6 = (f32[2,2,128,128]{3,2,1,0:T(8,128)S(1)}, f32[2,2,128,128]{3,2,1,0:T(8,128)S(1)}, u32[]{:S(2)}, u32[]{:S(2)}) collective-permute-start(f32[2,2,128,128]{3,2,1,0:T(8,128)S(1)} %get-tuple-element.33), channel_id=1, source_target_pairs={{0,6},{1,7},{2,4},{3,5},{4,2},{5,3},{6,0},{7,1},{8,14},{9,15},{10,... | collective-permute-start | bytes 786440 | tf_op jit(solution)/shard_map/ppermute | solution.py:374
  10.4 15.9 %collective-permute-start.8 = (f32[2,4,128,128]{3,2,1,0:T(8,128)S(1)}, f32[2,4,128,128]{3,2,1,0:T(8,128)S(1)}, u32[]{:S(2)}, u32[]{:S(2)}) collective-permute-start(f32[2,4,128,128]{3,2,1,0:T(8,128)S(1)} %get-tuple-element.41), channel_id=1, source_target_pairs={{0,1},{1,0},{2,3},{3,2},{4,5},{5,4},{6,7},{7,6},{8,9},{9,8},{10,11... | collective-permute-start | bytes 1572872 | tf_op jit(solution)/shard_map/ppermute | solution.py:374
  12.5 12.9 %collective-permute-start.1 = (f32[2,128,128]{2,1,0:T(8,128)S(1)}, f32[2,128,128]{2,1,0:T(8,128)S(1)}, u32[]{:S(2)}, u32[]{:S(2)}) collective-permute-start(f32[2,128,128]{2,1,0:T(8,128)S(1)} %copy-done.3), channel_id=1, source_target_pairs={{0,4},{1,5},{2,6},{3,7},{4,0},{5,1},{6,2},{7,3},{8,12},{9,13},{10,... | collective-permute-start | bytes 393224 | tf_op jit(solution)/shard_map/ppermute | solution.py:374
  25.5 4.4 %collective-permute-start.3 = (f32[4,2,128,128]{3,2,1,0:T(8,128)S(1)}, f32[4,2,128,128]{3,2,1,0:T(8,128)S(1)}, u32[]{:S(2)}, u32[]{:S(2)}) collective-permute-start(f32[4,2,128,128]{3,2,1,0:T(8,128)S(1)} %pad_maximum_fusion.own), channel_id=1, source_target_pairs={{0,1},{1,0},{2,3},{3,2},{4,5},{5,4},{6,7},{7,6},{8,9},{9,8},{10,11... | collective-permute-start | bytes 1572872 | tf_op jit(solution)/shard_map/ppermute | solution.py:374
  25.7 8.7 %copy-start = (s32[8,4]{0,1:T(4,128)S(1)}, s32[8,4]{0,1:T(4,128)}, u32[]{:S(2)}) copy-start(s32[8,4]{0,1:T(4,128)} %param.10) | copy-start | bytes 388
  25.7 8.7 %copy-start.1 = (s32[128]{0:T(128)S(1)}, s32[128]{0:T(128)}, u32[]{:S(2)}) copy-start(s32[128]{0:T(128)} %electrodes.3) | copy-start | bytes 1540
  25.7 8.7 %collective-permute-start.7 = (f32[4,2,128,128]{3,2,1,0:T(8,128)S(1)}, f32[4,2,128,128]{3,2,1,0:T(8,128)S(1)}, u32[]{:S(2)}, u32[]{:S(2)}) collective-permute-start(f32[4,2,128,128]{3,2,1,0:T(8,128)S(1)} %get-tuple-element.35), channel_id=1, source_target_pairs={{0,1},{1,0},{2,3},{3,2},{4,5},{5,4},{6,7},{7,6},{8,9},{9,8},{10,11... | collective-permute-start | bytes 1572872 | tf_op jit(solution)/shard_map/ppermute | solution.py:374
  26.3 14.0 %collective-permute-start.9 = (f32[2,2,128,128]{3,2,1,0:T(8,128)S(1)}, f32[2,2,128,128]{3,2,1,0:T(8,128)S(1)}, u32[]{:S(2)}, u32[]{:S(2)}) collective-permute-start(f32[2,2,128,128]{3,2,1,0:T(8,128)S(1)} %get-tuple-element.43), channel_id=1, source_target_pairs={{0,2},{1,3},{2,0},{3,1},{4,6},{5,7},{6,4},{7,5},{8,10},{9,11},{10,... | collective-permute-start | bytes 786440 | tf_op jit(solution)/shard_map/ppermute | solution.py:374
  27.5 13.6 %collective-permute-start.10 = (f32[2,2,128,128]{3,2,1,0:T(8,128)S(1)}, f32[2,2,128,128]{3,2,1,0:T(8,128)S(1)}, u32[]{:S(2)}, u32[]{:S(2)}) collective-permute-start(f32[2,2,128,128]{3,2,1,0:T(8,128)S(1)} %get-tuple-element.44), channel_id=1, source_target_pairs={{0,4},{1,5},{2,6},{3,7},{4,0},{5,1},{6,2},{7,3},{8,12},{9,13},{10,... | collective-permute-start | bytes 786440 | tf_op jit(solution)/shard_map/ppermute | solution.py:374
  27.9 13.2 %collective-permute-start.11 = (f32[2,2,128,128]{3,2,1,0:T(8,128)S(1)}, f32[2,2,128,128]{3,2,1,0:T(8,128)S(1)}, u32[]{:S(2)}, u32[]{:S(2)}) collective-permute-start(f32[2,2,128,128]{3,2,1,0:T(8,128)S(1)} %get-tuple-element.45), channel_id=1, source_target_pairs={{0,6},{1,7},{2,4},{3,5},{4,2},{5,3},{6,0},{7,1},{8,14},{9,15},{10,... | collective-permute-start | bytes 786440 | tf_op jit(solution)/shard_map/ppermute | solution.py:374
  34.4 6.7 %copy-start.2 = (f32[8]{0:T(128)S(1)}, f32[8]{0:T(128)}, u32[]{:S(2)}) copy-start(f32[8]{0:T(128)} %observed.1) | copy-start | bytes 100
  46.3 2.0 %collective-permute-start.12 = (f32[4,264,128]{2,1,0:T(8,128)S(1)}, f32[4,264,128]{2,1,0:T(8,128)S(1)}, u32[]{:S(2)}, u32[]{:S(2)}) collective-permute-start(f32[4,264,128]{2,1,0:T(8,128)S(1)} %get-tuple-element.47), channel_id=1, source_target_pairs={{0,1},{1,0},{2,3},{3,2},{4,5},{5,4},{6,7},{7,6},{8,9},{9,8},{10,11... | collective-permute-start | bytes 1622024 | tf_op jit(solution)/shard_map/ppermute | solution.py:374
  48.4 6.5 %collective-permute-start.13 = (f32[264,128]{1,0:T(8,128)S(1)}, f32[264,128]{1,0:T(8,128)S(1)}, u32[]{:S(2)}, u32[]{:S(2)}) collective-permute-start(f32[264,128]{1,0:T(8,128)S(1)} %get-tuple-element.48), channel_id=1, source_target_pairs={{0,2},{1,3},{2,0},{3,1},{4,6},{5,7},{6,4},{7,5},{8,10},{9,11},{10,... | collective-permute-start | bytes 405512 | tf_op jit(solution)/shard_map/ppermute | solution.py:374
  49.3 7.8 %collective-permute-start.15 = (f32[264,128]{1,0:T(8,128)S(1)}, f32[264,128]{1,0:T(8,128)S(1)}, u32[]{:S(2)}, u32[]{:S(2)}) collective-permute-start(f32[264,128]{1,0:T(8,128)S(1)} %get-tuple-element.49), channel_id=1, source_target_pairs={{0,6},{1,7},{2,4},{3,5},{4,2},{5,3},{6,0},{7,1},{8,14},{9,15},{10,... | collective-permute-start | bytes 405512 | tf_op jit(solution)/shard_map/ppermute | solution.py:374
  50.5 8.0 %collective-permute-start.14 = (f32[264,128]{1,0:T(8,128)S(1)}, f32[264,128]{1,0:T(8,128)S(1)}, u32[]{:S(2)}, u32[]{:S(2)}) collective-permute-start(f32[264,128]{1,0:T(8,128)S(1)} %get-tuple-element.50), channel_id=1, source_target_pairs={{0,4},{1,5},{2,6},{3,7},{4,0},{5,1},{6,2},{7,3},{8,12},{9,13},{10,... | collective-permute-start | bytes 405512 | tf_op jit(solution)/shard_map/ppermute | solution.py:374
  58.5 5.0 %collective-permute-start.16 = (f32[2,128,128]{2,1,0:T(8,128)S(1)}, f32[2,128,128]{2,1,0:T(8,128)S(1)}, u32[]{:S(2)}, u32[]{:S(2)}) collective-permute-start(f32[2,128,128]{2,1,0:T(8,128)S(1)} %bitcast.24), channel_id=1, source_target_pairs={{0,8},{8,0},{16,24},{24,16},{1,9},{9,1},{17,25},{25,17},{2,10},{10... | collective-permute-start | bytes 393224 | tf_op jit(solution)/shard_map/ppermute | solution.py:374
  63.6 7.3 %collective-permute-start.17 = (f32[2,128,128]{2,1,0:T(8,128)S(1)}, f32[2,128,128]{2,1,0:T(8,128)S(1)}, u32[]{:S(2)}, u32[]{:S(2)}) collective-permute-start(f32[2,128,128]{2,1,0:T(8,128)S(1)} %add.22), channel_id=1, source_target_pairs={{0,16},{8,24},{16,0},{24,8},{1,17},{9,25},{17,1},{25,9},{2,18},{10... | collective-permute-start | bytes 393224 | tf_op jit(solution)/shard_map/ppermute | solution.py:374

commit v4 on v3

--- a/solution.py
+++ b/solution.py
@@ -99,28 +99,35 @@
     return lax.div(position, CORES), lax.rem(position, CORES), position
 
 
-def stage_kernel(forward, adjoint, *refs):
-    place = my_place()
-    outs, sems = refs[:-1], refs[-1]
-    own, give = outs[-2], outs[-1]
-    sends = outs[:-2]
-    chip, core = place[0], place[1]
-    planes, chips = own.shape[:2]
-    copies = []
-    for step, out in enumerate(sends):
-        copies.append((forward.at[:, pl.ds(CORES * (chip ^ step), CORES)], out))
-    for plane in range(planes):
-        for other in range(chips):
-            copies.append((adjoint.at[plane, CORES * other + 1 - core], give.at[plane, other]))
-            copies.append((adjoint.at[plane, CORES * other + core], own.at[plane, other]))
-    started = [
+def copy_all(pairs, sems):
+    copies = [
         pltpu.make_async_copy(source, target, sems.at[number])
-        for number, (source, target) in enumerate(copies)
+        for number, (source, target) in enumerate(pairs)
     ]
-    for copy in started:
+    for copy in copies:
         copy.start()
-    for copy in started:
+    for copy in copies:
         copy.wait()
+
+
+def stage_kernel(share, conductivity, forward, fetched, *refs):
+    chip = my_place()[0]
+    size = fetched.shape[0]
+    first = lax.rem(lax.axis_index("pat"), share) * size
+    pairs = [(conductivity.at[pl.ds(first, size)], fetched)]
+    for step, out in enumerate(refs[:-1]):
+        pairs.append((forward.at[:, pl.ds(CORES * (chip ^ step), CORES)], out))
+    copy_all(pairs, refs[-1])
+
+
+def stage_adjoint_kernel(adjoint, own, give, sems):
+    core = my_place()[1]
+    pairs = []
+    for plane in range(own.shape[0]):
+        for other in range(own.shape[1]):
+            pairs.append((adjoint.at[plane, CORES * other + 1 - core], give.at[plane, other]))
+            pairs.append((adjoint.at[plane, CORES * other + core], own.at[plane, other]))
+    copy_all(pairs, sems)
 
 
 def pack_kernel(own, got, *outs):
@@ -147,32 +154,38 @@
     return pl.ds(pl.multiple_of((level + 1) * height, height), height)
 
 
-def coefficient_kernel(own, others, depth, rows, columns, scale, root, sigma):
+def coefficient_kernel(chips, share, own, others, depth, rows, columns, scale, root, sigma):
     place = my_place()
-    chips, planes, height, width = own.shape
+    total_planes, height, width = own.shape
+    planes = total_planes // chips
     count = chips * CORES * planes
+    part_planes = planes // share
+    mine = lax.rem(lax.axis_index("pat"), share)
     clear_edges(depth, rows, columns, scale, root, sigma, height=height)
-    for step in range(chips):
-        for relative, source in enumerate((own, others)):
-            for plane in range(planes):
-                sigma[plane_rows(place, step, relative, plane, planes, height), :] = source[
-                    step, plane
-                ]
+    fetched = [(0, plane) for plane in range(planes)]
+    for half in range(share):
+        owner = lax.rem(mine + half, share)
+        for step in range(1, chips):
+            fetched += [(step, owner * part_planes + plane) for plane in range(part_planes)]
+    for relative, source in enumerate((own, others)):
+        for number, (step, plane) in enumerate(fetched):
+            sigma[plane_rows(place, step, relative, plane, planes, height), :] = source[number]
     row = lax.broadcasted_iota(jnp.int32, (height, width), 0)
     lane = lax.broadcasted_iota(jnp.int32, (height, width), 1)
     row_ahead, row_behind, lane_ahead = row < height - 1, row > 0, lane < width - 1
 
     def diagonals(at, first, carry):
-        level = first // height
         here = at(sigma)
-        along_depth = jnp.where(level > 0, 0.5, 0.0) * (here + at(sigma, -height))
-        along_depth += jnp.where(level < count - 1, 0.5, 0.0) * (here + at(sigma, height))
-        along_row = jnp.where(row_behind, 0.5 * (here + at(sigma, -1)), 0.0)
-        along_row += jnp.where(row_ahead, 0.5 * (here + at(sigma, 1)), 0.0)
+        upper = jnp.where(first // height < count - 1, 0.5, 0.0) * (here + at(sigma, height))
+        row_face = jnp.where(row_ahead, 0.5 * (here + at(sigma, 1)), 0.0)
+        row_faces = row_face + jnp.where(row_behind, 0.5 * (here + at(sigma, -1)), 0.0)
         face = jnp.where(lane_ahead, 0.5 * (here + ahead(here)), 0.0)
-        diagonal = leakage + along_depth + along_row + (behind(face) + face)
+        diagonal = leakage + (at(depth, -height) + upper) + row_faces + (behind(face) + face)
         inverse = lax.rsqrt(diagonal)
         inverse = inverse * (1.5 - 0.5 * diagonal * inverse * inverse)
+        at(depth, value=upper)
+        at(rows, value=row_face)
+        at(columns, value=face)
         at(scale, value=inverse)
         at(root, value=diagonal * inverse)
         return carry
@@ -180,17 +193,13 @@
     each_chunk(count * height, height, diagonals, 0, height)
 
     def couplings(at, first, carry):
-        here, size = at(sigma), at(scale)
-        half = 0.5 * size
-        upper = jnp.where(first // height < count - 1, half, 0.0)
-        at(depth, value=upper * ((here + at(sigma, height)) * at(scale, height)))
-        face = half * ((here + at(sigma, 1)) * at(scale, 1))
-        at(rows, value=jnp.where(row_ahead, face, 0.0))
-        face = half * ((here + ahead(here)) * ahead(size))
-        at(columns, value=jnp.where(lane_ahead, face, 0.0))
+        size = at(scale)
+        at(depth, value=at(depth) * (size * at(scale, height)))
+        at(rows, value=at(rows) * (size * at(scale, 1)))
+        at(columns, value=at(columns) * (size * ahead(size)))
         return carry
 
-    each_chunk(count * height, height, couplings, 0, height)
+    each_chunk(count * height, height, couplings, 0)
 
 
 def spot(ref, cell, height):
@@ -392,36 +401,54 @@
     def core_swap(values):
         return swap(values, "vox", layers, 1)
 
-    sigma = [conductivity] + [chip_swap(conductivity, step) for step in range(1, chips)]
-    *sends, own, give = call(
-        stage_kernel,
-        [shape(plane_count, CORES, *plane)] * chips
-        + [shape(plane_count, chips, *plane)] * 2,
-        (
-            pltpu.with_memory_space_constraint(warm_forward, pltpu.HBM),
-            pltpu.with_memory_space_constraint(warm_adjoint, pltpu.HBM),
-        ),
+    share = 2 if groups % 2 == 0 and plane_count % 2 == 0 else 1
+
+    def in_place(values):
+        return pltpu.with_memory_space_constraint(values, pltpu.HBM)
+
+    fetched, *sends = call(
+        functools.partial(stage_kernel, share),
+        [shape(plane_count // share, *plane)] + [shape(plane_count, CORES, *plane)] * chips,
+        (in_place(conductivity), in_place(warm_forward)),
         [HBM, HBM],
-        scratch=[pltpu.SemaphoreType.DMA((chips + 2 * chips * plane_count,))],
-    )
-    blocks = [sends[0]] + [chip_swap(sends[step], step) for step in range(1, chips)]
+        scratch=[pltpu.SemaphoreType.DMA((1 + chips,))],
+    )
+    order = list(reversed(range(1, chips)))
+    fetched = {step: chip_swap(fetched, step) for step in order}
+    fetched = [fetched[step] for step in range(1, chips)]
+    blocks = {step: chip_swap(sends[step], step) for step in order}
+    blocks = [sends[0]] + [blocks[step] for step in range(1, chips)]
+    own, give = call(
+        stage_adjoint_kernel,
+        [shape(plane_count, chips, *plane)] * 2,
+        (in_place(warm_adjoint),),
+        [HBM],
+        scratch=[pltpu.SemaphoreType.DMA((2 * chips * plane_count,))],
+    )
     got = core_swap(give)
     packed = call(
         pack_kernel, [shape(CORES, plane_count, *plane)] * chips, (own, got), [VMEM, VMEM]
     )
-    adjoint_blocks = [packed[0]] + [chip_swap(packed[step], step) for step in range(1, chips)]
-    own_sigma = jnp.stack(sigma)
+    adjoint_blocks = {0: packed[0]}
+    for step in order:
+        adjoint_blocks[step] = chip_swap(packed[step], step)
+    adjoint_blocks = [adjoint_blocks[step] for step in range(chips)]
+    others = [swap(jnp.concatenate(fetched), "pat", groups, 1)] if share == 2 else []
+    own_sigma = jnp.concatenate([conductivity] + fetched + others)
     other_sigma = core_swap(own_sigma)
     coefficients = call(
-        coefficient_kernel,
+        functools.partial(coefficient_kernel, chips, share),
         [whole] * 5,
         (own_sigma, other_sigma),
         [VMEM, VMEM],
         scratch=[room],
         limit=3,
     )
-    half = shape(chips, plane_count, *plane)
-    keep, pass_on = call(sort_kernel, [half] * 2, tuple(blocks), [VMEM] * chips)
+    keep, pass_on = call(
+        sort_kernel,
+        [shape(chips, plane_count, *plane)] * 2,
+        tuple(blocks), [VMEM] * chips,
+    )
     received = core_swap(pass_on)
     *slopes, voltage = call(
         functools.partial(forward_kernel, strength),
@@ -450,15 +477,25 @@
         [VMEM] * 5,
     )
     summed = kept + core_swap(given)
-    mine = summed[0]
+    first_rows = row_count * ((plane_count + 1) // 2)
+    cuts = ((0, first_rows), (first_rows, plane_count * row_count + SPARE))
+    cut = [summed[:, low:high] for low, high in cuts]
+    pieces = [piece[0] for piece in cut]
+    received = {}
     for step in range(1, chips):
-        mine = mine + chip_swap(summed[step], step)
-    predicted = mine[plane_count * row_count, :pattern_count]
-    gradient = mine[: plane_count * row_count].reshape(plane_count, *plane)
+        for number, piece in enumerate(cut):
+            received[number, step] = chip_swap(piece[step], step)
+    for number in range(len(pieces)):
+        for step in range(1, chips):
+            pieces[number] = pieces[number] + received[number, step]
+    predicted = pieces[-1][-SPARE, :pattern_count]
+    pieces[-1] = pieces[-1][:-SPARE]
     bit = 1
     while bit < groups:
-        gradient = gradient + swap(gradient, "pat", groups, bit)
+        for number in range(len(pieces)):
+            pieces[number] = pieces[number] + swap(pieces[number], "pat", groups, bit)
         bit *= 2
+    gradient = jnp.concatenate(pieces).reshape(plane_count, *plane)
     return gradient, predicted
 
 

time: 71.7 us -> 68.5 us (0.955)
  waiting for transfers between devices: 30.9 us -> 18.5 us
  starting transfers between devices: 20.3 us -> 29.1 us
    ppermute x18 -> x24, waiting for transfers between devices: 30.9 us -> 18.5 us  [swap(): return lax.ppermute(values, axis, [(i, i ^ bit) for i in range(size)])]
    ppermute x18 -> x24, starting transfers between devices: 20.3 us -> 29.1 us  [swap(): return lax.ppermute(values, axis, [(i, i ^ bit) for i in range(size)])]
    pallas_call x7 -> x8, Pallas kernels: 18.1 us -> 18.4 us  [call(): pl.pallas_call(body, out_shape=out_shape, in_specs=in_specs, out_specs=[V...]
  transfers between devices with their start and end apart: 18 -> 24, of which waited for: 9 -> 11; matrix products, arithmetic and copies ran while one was open for 1% -> 1% of each run, Pallas kernels for 18% -> 17%
where the time goes in v4:
time: 68.5 us; the launch traced here: 68.3 us
  starting transfers between devices  29.1 us (42%)
  waiting for transfers between devices  18.5 us (27%)
  Pallas kernels  18.4 us (27%)
  between operations  0.89 us (1%)
  other arithmetic  0.83 us (1%)
    ppermute x24, starting transfers between devices, swap(): return lax.ppermute(values, axis, [(i, i ^ bit) for i in range(size)])  29.1 us
    ppermute x24, waiting for transfers between devices, swap(): return lax.ppermute(values, axis, [(i, i ^ bit) for i in range(size)])  18.5 us
    pallas_call x8, Pallas kernels, call(): pl.pallas_call(body, out_shape=out_shape, in_specs=in_specs, out_specs=[V...  18.4 us
  transfers between devices with their start and end apart: 24, of which 11 were waited for; matrix products, arithmetic and copies ran while one was open for 1% of the time, Pallas kernels for 17%

profile of v4, /device:TPU:0, one launch (start us, length us, event | category | flops | bytes accessed | tf_op | source)
XLA Modules:
  0.0 68.3 jit_solution(4419061792393388863)
XLA Ops:
  0.6 1.3 %shard_map.77 = (f32[1,128,128]{2,1,0:T(8,128)S(1)}, f32[2,2,128,128]{3,2,1,0:T(8,128)S(1)}, f32[2,2,128,128]{3,2,1,0:T(8,128)S(1)}, f32[2,2,128,128]{3,2,1,0:T(8,128)S(1)}, f32[2,2,128,128]{3,2,1,0:T(8,128)S(1)}) custom-call(f32[2,128,128]{2,1,0:T(8,128)} %conductivity.1, f32[2,8,128,128]{3,2,1,0:T(8,128)} %forward.1), custom_call_target="tpu_custom_call" | custom-call | flops 2293760 | bytes 2293760 | tf_op jit(solution)/shard_map/pallas_call | solution.py:29
  2.0 4.0 %collective-permute-start.2 = (f32[1,128,128]{2,1,0:T(8,128)S(1)}, f32[1,128,128]{2,1,0:T(8,128)S(1)}, u32[]{:S(2)}, u32[]{:S(2)}) collective-permute-start(f32[1,128,128]{2,1,0:T(8,128)S(1)} %get-tuple-element.26), channel_id=1, source_target_pairs={{0,6},{1,7},{2,4},{3,5},{4,2},{5,3},{6,0},{7,1},{8,14},{9,15},{10,... | collective-permute-start | bytes 196616 | tf_op jit(solution)/shard_map/ppermute | solution.py:383
  6.6 1.4 %shard_map.81 = (f32[2,4,128,128]{3,2,1,0:T(8,128)S(1)}, f32[2,4,128,128]{3,2,1,0:T(8,128)S(1)}) custom-call(f32[2,8,128,128]{3,2,1,0:T(8,128)} %adjoint.1), custom_call_target="tpu_custom_call" | custom-call | flops 2097152 | bytes 2097152 | tf_op jit(solution)/shard_map/pallas_call | solution.py:29
  8.1 2.0 %collective-permute-start.5 = (f32[2,2,128,128]{3,2,1,0:T(8,128)S(1)}, f32[2,2,128,128]{3,2,1,0:T(8,128)S(1)}, u32[]{:S(2)}, u32[]{:S(2)}) collective-permute-start(f32[2,2,128,128]{3,2,1,0:T(8,128)S(1)} %get-tuple-element.33), channel_id=1, source_target_pairs={{0,2},{1,3},{2,0},{3,1},{4,6},{5,7},{6,4},{7,5},{8,10},{9,11},{10,... | collective-permute-start | bytes 786440 | tf_op jit(solution)/shard_map/ppermute | solution.py:383
  10.0 1.6 %collective-permute-start.6 = (f32[2,2,128,128]{3,2,1,0:T(8,128)S(1)}, f32[2,2,128,128]{3,2,1,0:T(8,128)S(1)}, u32[]{:S(2)}, u32[]{:S(2)}) collective-permute-start(f32[2,2,128,128]{3,2,1,0:T(8,128)S(1)} %get-tuple-element.34), channel_id=1, source_target_pairs={{0,4},{1,5},{2,6},{3,7},{4,0},{5,1},{6,2},{7,3},{8,12},{9,13},{10,... | collective-permute-start | bytes 786440 | tf_op jit(solution)/shard_map/ppermute | solution.py:383
  12.0 1.8 %collective-permute-start.3 = (f32[3,128,128]{2,1,0:T(8,128)S(1)}, f32[3,128,128]{2,1,0:T(8,128)S(1)}, u32[]{:S(2)}, u32[]{:S(2)}) collective-permute-start(f32[3,128,128]{2,1,0:T(8,128)S(1)} %pad_maximum_fusion), channel_id=1, source_target_pairs={{0,8},{8,0},{16,24},{24,16},{1,9},{9,1},{17,25},{25,17},{2,10},{10... | collective-permute-start | bytes 589832 | tf_op jit(solution)/shard_map/ppermute | solution.py:383
  13.8 4.7 %collective-permute-done.3 = f32[3,128,128]{2,1,0:T(8,128)S(1)} collective-permute-done((f32[3,128,128]{2,1,0:T(8,128)S(1)}, f32[3,128,128]{2,1,0:T(8,128)S(1)}, u32[]{:S(2)}, u32[]{:S(2)}) %collective-permute-start.3) | collective-permute-done | bytes 196640 | tf_op jit(solution)/shard_map/ppermute | solution.py:383
  18.6 5.5 %collective-permute-done.6.refs_2_ = f32[2,2,128,128]{3,2,1,0:T(8,128)S(1)} collective-permute-done((f32[2,2,128,128]{3,2,1,0:T(8,128)S(1)}, f32[2,2,128,128]{3,2,1,0:T(8,128)S(1)}, u32[]{:S(2)}, u32[]{:S(2)}) %collective-permute-start.6) | collective-permute-done | bytes 262176 | tf_op jit(solution)/shard_map/ppermute | solution.py:383
  24.4 1.2 %collective-permute-start.10 = (f32[2,2,128,128]{3,2,1,0:T(8,128)S(1)}, f32[2,2,128,128]{3,2,1,0:T(8,128)S(1)}, u32[]{:S(2)}, u32[]{:S(2)}) collective-permute-start(f32[2,2,128,128]{3,2,1,0:T(8,128)S(1)} %get-tuple-element.45), channel_id=1, source_target_pairs={{0,2},{1,3},{2,0},{3,1},{4,6},{5,7},{6,4},{7,5},{8,10},{9,11},{10,... | collective-permute-start | bytes 786440 | tf_op jit(solution)/shard_map/ppermute | solution.py:383
  26.5 1.4 %collective-permute-start.12 = (f32[2,2,128,128]{3,2,1,0:T(8,128)S(1)}, f32[2,2,128,128]{3,2,1,0:T(8,128)S(1)}, u32[]{:S(2)}, u32[]{:S(2)}) collective-permute-start(f32[2,2,128,128]{3,2,1,0:T(8,128)S(1)} %get-tuple-element.47), channel_id=1, source_target_pairs={{0,6},{1,7},{2,4},{3,5},{4,2},{5,3},{6,0},{7,1},{8,14},{9,15},{10,... | collective-permute-start | bytes 786440 | tf_op jit(solution)/shard_map/ppermute | solution.py:383
  27.9 3.7 %shard_map.78 = (f32[2304,128]{1,0:T(8,128)S(1)}, f32[2304,128]{1,0:T(8,128)S(1)}, f32[2304,128]{1,0:T(8,128)S(1)}, f32[2304,128]{1,0:T(8,128)S(1)}, f32[2304,128]{1,0:T(8,128)S(1)}) custom-call(f32[8,128,128]{2,1,0:T(8,128)S(1)} %constant_dynamic-update-slice_fusion.own, f32[8,128,128]{2,1,0:T(8,128)S(1)} %collective-permute-done.4.others), custom_call_target="tpu_custom_call" | custom-call | flops 6946816 | bytes 6946816 | tf_op jit(solution)/shard_map/pallas_call | solution.py:29
  31.7 5.9 %shard_map.80 = (f32[2304,128]{1,0:T(8,128)S(1)}, f32[2304,128]{1,0:T(8,128)S(1)}, f32[2304,128]{1,0:T(8,128)S(1)}, f32[8,128]{1,0:T(8,128)S(1)}) custom-call(s32[128]{0:T(128)S(1)} %copy-done.1, s32[4,8]{1,0:T(4,128)S(1)} %bitcast.32, f32[2304,128]{1,0:T(8,128)S(1)} %get-tuple-element.27.refs_0_, f32[2304,128]{1,0:T(8,128)S(1)} %get-tuple-element.28.refs_1_, ...), custom_call_target="tpu_custom_call" | custom-call | flops 10490496 | bytes 10490496 | tf_op jit(solution)/shard_map/pallas_call | solution.py:29
  38.1 1.6 %collective-permute-done.12.refs_12_ = f32[2,2,128,128]{3,2,1,0:T(8,128)S(1)} collective-permute-done((f32[2,2,128,128]{3,2,1,0:T(8,128)S(1)}, f32[2,2,128,128]{3,2,1,0:T(8,128)S(1)}, u32[]{:S(2)}, u32[]{:S(2)}) %collective-permute-start.12) | collective-permute-done | bytes 262176 | tf_op jit(solution)/shard_map/ppermute | solution.py:383
  39.7 5.2 %shard_map.83 = (f32[2304,128]{1,0:T(8,128)S(1)}, f32[4,264,128]{2,1,0:T(8,128)S(1)}) custom-call(s32[128]{0:T(128)S(1)} %copy-done.1, s32[4,8]{1,0:T(4,128)S(1)} %bitcast.33, f32[8]{0:T(128)S(1)} %copy-done.2, f32[2304,128]{1,0:T(8,128)S(1)} %get-tuple-element.27.refs_0_, f32[2304,128]{1,0:T(8,128)S(1)} %get-tuple-element.28.refs_1_, ...), custom_call_target="tpu_custom_call" | custom-call | flops 12210848 | bytes 12210848 | tf_op jit(solution)/shard_map/pallas_call | solution.py:29
  47.8 1.5 %collective-permute-start.16 = (f32[128,128]{1,0:T(8,128)S(1)}, f32[128,128]{1,0:T(8,128)S(1)}, u32[]{:S(2)}, u32[]{:S(2)}) collective-permute-start(f32[128,128]{1,0:T(8,128)S(1)} %get-tuple-element.51), channel_id=1, source_target_pairs={{0,6},{1,7},{2,4},{3,5},{4,2},{5,3},{6,0},{7,1},{8,14},{9,15},{10,... | collective-permute-start | bytes 196616 | tf_op jit(solution)/shard_map/ppermute | solution.py:383
  49.3 1.2 %collective-permute-start.15 = (f32[128,128]{1,0:T(8,128)S(1)}, f32[128,128]{1,0:T(8,128)S(1)}, u32[]{:S(2)}, u32[]{:S(2)}) collective-permute-start(f32[128,128]{1,0:T(8,128)S(1)} %get-tuple-element.52), channel_id=1, source_target_pairs={{0,4},{1,5},{2,6},{3,7},{4,0},{5,1},{6,2},{7,3},{8,12},{9,13},{10,... | collective-permute-start | bytes 196616 | tf_op jit(solution)/shard_map/ppermute | solution.py:383
  51.4 1.5 %collective-permute-start.21 = (f32[136,128]{1,0:T(8,128)S(1)}, f32[136,128]{1,0:T(8,128)S(1)}, u32[]{:S(2)}, u32[]{:S(2)}) collective-permute-start(f32[136,128]{1,0:T(8,128)S(1)} %get-tuple-element.54), channel_id=1, source_target_pairs={{0,6},{1,7},{2,4},{3,5},{4,2},{5,3},{6,0},{7,1},{8,14},{9,15},{10,... | collective-permute-start | bytes 208904 | tf_op jit(solution)/shard_map/ppermute | solution.py:383
  52.9 1.2 %collective-permute-start.20 = (f32[136,128]{1,0:T(8,128)S(1)}, f32[136,128]{1,0:T(8,128)S(1)}, u32[]{:S(2)}, u32[]{:S(2)}) collective-permute-start(f32[136,128]{1,0:T(8,128)S(1)} %get-tuple-element.55), channel_id=1, source_target_pairs={{0,4},{1,5},{2,6},{3,7},{4,0},{5,1},{6,2},{7,3},{8,12},{9,13},{10,... | collective-permute-start | bytes 208904 | tf_op jit(solution)/shard_map/ppermute | solution.py:383
  55.0 1.6 %collective-permute-start.17 = (f32[128,128]{1,0:T(8,128)S(1)}, f32[128,128]{1,0:T(8,128)S(1)}, u32[]{:S(2)}, u32[]{:S(2)}) collective-permute-start(f32[128,128]{1,0:T(8,128)S(1)} %fusion.5), channel_id=1, source_target_pairs={{0,8},{8,0},{16,24},{24,16},{1,9},{9,1},{17,25},{25,17},{2,10},{10... | collective-permute-start | bytes 196616 | tf_op jit(solution)/shard_map/ppermute | solution.py:383
  57.4 1.6 %collective-permute-start.22 = (f32[128,128]{1,0:T(8,128)S(1)}, f32[128,128]{1,0:T(8,128)S(1)}, u32[]{:S(2)}, u32[]{:S(2)}) collective-permute-start(f32[128,128]{1,0:T(8,128)S(1)} %slice.58), channel_id=1, source_target_pairs={{0,8},{8,0},{16,24},{24,16},{1,9},{9,1},{17,25},{25,17},{2,10},{10... | collective-permute-start | bytes 196616 | tf_op jit(solution)/shard_map/ppermute | solution.py:383
  59.7 2.7 %collective-permute-start.18 = (f32[128,128]{1,0:T(8,128)S(1)}, f32[128,128]{1,0:T(8,128)S(1)}, u32[]{:S(2)}, u32[]{:S(2)}) collective-permute-start(f32[128,128]{1,0:T(8,128)S(1)} %add.37), channel_id=1, source_target_pairs={{0,16},{8,24},{16,0},{24,8},{1,17},{9,25},{17,1},{25,9},{2,18},{10... | collective-permute-start | bytes 196616 | tf_op jit(solution)/shard_map/ppermute | solution.py:383
  62.4 2.0 %collective-permute-start.23 = (f32[128,128]{1,0:T(8,128)S(1)}, f32[128,128]{1,0:T(8,128)S(1)}, u32[]{:S(2)}, u32[]{:S(2)}) collective-permute-start(f32[128,128]{1,0:T(8,128)S(1)} %slice_add_fusion), channel_id=1, source_target_pairs={{0,16},{8,24},{16,0},{24,8},{1,17},{9,25},{17,1},{25,9},{2,18},{10... | collective-permute-start | bytes 196616 | tf_op jit(solution)/shard_map/ppermute | solution.py:383
  64.9 1.4 %collective-permute-done.18 = f32[128,128]{1,0:T(8,128)S(1)} collective-permute-done((f32[128,128]{1,0:T(8,128)S(1)}, f32[128,128]{1,0:T(8,128)S(1)}, u32[]{:S(2)}, u32[]{:S(2)}) %collective-permute-start.18) | collective-permute-done | bytes 65568 | tf_op jit(solution)/shard_map/ppermute | solution.py:383
  66.3 1.3 %collective-permute-done.23 = f32[128,128]{1,0:T(8,128)S(1)} collective-permute-done((f32[128,128]{1,0:T(8,128)S(1)}, f32[128,128]{1,0:T(8,128)S(1)}, u32[]{:S(2)}, u32[]{:S(2)}) %collective-permute-start.23) | collective-permute-done | bytes 65568 | tf_op jit(solution)/shard_map/ppermute | solution.py:383
  (58 shorter events, 10.2 us)
Async XLA Ops:
  2.0 8.1 %collective-permute-start.2 = (f32[1,128,128]{2,1,0:T(8,128)S(1)}, f32[1,128,128]{2,1,0:T(8,128)S(1)}, u32[]{:S(2)}, u32[]{:S(2)}) collective-permute-start(f32[1,128,128]{2,1,0:T(8,128)S(1)} %get-tuple-element.26), channel_id=1, source_target_pairs={{0,6},{1,7},{2,4},{3,5},{4,2},{5,3},{6,0},{7,1},{8,14},{9,15},{10,... | collective-permute-start | bytes 196616 | tf_op jit(solution)/shard_map/ppermute | solution.py:383
  6.0 5.7 %collective-permute-start.1 = (f32[1,128,128]{2,1,0:T(8,128)S(1)}, f32[1,128,128]{2,1,0:T(8,128)S(1)}, u32[]{:S(2)}, u32[]{:S(2)}) collective-permute-start(f32[1,128,128]{2,1,0:T(8,128)S(1)} %get-tuple-element.26), channel_id=1, source_target_pairs={{0,4},{1,5},{2,6},{3,7},{4,0},{5,1},{6,2},{7,3},{8,12},{9,13},{10,... | collective-permute-start | bytes 196616 | tf_op jit(solution)/shard_map/ppermute | solution.py:383
  6.5 5.5 %collective-permute-start = (f32[1,128,128]{2,1,0:T(8,128)S(1)}, f32[1,128,128]{2,1,0:T(8,128)S(1)}, u32[]{:S(2)}, u32[]{:S(2)}) collective-permute-start(f32[1,128,128]{2,1,0:T(8,128)S(1)} %get-tuple-element.26), channel_id=1, source_target_pairs={{0,2},{1,3},{2,0},{3,1},{4,6},{5,7},{6,4},{7,5},{8,10},{9,11},{10,... | collective-permute-start | bytes 196616 | tf_op jit(solution)/shard_map/ppermute | solution.py:383
  8.0 16.3 %collective-permute-start.9 = (f32[2,4,128,128]{3,2,1,0:T(8,128)S(1)}, f32[2,4,128,128]{3,2,1,0:T(8,128)S(1)}, u32[]{:S(2)}, u32[]{:S(2)}) collective-permute-start(f32[2,4,128,128]{3,2,1,0:T(8,128)S(1)} %get-tuple-element.43), channel_id=1, source_target_pairs={{0,1},{1,0},{2,3},{3,2},{4,5},{5,4},{6,7},{7,6},{8,9},{9,8},{10,11... | collective-permute-start | bytes 1572872 | tf_op jit(solution)/shard_map/ppermute | solution.py:383
  8.1 10.5 %collective-permute-start.5 = (f32[2,2,128,128]{3,2,1,0:T(8,128)S(1)}, f32[2,2,128,128]{3,2,1,0:T(8,128)S(1)}, u32[]{:S(2)}, u32[]{:S(2)}) collective-permute-start(f32[2,2,128,128]{3,2,1,0:T(8,128)S(1)} %get-tuple-element.33), channel_id=1, source_target_pairs={{0,2},{1,3},{2,0},{3,1},{4,6},{5,7},{6,4},{7,5},{8,10},{9,11},{10,... | collective-permute-start | bytes 786440 | tf_op jit(solution)/shard_map/ppermute | solution.py:383
  10.0 14.0 %collective-permute-start.6 = (f32[2,2,128,128]{3,2,1,0:T(8,128)S(1)}, f32[2,2,128,128]{3,2,1,0:T(8,128)S(1)}, u32[]{:S(2)}, u32[]{:S(2)}) collective-permute-start(f32[2,2,128,128]{3,2,1,0:T(8,128)S(1)} %get-tuple-element.34), channel_id=1, source_target_pairs={{0,4},{1,5},{2,6},{3,7},{4,0},{5,1},{6,2},{7,3},{8,12},{9,13},{10,... | collective-permute-start | bytes 786440 | tf_op jit(solution)/shard_map/ppermute | solution.py:383
  11.6 12.5 %collective-permute-start.7 = (f32[2,2,128,128]{3,2,1,0:T(8,128)S(1)}, f32[2,2,128,128]{3,2,1,0:T(8,128)S(1)}, u32[]{:S(2)}, u32[]{:S(2)}) collective-permute-start(f32[2,2,128,128]{3,2,1,0:T(8,128)S(1)} %get-tuple-element.35), channel_id=1, source_target_pairs={{0,6},{1,7},{2,4},{3,5},{4,2},{5,3},{6,0},{7,1},{8,14},{9,15},{10,... | collective-permute-start | bytes 786440 | tf_op jit(solution)/shard_map/ppermute | solution.py:383
  12.0 6.5 %collective-permute-start.3 = (f32[3,128,128]{2,1,0:T(8,128)S(1)}, f32[3,128,128]{2,1,0:T(8,128)S(1)}, u32[]{:S(2)}, u32[]{:S(2)}) collective-permute-start(f32[3,128,128]{2,1,0:T(8,128)S(1)} %pad_maximum_fusion), channel_id=1, source_target_pairs={{0,8},{8,0},{16,24},{24,16},{1,9},{9,1},{17,25},{25,17},{2,10},{10... | collective-permute-start | bytes 589832 | tf_op jit(solution)/shard_map/ppermute | solution.py:383
  18.5 9.5 %collective-permute-start.4 = (f32[8,128,128]{2,1,0:T(8,128)S(1)}, f32[8,128,128]{2,1,0:T(8,128)S(1)}, u32[]{:S(2)}, u32[]{:S(2)}) collective-permute-start(f32[8,128,128]{2,1,0:T(8,128)S(1)} %constant_dynamic-update-slice_fusion.own), channel_id=1, source_target_pairs={{0,1},{1,0},{2,3},{3,2},{4,5},{5,4},{6,7},{7,6},{8,9},{9,8},{10,11... | collective-permute-start | bytes 1572872 | tf_op jit(solution)/shard_map/ppermute | solution.py:383
  24.2 7.4 %collective-permute-start.8 = (f32[4,2,128,128]{3,2,1,0:T(8,128)S(1)}, f32[4,2,128,128]{3,2,1,0:T(8,128)S(1)}, u32[]{:S(2)}, u32[]{:S(2)}) collective-permute-start(f32[4,2,128,128]{3,2,1,0:T(8,128)S(1)} %get-tuple-element.37), channel_id=1, source_target_pairs={{0,1},{1,0},{2,3},{3,2},{4,5},{5,4},{6,7},{7,6},{8,9},{9,8},{10,11... | collective-permute-start | bytes 1572872 | tf_op jit(solution)/shard_map/ppermute | solution.py:383
  24.4 13.2 %collective-permute-start.10 = (f32[2,2,128,128]{3,2,1,0:T(8,128)S(1)}, f32[2,2,128,128]{3,2,1,0:T(8,128)S(1)}, u32[]{:S(2)}, u32[]{:S(2)}) collective-permute-start(f32[2,2,128,128]{3,2,1,0:T(8,128)S(1)} %get-tuple-element.45), channel_id=1, source_target_pairs={{0,2},{1,3},{2,0},{3,1},{4,6},{5,7},{6,4},{7,5},{8,10},{9,11},{10,... | collective-permute-start | bytes 786440 | tf_op jit(solution)/shard_map/ppermute | solution.py:383
  25.6 12.5 %collective-permute-start.11 = (f32[2,2,128,128]{3,2,1,0:T(8,128)S(1)}, f32[2,2,128,128]{3,2,1,0:T(8,128)S(1)}, u32[]{:S(2)}, u32[]{:S(2)}) collective-permute-start(f32[2,2,128,128]{3,2,1,0:T(8,128)S(1)} %get-tuple-element.46), channel_id=1, source_target_pairs={{0,4},{1,5},{2,6},{3,7},{4,0},{5,1},{6,2},{7,3},{8,12},{9,13},{10,... | collective-permute-start | bytes 786440 | tf_op jit(solution)/shard_map/ppermute | solution.py:383
  26.5 13.2 %collective-permute-start.12 = (f32[2,2,128,128]{3,2,1,0:T(8,128)S(1)}, f32[2,2,128,128]{3,2,1,0:T(8,128)S(1)}, u32[]{:S(2)}, u32[]{:S(2)}) collective-permute-start(f32[2,2,128,128]{3,2,1,0:T(8,128)S(1)} %get-tuple-element.47), channel_id=1, source_target_pairs={{0,6},{1,7},{2,4},{3,5},{4,2},{5,3},{6,0},{7,1},{8,14},{9,15},{10,... | collective-permute-start | bytes 786440 | tf_op jit(solution)/shard_map/ppermute | solution.py:383
  44.9 2.0 %collective-permute-start.13 = (f32[4,264,128]{2,1,0:T(8,128)S(1)}, f32[4,264,128]{2,1,0:T(8,128)S(1)}, u32[]{:S(2)}, u32[]{:S(2)}) collective-permute-start(f32[4,264,128]{2,1,0:T(8,128)S(1)} %get-tuple-element.49), channel_id=1, source_target_pairs={{0,1},{1,0},{2,3},{3,2},{4,5},{5,4},{6,7},{7,6},{8,9},{9,8},{10,11... | collective-permute-start | bytes 1622024 | tf_op jit(solution)/shard_map/ppermute | solution.py:383
  47.0 5.9 %collective-permute-start.14 = (f32[128,128]{1,0:T(8,128)S(1)}, f32[128,128]{1,0:T(8,128)S(1)}, u32[]{:S(2)}, u32[]{:S(2)}) collective-permute-start(f32[128,128]{1,0:T(8,128)S(1)} %get-tuple-element.50), channel_id=1, source_target_pairs={{0,2},{1,3},{2,0},{3,1},{4,6},{5,7},{6,4},{7,5},{8,10},{9,11},{10,... | collective-permute-start | bytes 196616 | tf_op jit(solution)/shard_map/ppermute | solution.py:383
  47.8 6.3 %collective-permute-start.16 = (f32[128,128]{1,0:T(8,128)S(1)}, f32[128,128]{1,0:T(8,128)S(1)}, u32[]{:S(2)}, u32[]{:S(2)}) collective-permute-start(f32[128,128]{1,0:T(8,128)S(1)} %get-tuple-element.51), channel_id=1, source_target_pairs={{0,6},{1,7},{2,4},{3,5},{4,2},{5,3},{6,0},{7,1},{8,14},{9,15},{10,... | collective-permute-start | bytes 196616 | tf_op jit(solution)/shard_map/ppermute | solution.py:383
  49.3 5.7 %collective-permute-start.15 = (f32[128,128]{1,0:T(8,128)S(1)}, f32[128,128]{1,0:T(8,128)S(1)}, u32[]{:S(2)}, u32[]{:S(2)}) collective-permute-start(f32[128,128]{1,0:T(8,128)S(1)} %get-tuple-element.52), channel_id=1, source_target_pairs={{0,4},{1,5},{2,6},{3,7},{4,0},{5,1},{6,2},{7,3},{8,12},{9,13},{10,... | collective-permute-start | bytes 196616 | tf_op jit(solution)/shard_map/ppermute | solution.py:383
  50.5 6.1 %collective-permute-start.19 = (f32[136,128]{1,0:T(8,128)S(1)}, f32[136,128]{1,0:T(8,128)S(1)}, u32[]{:S(2)}, u32[]{:S(2)}) collective-permute-start(f32[136,128]{1,0:T(8,128)S(1)} %get-tuple-element.53), channel_id=1, source_target_pairs={{0,2},{1,3},{2,0},{3,1},{4,6},{5,7},{6,4},{7,5},{8,10},{9,11},{10,... | collective-permute-start | bytes 208904 | tf_op jit(solution)/shard_map/ppermute | solution.py:383
  51.4 5.3 %collective-permute-start.21 = (f32[136,128]{1,0:T(8,128)S(1)}, f32[136,128]{1,0:T(8,128)S(1)}, u32[]{:S(2)}, u32[]{:S(2)}) collective-permute-start(f32[136,128]{1,0:T(8,128)S(1)} %get-tuple-element.54), channel_id=1, source_target_pairs={{0,6},{1,7},{2,4},{3,5},{4,2},{5,3},{6,0},{7,1},{8,14},{9,15},{10,... | collective-permute-start | bytes 208904 | tf_op jit(solution)/shard_map/ppermute | solution.py:383
  52.9 4.5 %collective-permute-start.20 = (f32[136,128]{1,0:T(8,128)S(1)}, f32[136,128]{1,0:T(8,128)S(1)}, u32[]{:S(2)}, u32[]{:S(2)}) collective-permute-start(f32[136,128]{1,0:T(8,128)S(1)} %get-tuple-element.55), channel_id=1, source_target_pairs={{0,4},{1,5},{2,6},{3,7},{4,0},{5,1},{6,2},{7,3},{8,12},{9,13},{10,... | collective-permute-start | bytes 208904 | tf_op jit(solution)/shard_map/ppermute | solution.py:383
  55.0 4.6 %collective-permute-start.17 = (f32[128,128]{1,0:T(8,128)S(1)}, f32[128,128]{1,0:T(8,128)S(1)}, u32[]{:S(2)}, u32[]{:S(2)}) collective-permute-start(f32[128,128]{1,0:T(8,128)S(1)} %fusion.5), channel_id=1, source_target_pairs={{0,8},{8,0},{16,24},{24,16},{1,9},{9,1},{17,25},{25,17},{2,10},{10... | collective-permute-start | bytes 196616 | tf_op jit(solution)/shard_map/ppermute | solution.py:383
  57.4 5.0 %collective-permute-start.22 = (f32[128,128]{1,0:T(8,128)S(1)}, f32[128,128]{1,0:T(8,128)S(1)}, u32[]{:S(2)}, u32[]{:S(2)}) collective-permute-start(f32[128,128]{1,0:T(8,128)S(1)} %slice.58), channel_id=1, source_target_pairs={{0,8},{8,0},{16,24},{24,16},{1,9},{9,1},{17,25},{25,17},{2,10},{10... | collective-permute-start | bytes 196616 | tf_op jit(solution)/shard_map/ppermute | solution.py:383
  59.7 6.6 %collective-permute-start.18 = (f32[128,128]{1,0:T(8,128)S(1)}, f32[128,128]{1,0:T(8,128)S(1)}, u32[]{:S(2)}, u32[]{:S(2)}) collective-permute-start(f32[128,128]{1,0:T(8,128)S(1)} %add.37), channel_id=1, source_target_pairs={{0,16},{8,24},{16,0},{24,8},{1,17},{9,25},{17,1},{25,9},{2,18},{10... | collective-permute-start | bytes 196616 | tf_op jit(solution)/shard_map/ppermute | solution.py:383
  62.4 5.2 %collective-permute-start.23 = (f32[128,128]{1,0:T(8,128)S(1)}, f32[128,128]{1,0:T(8,128)S(1)}, u32[]{:S(2)}, u32[]{:S(2)}) collective-permute-start(f32[128,128]{1,0:T(8,128)S(1)} %slice_add_fusion), channel_id=1, source_target_pairs={{0,16},{8,24},{16,0},{24,8},{1,17},{9,25},{17,1},{25,9},{2,18},{10... | collective-permute-start | bytes 196616 | tf_op jit(solution)/shard_map/ppermute | solution.py:383
  (4 other events, 32.4 us)

commit v5 on v4

--- a/solution.py
+++ b/solution.py
@@ -413,11 +413,12 @@
         [HBM, HBM],
         scratch=[pltpu.SemaphoreType.DMA((1 + chips,))],
     )
-    order = list(reversed(range(1, chips)))
-    fetched = {step: chip_swap(fetched, step) for step in order}
-    fetched = [fetched[step] for step in range(1, chips)]
-    blocks = {step: chip_swap(sends[step], step) for step in order}
-    blocks = [sends[0]] + [blocks[step] for step in range(1, chips)]
+    sigma_got, blocks, adjoint_blocks = {}, {0: sends[0]}, {}
+    for step in range(1, chips):
+        sigma_got[step] = chip_swap(fetched, step)
+        blocks[step] = chip_swap(sends[step], step)
+    fetched = [sigma_got[step] for step in range(1, chips)]
+    blocks = [blocks[step] for step in range(chips)]
     own, give = call(
         stage_adjoint_kernel,
         [shape(plane_count, chips, *plane)] * 2,
@@ -429,8 +430,8 @@
     packed = call(
         pack_kernel, [shape(CORES, plane_count, *plane)] * chips, (own, got), [VMEM, VMEM]
     )
-    adjoint_blocks = {0: packed[0]}
-    for step in order:
+    adjoint_blocks[0] = packed[0]
+    for step in range(1, chips):
         adjoint_blocks[step] = chip_swap(packed[step], step)
     adjoint_blocks = [adjoint_blocks[step] for step in range(chips)]
     others = [swap(jnp.concatenate(fetched), "pat", groups, 1)] if share == 2 else []
@@ -445,9 +446,7 @@
         limit=3,
     )
     keep, pass_on = call(
-        sort_kernel,
-        [shape(chips, plane_count, *plane)] * 2,
-        tuple(blocks), [VMEM] * chips,
+        sort_kernel, [shape(chips, plane_count, *plane)] * 2, tuple(blocks), [VMEM] * chips
     )
     received = core_swap(pass_on)
     *slopes, voltage = call(

time: 68.5 us -> 68.5 us (level)
  no operation moved by 1% of the time
where the time goes in v5:
time: 68.5 us; the launch traced here: 68.3 us
  starting transfers between devices  29.1 us (42%)
  waiting for transfers between devices  18.5 us (27%)
  Pallas kernels  18.4 us (27%)
  between operations  0.89 us (1%)
  other arithmetic  0.83 us (1%)
    ppermute x24, starting transfers between devices, swap(): return lax.ppermute(values, axis, [(i, i ^ bit) for i in range(size)])  29.1 us
    ppermute x24, waiting for transfers between devices, swap(): return lax.ppermute(values, axis, [(i, i ^ bit) for i in range(size)])  18.5 us
    pallas_call x8, Pallas kernels, call(): pl.pallas_call(body, out_shape=out_shape, in_specs=in_specs, out_specs=[V...  18.4 us
  transfers between devices with their start and end apart: 24, of which 11 were waited for; matrix products, arithmetic and copies ran while one was open for 1% of the time, Pallas kernels for 17%

profile of v5, /device:TPU:0, one launch (start us, length us, event | category | flops | bytes accessed | tf_op | source)
XLA Modules:
  0.0 68.3 jit_solution(4419061792393388863)
XLA Ops:
  0.6 1.3 %shard_map.77 = (f32[1,128,128]{2,1,0:T(8,128)S(1)}, f32[2,2,128,128]{3,2,1,0:T(8,128)S(1)}, f32[2,2,128,128]{3,2,1,0:T(8,128)S(1)}, f32[2,2,128,128]{3,2,1,0:T(8,128)S(1)}, f32[2,2,128,128]{3,2,1,0:T(8,128)S(1)}) custom-call(f32[2,128,128]{2,1,0:T(8,128)} %conductivity.1, f32[2,8,128,128]{3,2,1,0:T(8,128)} %forward.1), custom_call_target="tpu_custom_call" | custom-call | flops 2293760 | bytes 2293760 | tf_op jit(solution)/shard_map/pallas_call | solution.py:29
  2.0 4.0 %collective-permute-start.2 = (f32[1,128,128]{2,1,0:T(8,128)S(1)}, f32[1,128,128]{2,1,0:T(8,128)S(1)}, u32[]{:S(2)}, u32[]{:S(2)}) collective-permute-start(f32[1,128,128]{2,1,0:T(8,128)S(1)} %get-tuple-element.26), channel_id=1, source_target_pairs={{0,6},{1,7},{2,4},{3,5},{4,2},{5,3},{6,0},{7,1},{8,14},{9,15},{10,... | collective-permute-start | bytes 196616 | tf_op jit(solution)/shard_map/ppermute | solution.py:383
  6.6 1.4 %shard_map.81 = (f32[2,4,128,128]{3,2,1,0:T(8,128)S(1)}, f32[2,4,128,128]{3,2,1,0:T(8,128)S(1)}) custom-call(f32[2,8,128,128]{3,2,1,0:T(8,128)} %adjoint.1), custom_call_target="tpu_custom_call" | custom-call | flops 2097152 | bytes 2097152 | tf_op jit(solution)/shard_map/pallas_call | solution.py:29
  8.1 2.0 %collective-permute-start.5 = (f32[2,2,128,128]{3,2,1,0:T(8,128)S(1)}, f32[2,2,128,128]{3,2,1,0:T(8,128)S(1)}, u32[]{:S(2)}, u32[]{:S(2)}) collective-permute-start(f32[2,2,128,128]{3,2,1,0:T(8,128)S(1)} %get-tuple-element.33), channel_id=1, source_target_pairs={{0,2},{1,3},{2,0},{3,1},{4,6},{5,7},{6,4},{7,5},{8,10},{9,11},{10,... | collective-permute-start | bytes 786440 | tf_op jit(solution)/shard_map/ppermute | solution.py:383
  10.0 1.6 %collective-permute-start.6 = (f32[2,2,128,128]{3,2,1,0:T(8,128)S(1)}, f32[2,2,128,128]{3,2,1,0:T(8,128)S(1)}, u32[]{:S(2)}, u32[]{:S(2)}) collective-permute-start(f32[2,2,128,128]{3,2,1,0:T(8,128)S(1)} %get-tuple-element.34), channel_id=1, source_target_pairs={{0,4},{1,5},{2,6},{3,7},{4,0},{5,1},{6,2},{7,3},{8,12},{9,13},{10,... | collective-permute-start | bytes 786440 | tf_op jit(solution)/shard_map/ppermute | solution.py:383
  12.0 1.8 %collective-permute-start.3 = (f32[3,128,128]{2,1,0:T(8,128)S(1)}, f32[3,128,128]{2,1,0:T(8,128)S(1)}, u32[]{:S(2)}, u32[]{:S(2)}) collective-permute-start(f32[3,128,128]{2,1,0:T(8,128)S(1)} %pad_maximum_fusion), channel_id=1, source_target_pairs={{0,8},{8,0},{16,24},{24,16},{1,9},{9,1},{17,25},{25,17},{2,10},{10... | collective-permute-start | bytes 589832 | tf_op jit(solution)/shard_map/ppermute | solution.py:383
  13.8 4.7 %collective-permute-done.3 = f32[3,128,128]{2,1,0:T(8,128)S(1)} collective-permute-done((f32[3,128,128]{2,1,0:T(8,128)S(1)}, f32[3,128,128]{2,1,0:T(8,128)S(1)}, u32[]{:S(2)}, u32[]{:S(2)}) %collective-permute-start.3) | collective-permute-done | bytes 196640 | tf_op jit(solution)/shard_map/ppermute | solution.py:383
  18.6 5.5 %collective-permute-done.6.refs_2_ = f32[2,2,128,128]{3,2,1,0:T(8,128)S(1)} collective-permute-done((f32[2,2,128,128]{3,2,1,0:T(8,128)S(1)}, f32[2,2,128,128]{3,2,1,0:T(8,128)S(1)}, u32[]{:S(2)}, u32[]{:S(2)}) %collective-permute-start.6) | collective-permute-done | bytes 262176 | tf_op jit(solution)/shard_map/ppermute | solution.py:383
  24.4 1.2 %collective-permute-start.10 = (f32[2,2,128,128]{3,2,1,0:T(8,128)S(1)}, f32[2,2,128,128]{3,2,1,0:T(8,128)S(1)}, u32[]{:S(2)}, u32[]{:S(2)}) collective-permute-start(f32[2,2,128,128]{3,2,1,0:T(8,128)S(1)} %get-tuple-element.45), channel_id=1, source_target_pairs={{0,2},{1,3},{2,0},{3,1},{4,6},{5,7},{6,4},{7,5},{8,10},{9,11},{10,... | collective-permute-start | bytes 786440 | tf_op jit(solution)/shard_map/ppermute | solution.py:383
  26.5 1.4 %collective-permute-start.12 = (f32[2,2,128,128]{3,2,1,0:T(8,128)S(1)}, f32[2,2,128,128]{3,2,1,0:T(8,128)S(1)}, u32[]{:S(2)}, u32[]{:S(2)}) collective-permute-start(f32[2,2,128,128]{3,2,1,0:T(8,128)S(1)} %get-tuple-element.47), channel_id=1, source_target_pairs={{0,6},{1,7},{2,4},{3,5},{4,2},{5,3},{6,0},{7,1},{8,14},{9,15},{10,... | collective-permute-start | bytes 786440 | tf_op jit(solution)/shard_map/ppermute | solution.py:383
  27.9 3.7 %shard_map.78 = (f32[2304,128]{1,0:T(8,128)S(1)}, f32[2304,128]{1,0:T(8,128)S(1)}, f32[2304,128]{1,0:T(8,128)S(1)}, f32[2304,128]{1,0:T(8,128)S(1)}, f32[2304,128]{1,0:T(8,128)S(1)}) custom-call(f32[8,128,128]{2,1,0:T(8,128)S(1)} %constant_dynamic-update-slice_fusion.own, f32[8,128,128]{2,1,0:T(8,128)S(1)} %collective-permute-done.4.others), custom_call_target="tpu_custom_call" | custom-call | flops 6946816 | bytes 6946816 | tf_op jit(solution)/shard_map/pallas_call | solution.py:29
  31.7 5.9 %shard_map.80 = (f32[2304,128]{1,0:T(8,128)S(1)}, f32[2304,128]{1,0:T(8,128)S(1)}, f32[2304,128]{1,0:T(8,128)S(1)}, f32[8,128]{1,0:T(8,128)S(1)}) custom-call(s32[128]{0:T(128)S(1)} %copy-done.1, s32[4,8]{1,0:T(4,128)S(1)} %bitcast.32, f32[2304,128]{1,0:T(8,128)S(1)} %get-tuple-element.27.refs_0_, f32[2304,128]{1,0:T(8,128)S(1)} %get-tuple-element.28.refs_1_, ...), custom_call_target="tpu_custom_call" | custom-call | flops 10490496 | bytes 10490496 | tf_op jit(solution)/shard_map/pallas_call | solution.py:29
  38.1 1.6 %collective-permute-done.12.refs_12_ = f32[2,2,128,128]{3,2,1,0:T(8,128)S(1)} collective-permute-done((f32[2,2,128,128]{3,2,1,0:T(8,128)S(1)}, f32[2,2,128,128]{3,2,1,0:T(8,128)S(1)}, u32[]{:S(2)}, u32[]{:S(2)}) %collective-permute-start.12) | collective-permute-done | bytes 262176 | tf_op jit(solution)/shard_map/ppermute | solution.py:383
  39.7 5.2 %shard_map.83 = (f32[2304,128]{1,0:T(8,128)S(1)}, f32[4,264,128]{2,1,0:T(8,128)S(1)}) custom-call(s32[128]{0:T(128)S(1)} %copy-done.1, s32[4,8]{1,0:T(4,128)S(1)} %bitcast.33, f32[8]{0:T(128)S(1)} %copy-done.2, f32[2304,128]{1,0:T(8,128)S(1)} %get-tuple-element.27.refs_0_, f32[2304,128]{1,0:T(8,128)S(1)} %get-tuple-element.28.refs_1_, ...), custom_call_target="tpu_custom_call" | custom-call | flops 12210848 | bytes 12210848 | tf_op jit(solution)/shard_map/pallas_call | solution.py:29
  47.8 1.5 %collective-permute-start.16 = (f32[128,128]{1,0:T(8,128)S(1)}, f32[128,128]{1,0:T(8,128)S(1)}, u32[]{:S(2)}, u32[]{:S(2)}) collective-permute-start(f32[128,128]{1,0:T(8,128)S(1)} %get-tuple-element.51), channel_id=1, source_target_pairs={{0,6},{1,7},{2,4},{3,5},{4,2},{5,3},{6,0},{7,1},{8,14},{9,15},{10,... | collective-permute-start | bytes 196616 | tf_op jit(solution)/shard_map/ppermute | solution.py:383
  49.3 1.2 %collective-permute-start.15 = (f32[128,128]{1,0:T(8,128)S(1)}, f32[128,128]{1,0:T(8,128)S(1)}, u32[]{:S(2)}, u32[]{:S(2)}) collective-permute-start(f32[128,128]{1,0:T(8,128)S(1)} %get-tuple-element.52), channel_id=1, source_target_pairs={{0,4},{1,5},{2,6},{3,7},{4,0},{5,1},{6,2},{7,3},{8,12},{9,13},{10,... | collective-permute-start | bytes 196616 | tf_op jit(solution)/shard_map/ppermute | solution.py:383
  51.4 1.5 %collective-permute-start.21 = (f32[136,128]{1,0:T(8,128)S(1)}, f32[136,128]{1,0:T(8,128)S(1)}, u32[]{:S(2)}, u32[]{:S(2)}) collective-permute-start(f32[136,128]{1,0:T(8,128)S(1)} %get-tuple-element.54), channel_id=1, source_target_pairs={{0,6},{1,7},{2,4},{3,5},{4,2},{5,3},{6,0},{7,1},{8,14},{9,15},{10,... | collective-permute-start | bytes 208904 | tf_op jit(solution)/shard_map/ppermute | solution.py:383
  52.9 1.2 %collective-permute-start.20 = (f32[136,128]{1,0:T(8,128)S(1)}, f32[136,128]{1,0:T(8,128)S(1)}, u32[]{:S(2)}, u32[]{:S(2)}) collective-permute-start(f32[136,128]{1,0:T(8,128)S(1)} %get-tuple-element.55), channel_id=1, source_target_pairs={{0,4},{1,5},{2,6},{3,7},{4,0},{5,1},{6,2},{7,3},{8,12},{9,13},{10,... | collective-permute-start | bytes 208904 | tf_op jit(solution)/shard_map/ppermute | solution.py:383
  55.0 1.6 %collective-permute-start.17 = (f32[128,128]{1,0:T(8,128)S(1)}, f32[128,128]{1,0:T(8,128)S(1)}, u32[]{:S(2)}, u32[]{:S(2)}) collective-permute-start(f32[128,128]{1,0:T(8,128)S(1)} %fusion.5), channel_id=1, source_target_pairs={{0,8},{8,0},{16,24},{24,16},{1,9},{9,1},{17,25},{25,17},{2,10},{10... | collective-permute-start | bytes 196616 | tf_op jit(solution)/shard_map/ppermute | solution.py:383
  57.4 1.6 %collective-permute-start.22 = (f32[128,128]{1,0:T(8,128)S(1)}, f32[128,128]{1,0:T(8,128)S(1)}, u32[]{:S(2)}, u32[]{:S(2)}) collective-permute-start(f32[128,128]{1,0:T(8,128)S(1)} %slice.58), channel_id=1, source_target_pairs={{0,8},{8,0},{16,24},{24,16},{1,9},{9,1},{17,25},{25,17},{2,10},{10... | collective-permute-start | bytes 196616 | tf_op jit(solution)/shard_map/ppermute | solution.py:383
  59.7 2.7 %collective-permute-start.18 = (f32[128,128]{1,0:T(8,128)S(1)}, f32[128,128]{1,0:T(8,128)S(1)}, u32[]{:S(2)}, u32[]{:S(2)}) collective-permute-start(f32[128,128]{1,0:T(8,128)S(1)} %add.37), channel_id=1, source_target_pairs={{0,16},{8,24},{16,0},{24,8},{1,17},{9,25},{17,1},{25,9},{2,18},{10... | collective-permute-start | bytes 196616 | tf_op jit(solution)/shard_map/ppermute | solution.py:383
  62.4 2.0 %collective-permute-start.23 = (f32[128,128]{1,0:T(8,128)S(1)}, f32[128,128]{1,0:T(8,128)S(1)}, u32[]{:S(2)}, u32[]{:S(2)}) collective-permute-start(f32[128,128]{1,0:T(8,128)S(1)} %slice_add_fusion), channel_id=1, source_target_pairs={{0,16},{8,24},{16,0},{24,8},{1,17},{9,25},{17,1},{25,9},{2,18},{10... | collective-permute-start | bytes 196616 | tf_op jit(solution)/shard_map/ppermute | solution.py:383
  64.9 1.4 %collective-permute-done.18 = f32[128,128]{1,0:T(8,128)S(1)} collective-permute-done((f32[128,128]{1,0:T(8,128)S(1)}, f32[128,128]{1,0:T(8,128)S(1)}, u32[]{:S(2)}, u32[]{:S(2)}) %collective-permute-start.18) | collective-permute-done | bytes 65568 | tf_op jit(solution)/shard_map/ppermute | solution.py:383
  66.3 1.3 %collective-permute-done.23 = f32[128,128]{1,0:T(8,128)S(1)} collective-permute-done((f32[128,128]{1,0:T(8,128)S(1)}, f32[128,128]{1,0:T(8,128)S(1)}, u32[]{:S(2)}, u32[]{:S(2)}) %collective-permute-start.23) | collective-permute-done | bytes 65568 | tf_op jit(solution)/shard_map/ppermute | solution.py:383
  (58 shorter events, 10.2 us)
Async XLA Ops:
  2.0 8.1 %collective-permute-start.2 = (f32[1,128,128]{2,1,0:T(8,128)S(1)}, f32[1,128,128]{2,1,0:T(8,128)S(1)}, u32[]{:S(2)}, u32[]{:S(2)}) collective-permute-start(f32[1,128,128]{2,1,0:T(8,128)S(1)} %get-tuple-element.26), channel_id=1, source_target_pairs={{0,6},{1,7},{2,4},{3,5},{4,2},{5,3},{6,0},{7,1},{8,14},{9,15},{10,... | collective-permute-start | bytes 196616 | tf_op jit(solution)/shard_map/ppermute | solution.py:383
  6.0 5.7 %collective-permute-start.1 = (f32[1,128,128]{2,1,0:T(8,128)S(1)}, f32[1,128,128]{2,1,0:T(8,128)S(1)}, u32[]{:S(2)}, u32[]{:S(2)}) collective-permute-start(f32[1,128,128]{2,1,0:T(8,128)S(1)} %get-tuple-element.26), channel_id=1, source_target_pairs={{0,4},{1,5},{2,6},{3,7},{4,0},{5,1},{6,2},{7,3},{8,12},{9,13},{10,... | collective-permute-start | bytes 196616 | tf_op jit(solution)/shard_map/ppermute | solution.py:383
  6.5 5.5 %collective-permute-start = (f32[1,128,128]{2,1,0:T(8,128)S(1)}, f32[1,128,128]{2,1,0:T(8,128)S(1)}, u32[]{:S(2)}, u32[]{:S(2)}) collective-permute-start(f32[1,128,128]{2,1,0:T(8,128)S(1)} %get-tuple-element.26), channel_id=1, source_target_pairs={{0,2},{1,3},{2,0},{3,1},{4,6},{5,7},{6,4},{7,5},{8,10},{9,11},{10,... | collective-permute-start | bytes 196616 | tf_op jit(solution)/shard_map/ppermute | solution.py:383
  8.0 16.3 %collective-permute-start.9 = (f32[2,4,128,128]{3,2,1,0:T(8,128)S(1)}, f32[2,4,128,128]{3,2,1,0:T(8,128)S(1)}, u32[]{:S(2)}, u32[]{:S(2)}) collective-permute-start(f32[2,4,128,128]{3,2,1,0:T(8,128)S(1)} %get-tuple-element.43), channel_id=1, source_target_pairs={{0,1},{1,0},{2,3},{3,2},{4,5},{5,4},{6,7},{7,6},{8,9},{9,8},{10,11... | collective-permute-start | bytes 1572872 | tf_op jit(solution)/shard_map/ppermute | solution.py:383
  8.1 10.5 %collective-permute-start.5 = (f32[2,2,128,128]{3,2,1,0:T(8,128)S(1)}, f32[2,2,128,128]{3,2,1,0:T(8,128)S(1)}, u32[]{:S(2)}, u32[]{:S(2)}) collective-permute-start(f32[2,2,128,128]{3,2,1,0:T(8,128)S(1)} %get-tuple-element.33), channel_id=1, source_target_pairs={{0,2},{1,3},{2,0},{3,1},{4,6},{5,7},{6,4},{7,5},{8,10},{9,11},{10,... | collective-permute-start | bytes 786440 | tf_op jit(solution)/shard_map/ppermute | solution.py:383
  10.0 14.0 %collective-permute-start.6 = (f32[2,2,128,128]{3,2,1,0:T(8,128)S(1)}, f32[2,2,128,128]{3,2,1,0:T(8,128)S(1)}, u32[]{:S(2)}, u32[]{:S(2)}) collective-permute-start(f32[2,2,128,128]{3,2,1,0:T(8,128)S(1)} %get-tuple-element.34), channel_id=1, source_target_pairs={{0,4},{1,5},{2,6},{3,7},{4,0},{5,1},{6,2},{7,3},{8,12},{9,13},{10,... | collective-permute-start | bytes 786440 | tf_op jit(solution)/shard_map/ppermute | solution.py:383
  11.6 12.5 %collective-permute-start.7 = (f32[2,2,128,128]{3,2,1,0:T(8,128)S(1)}, f32[2,2,128,128]{3,2,1,0:T(8,128)S(1)}, u32[]{:S(2)}, u32[]{:S(2)}) collective-permute-start(f32[2,2,128,128]{3,2,1,0:T(8,128)S(1)} %get-tuple-element.35), channel_id=1, source_target_pairs={{0,6},{1,7},{2,4},{3,5},{4,2},{5,3},{6,0},{7,1},{8,14},{9,15},{10,... | collective-permute-start | bytes 786440 | tf_op jit(solution)/shard_map/ppermute | solution.py:383
  12.0 6.5 %collective-permute-start.3 = (f32[3,128,128]{2,1,0:T(8,128)S(1)}, f32[3,128,128]{2,1,0:T(8,128)S(1)}, u32[]{:S(2)}, u32[]{:S(2)}) collective-permute-start(f32[3,128,128]{2,1,0:T(8,128)S(1)} %pad_maximum_fusion), channel_id=1, source_target_pairs={{0,8},{8,0},{16,24},{24,16},{1,9},{9,1},{17,25},{25,17},{2,10},{10... | collective-permute-start | bytes 589832 | tf_op jit(solution)/shard_map/ppermute | solution.py:383
  18.5 9.5 %collective-permute-start.4 = (f32[8,128,128]{2,1,0:T(8,128)S(1)}, f32[8,128,128]{2,1,0:T(8,128)S(1)}, u32[]{:S(2)}, u32[]{:S(2)}) collective-permute-start(f32[8,128,128]{2,1,0:T(8,128)S(1)} %constant_dynamic-update-slice_fusion.own), channel_id=1, source_target_pairs={{0,1},{1,0},{2,3},{3,2},{4,5},{5,4},{6,7},{7,6},{8,9},{9,8},{10,11... | collective-permute-start | bytes 1572872 | tf_op jit(solution)/shard_map/ppermute | solution.py:383
  24.2 7.4 %collective-permute-start.8 = (f32[4,2,128,128]{3,2,1,0:T(8,128)S(1)}, f32[4,2,128,128]{3,2,1,0:T(8,128)S(1)}, u32[]{:S(2)}, u32[]{:S(2)}) collective-permute-start(f32[4,2,128,128]{3,2,1,0:T(8,128)S(1)} %get-tuple-element.37), channel_id=1, source_target_pairs={{0,1},{1,0},{2,3},{3,2},{4,5},{5,4},{6,7},{7,6},{8,9},{9,8},{10,11... | collective-permute-start | bytes 1572872 | tf_op jit(solution)/shard_map/ppermute | solution.py:383
  24.4 13.2 %collective-permute-start.10 = (f32[2,2,128,128]{3,2,1,0:T(8,128)S(1)}, f32[2,2,128,128]{3,2,1,0:T(8,128)S(1)}, u32[]{:S(2)}, u32[]{:S(2)}) collective-permute-start(f32[2,2,128,128]{3,2,1,0:T(8,128)S(1)} %get-tuple-element.45), channel_id=1, source_target_pairs={{0,2},{1,3},{2,0},{3,1},{4,6},{5,7},{6,4},{7,5},{8,10},{9,11},{10,... | collective-permute-start | bytes 786440 | tf_op jit(solution)/shard_map/ppermute | solution.py:383
  25.6 12.5 %collective-permute-start.11 = (f32[2,2,128,128]{3,2,1,0:T(8,128)S(1)}, f32[2,2,128,128]{3,2,1,0:T(8,128)S(1)}, u32[]{:S(2)}, u32[]{:S(2)}) collective-permute-start(f32[2,2,128,128]{3,2,1,0:T(8,128)S(1)} %get-tuple-element.46), channel_id=1, source_target_pairs={{0,4},{1,5},{2,6},{3,7},{4,0},{5,1},{6,2},{7,3},{8,12},{9,13},{10,... | collective-permute-start | bytes 786440 | tf_op jit(solution)/shard_map/ppermute | solution.py:383
  26.5 13.2 %collective-permute-start.12 = (f32[2,2,128,128]{3,2,1,0:T(8,128)S(1)}, f32[2,2,128,128]{3,2,1,0:T(8,128)S(1)}, u32[]{:S(2)}, u32[]{:S(2)}) collective-permute-start(f32[2,2,128,128]{3,2,1,0:T(8,128)S(1)} %get-tuple-element.47), channel_id=1, source_target_pairs={{0,6},{1,7},{2,4},{3,5},{4,2},{5,3},{6,0},{7,1},{8,14},{9,15},{10,... | collective-permute-start | bytes 786440 | tf_op jit(solution)/shard_map/ppermute | solution.py:383
  44.9 2.0 %collective-permute-start.13 = (f32[4,264,128]{2,1,0:T(8,128)S(1)}, f32[4,264,128]{2,1,0:T(8,128)S(1)}, u32[]{:S(2)}, u32[]{:S(2)}) collective-permute-start(f32[4,264,128]{2,1,0:T(8,128)S(1)} %get-tuple-element.49), channel_id=1, source_target_pairs={{0,1},{1,0},{2,3},{3,2},{4,5},{5,4},{6,7},{7,6},{8,9},{9,8},{10,11... | collective-permute-start | bytes 1622024 | tf_op jit(solution)/shard_map/ppermute | solution.py:383
  47.0 5.9 %collective-permute-start.14 = (f32[128,128]{1,0:T(8,128)S(1)}, f32[128,128]{1,0:T(8,128)S(1)}, u32[]{:S(2)}, u32[]{:S(2)}) collective-permute-start(f32[128,128]{1,0:T(8,128)S(1)} %get-tuple-element.50), channel_id=1, source_target_pairs={{0,2},{1,3},{2,0},{3,1},{4,6},{5,7},{6,4},{7,5},{8,10},{9,11},{10,... | collective-permute-start | bytes 196616 | tf_op jit(solution)/shard_map/ppermute | solution.py:383
  47.8 6.3 %collective-permute-start.16 = (f32[128,128]{1,0:T(8,128)S(1)}, f32[128,128]{1,0:T(8,128)S(1)}, u32[]{:S(2)}, u32[]{:S(2)}) collective-permute-start(f32[128,128]{1,0:T(8,128)S(1)} %get-tuple-element.51), channel_id=1, source_target_pairs={{0,6},{1,7},{2,4},{3,5},{4,2},{5,3},{6,0},{7,1},{8,14},{9,15},{10,... | collective-permute-start | bytes 196616 | tf_op jit(solution)/shard_map/ppermute | solution.py:383
  49.3 5.7 %collective-permute-start.15 = (f32[128,128]{1,0:T(8,128)S(1)}, f32[128,128]{1,0:T(8,128)S(1)}, u32[]{:S(2)}, u32[]{:S(2)}) collective-permute-start(f32[128,128]{1,0:T(8,128)S(1)} %get-tuple-element.52), channel_id=1, source_target_pairs={{0,4},{1,5},{2,6},{3,7},{4,0},{5,1},{6,2},{7,3},{8,12},{9,13},{10,... | collective-permute-start | bytes 196616 | tf_op jit(solution)/shard_map/ppermute | solution.py:383
  50.5 6.1 %collective-permute-start.19 = (f32[136,128]{1,0:T(8,128)S(1)}, f32[136,128]{1,0:T(8,128)S(1)}, u32[]{:S(2)}, u32[]{:S(2)}) collective-permute-start(f32[136,128]{1,0:T(8,128)S(1)} %get-tuple-element.53), channel_id=1, source_target_pairs={{0,2},{1,3},{2,0},{3,1},{4,6},{5,7},{6,4},{7,5},{8,10},{9,11},{10,... | collective-permute-start | bytes 208904 | tf_op jit(solution)/shard_map/ppermute | solution.py:383
  51.4 5.3 %collective-permute-start.21 = (f32[136,128]{1,0:T(8,128)S(1)}, f32[136,128]{1,0:T(8,128)S(1)}, u32[]{:S(2)}, u32[]{:S(2)}) collective-permute-start(f32[136,128]{1,0:T(8,128)S(1)} %get-tuple-element.54), channel_id=1, source_target_pairs={{0,6},{1,7},{2,4},{3,5},{4,2},{5,3},{6,0},{7,1},{8,14},{9,15},{10,... | collective-permute-start | bytes 208904 | tf_op jit(solution)/shard_map/ppermute | solution.py:383
  52.9 4.5 %collective-permute-start.20 = (f32[136,128]{1,0:T(8,128)S(1)}, f32[136,128]{1,0:T(8,128)S(1)}, u32[]{:S(2)}, u32[]{:S(2)}) collective-permute-start(f32[136,128]{1,0:T(8,128)S(1)} %get-tuple-element.55), channel_id=1, source_target_pairs={{0,4},{1,5},{2,6},{3,7},{4,0},{5,1},{6,2},{7,3},{8,12},{9,13},{10,... | collective-permute-start | bytes 208904 | tf_op jit(solution)/shard_map/ppermute | solution.py:383
  55.0 4.6 %collective-permute-start.17 = (f32[128,128]{1,0:T(8,128)S(1)}, f32[128,128]{1,0:T(8,128)S(1)}, u32[]{:S(2)}, u32[]{:S(2)}) collective-permute-start(f32[128,128]{1,0:T(8,128)S(1)} %fusion.5), channel_id=1, source_target_pairs={{0,8},{8,0},{16,24},{24,16},{1,9},{9,1},{17,25},{25,17},{2,10},{10... | collective-permute-start | bytes 196616 | tf_op jit(solution)/shard_map/ppermute | solution.py:383
  57.4 5.0 %collective-permute-start.22 = (f32[128,128]{1,0:T(8,128)S(1)}, f32[128,128]{1,0:T(8,128)S(1)}, u32[]{:S(2)}, u32[]{:S(2)}) collective-permute-start(f32[128,128]{1,0:T(8,128)S(1)} %slice.58), channel_id=1, source_target_pairs={{0,8},{8,0},{16,24},{24,16},{1,9},{9,1},{17,25},{25,17},{2,10},{10... | collective-permute-start | bytes 196616 | tf_op jit(solution)/shard_map/ppermute | solution.py:383
  59.7 6.6 %collective-permute-start.18 = (f32[128,128]{1,0:T(8,128)S(1)}, f32[128,128]{1,0:T(8,128)S(1)}, u32[]{:S(2)}, u32[]{:S(2)}) collective-permute-start(f32[128,128]{1,0:T(8,128)S(1)} %add.37), channel_id=1, source_target_pairs={{0,16},{8,24},{16,0},{24,8},{1,17},{9,25},{17,1},{25,9},{2,18},{10... | collective-permute-start | bytes 196616 | tf_op jit(solution)/shard_map/ppermute | solution.py:383
  62.4 5.2 %collective-permute-start.23 = (f32[128,128]{1,0:T(8,128)S(1)}, f32[128,128]{1,0:T(8,128)S(1)}, u32[]{:S(2)}, u32[]{:S(2)}) collective-permute-start(f32[128,128]{1,0:T(8,128)S(1)} %slice_add_fusion), channel_id=1, source_target_pairs={{0,16},{8,24},{16,0},{24,8},{1,17},{9,25},{17,1},{25,9},{2,18},{10... | collective-permute-start | bytes 196616 | tf_op jit(solution)/shard_map/ppermute | solution.py:383
  (4 other events, 32.4 us)

commit v6 on v5

--- a/solution.py
+++ b/solution.py
@@ -323,7 +323,7 @@
 def adjoint_kernel(weight, electrodes, patterns, observed, *refs):
     place = my_place()
     depth, rows, columns, scale, root, *slopes, voltage = refs[:9]
-    *blocks, adjoint, given, field, residue, applied, later = refs[9:]
+    *blocks, adjoint, given, last_given, field, residue, applied, later = refs[9:]
     planes, height, _ = blocks[0].shape[1:]
     for step, block in enumerate(blocks):
         for relative in range(CORES):
@@ -343,18 +343,19 @@
         field, residue, applied, later, end, height,
     )
     clear_edges(adjoint, height=height)
-    gradient_blocks(place, 1, slopes, voltage, adjoint, given, planes, height)
+    gradient_pieces(place, 1, slopes, voltage, adjoint, (given, last_given), planes, height)
 
 
 def gradient_kernel(planes, height, *refs):
-    place = my_place()
-    *slopes, voltage, adjoint, kept = refs
-    gradient_blocks(place, 0, slopes, voltage, adjoint, kept, planes, height)
-
-
-def gradient_blocks(place, relative, slopes, voltage, adjoint, out, planes, height):
+    *slopes, voltage, adjoint, kept, last_kept = refs
+    gradient_pieces(
+        my_place(), 0, slopes, voltage, adjoint, (kept, last_kept), planes, height
+    )
+
+
+def gradient_pieces(place, relative, slopes, voltage, adjoint, outs, planes, height):
     along_depth, along_row, along_column = slopes
-    chips, width = out.shape[0], out.shape[2]
+    chips, rows, width = outs[0].shape
     size = planes * height
 
     def step(block, carry):
@@ -369,14 +370,16 @@
         result += at(along_row) * (at(adjoint, 1) - here)
         result += at(along_row, -1) * (here - at(adjoint, -1))
         face = at(along_column) * (ahead(here) - here)
-        out[block, :size, :] = result + (face + behind(face))
+        result += face + behind(face)
+        outs[0][block] = result[:rows]
+        outs[1][block, : size - rows, :] = result[rows:]
         return carry
 
     lax.fori_loop(0, chips, step, 0)
     lane = lax.broadcasted_iota(jnp.int32, (SPARE, width), 1)
     note = jnp.where(lane == place[2], voltage[...], 0.0)
     for block in range(chips):
-        out[block, size:, :] = note
+        outs[1][block, size - rows :, :] = note
 
 
 def swap(values, axis, size, bit):
@@ -457,10 +460,12 @@
         scratch=[room] * 5,
         limit=8,
     )
-    block = shape(chips, plane_count * row_count + SPARE, column_count)
-    adjoint, given = call(
+    cut = (plane_count + 1) // 2 * row_count
+    sizes = (cut, plane_count * row_count - cut + SPARE)
+    pair = [shape(chips, size, column_count) for size in sizes]
+    adjoint, *given = call(
         functools.partial(adjoint_kernel, 0.1 * strength),
-        [whole, block],
+        [whole] + pair,
         (
             electrodes, patterns.T, observed,
             *coefficients, *slopes, voltage, *adjoint_blocks,
@@ -469,24 +474,23 @@
         scratch=[room] * 4,
         limit=8,
     )
-    (kept,) = call(
+    received = []
+    for piece in given:
+        received.append(core_swap(piece))
+    kept = call(
         functools.partial(gradient_kernel, plane_count, row_count),
-        [block],
+        pair,
         (*slopes, voltage, adjoint),
         [VMEM] * 5,
     )
-    summed = kept + core_swap(given)
-    first_rows = row_count * ((plane_count + 1) // 2)
-    cuts = ((0, first_rows), (first_rows, plane_count * row_count + SPARE))
-    cut = [summed[:, low:high] for low, high in cuts]
-    pieces = [piece[0] for piece in cut]
-    received = {}
-    for step in range(1, chips):
-        for number, piece in enumerate(cut):
-            received[number, step] = chip_swap(piece[step], step)
-    for number in range(len(pieces)):
+    summed, pieces = [], []
+    for number in range(len(pair)):
+        summed.append(kept[number] + received[number])
+    for piece in summed:
+        got = []
         for step in range(1, chips):
-            pieces[number] = pieces[number] + received[number, step]
+            got.append(chip_swap(piece[step], step))
+        pieces.append(piece[0] + sum(got[1:], got[0]))
     predicted = pieces[-1][-SPARE, :pattern_count]
     pieces[-1] = pieces[-1][:-SPARE]
     bit = 1

time: 68.5 us -> 67.4 us (0.984)
  waiting for transfers between devices: 18.5 us -> 16.4 us
  starting transfers between devices: 29.1 us -> 30.2 us
    ppermute x24 -> x25, waiting for transfers between devices: 18.5 us -> 16.4 us  [swap(): return lax.ppermute(values, axis, [(i, i ^ bit) for i in range(size)])]
    ppermute x24 -> x25, starting transfers between devices: 29.1 us -> 30.2 us  [swap(): return lax.ppermute(values, axis, [(i, i ^ bit) for i in range(size)])]
  transfers between devices with their start and end apart: 24 -> 25, of which waited for: 11 -> 10; matrix products, arithmetic and copies ran while one was open for 1% -> 1% of each run, Pallas kernels for 17% -> 18%
where the time goes in v6:
time: 67.4 us; the launch traced here: 67.2 us
  starting transfers between devices  30.2 us (45%)
  Pallas kernels  18.4 us (27%)
  waiting for transfers between devices  16.4 us (24%)
  between operations  0.9 us (1%)
  other arithmetic  0.83 us (1%)
    ppermute x25, starting transfers between devices, swap(): return lax.ppermute(values, axis, [(i, i ^ bit) for i in range(size)])  30.2 us
    pallas_call x8, Pallas kernels, call(): pl.pallas_call(body, out_shape=out_shape, in_specs=in_specs, out_specs=[V...  18.4 us
    ppermute x25, waiting for transfers between devices, swap(): return lax.ppermute(values, axis, [(i, i ^ bit) for i in range(size)])  16.4 us
  transfers between devices with their start and end apart: 25, of which 10 were waited for; matrix products, arithmetic and copies ran while one was open for 1% of the time, Pallas kernels for 18%

profile of v6, /device:TPU:0, one launch (start us, length us, event | category | flops | bytes accessed | tf_op | source)
XLA Modules:
  0.0 67.2 jit_solution(14353085397299822389)
XLA Ops:
  0.6 1.3 %shard_map.77 = (f32[1,128,128]{2,1,0:T(8,128)S(1)}, f32[2,2,128,128]{3,2,1,0:T(8,128)S(1)}, f32[2,2,128,128]{3,2,1,0:T(8,128)S(1)}, f32[2,2,128,128]{3,2,1,0:T(8,128)S(1)}, f32[2,2,128,128]{3,2,1,0:T(8,128)S(1)}) custom-call(f32[2,128,128]{2,1,0:T(8,128)} %conductivity.1, f32[2,8,128,128]{3,2,1,0:T(8,128)} %forward.1), custom_call_target="tpu_custom_call" | custom-call | flops 2293760 | bytes 2293760 | tf_op jit(solution)/shard_map/pallas_call | solution.py:29
  2.0 4.0 %collective-permute-start.2 = (f32[1,128,128]{2,1,0:T(8,128)S(1)}, f32[1,128,128]{2,1,0:T(8,128)S(1)}, u32[]{:S(2)}, u32[]{:S(2)}) collective-permute-start(f32[1,128,128]{2,1,0:T(8,128)S(1)} %get-tuple-element.29), channel_id=1, source_target_pairs={{0,6},{1,7},{2,4},{3,5},{4,2},{5,3},{6,0},{7,1},{8,14},{9,15},{10,... | collective-permute-start | bytes 196616 | tf_op jit(solution)/shard_map/ppermute | solution.py:386
  6.6 1.4 %shard_map.81 = (f32[2,4,128,128]{3,2,1,0:T(8,128)S(1)}, f32[2,4,128,128]{3,2,1,0:T(8,128)S(1)}) custom-call(f32[2,8,128,128]{3,2,1,0:T(8,128)} %adjoint.1), custom_call_target="tpu_custom_call" | custom-call | flops 2097152 | bytes 2097152 | tf_op jit(solution)/shard_map/pallas_call | solution.py:29
  8.1 2.0 %collective-permute-start.5 = (f32[2,2,128,128]{3,2,1,0:T(8,128)S(1)}, f32[2,2,128,128]{3,2,1,0:T(8,128)S(1)}, u32[]{:S(2)}, u32[]{:S(2)}) collective-permute-start(f32[2,2,128,128]{3,2,1,0:T(8,128)S(1)} %get-tuple-element.36), channel_id=1, source_target_pairs={{0,2},{1,3},{2,0},{3,1},{4,6},{5,7},{6,4},{7,5},{8,10},{9,11},{10,... | collective-permute-start | bytes 786440 | tf_op jit(solution)/shard_map/ppermute | solution.py:386
  10.0 1.6 %collective-permute-start.6 = (f32[2,2,128,128]{3,2,1,0:T(8,128)S(1)}, f32[2,2,128,128]{3,2,1,0:T(8,128)S(1)}, u32[]{:S(2)}, u32[]{:S(2)}) collective-permute-start(f32[2,2,128,128]{3,2,1,0:T(8,128)S(1)} %get-tuple-element.37), channel_id=1, source_target_pairs={{0,4},{1,5},{2,6},{3,7},{4,0},{5,1},{6,2},{7,3},{8,12},{9,13},{10,... | collective-permute-start | bytes 786440 | tf_op jit(solution)/shard_map/ppermute | solution.py:386
  12.0 1.8 %collective-permute-start.3 = (f32[3,128,128]{2,1,0:T(8,128)S(1)}, f32[3,128,128]{2,1,0:T(8,128)S(1)}, u32[]{:S(2)}, u32[]{:S(2)}) collective-permute-start(f32[3,128,128]{2,1,0:T(8,128)S(1)} %pad_maximum_fusion), channel_id=1, source_target_pairs={{0,8},{8,0},{16,24},{24,16},{1,9},{9,1},{17,25},{25,17},{2,10},{10... | collective-permute-start | bytes 589832 | tf_op jit(solution)/shard_map/ppermute | solution.py:386
  13.8 4.7 %collective-permute-done.3 = f32[3,128,128]{2,1,0:T(8,128)S(1)} collective-permute-done((f32[3,128,128]{2,1,0:T(8,128)S(1)}, f32[3,128,128]{2,1,0:T(8,128)S(1)}, u32[]{:S(2)}, u32[]{:S(2)}) %collective-permute-start.3) | collective-permute-done | bytes 196640 | tf_op jit(solution)/shard_map/ppermute | solution.py:386
  18.6 5.5 %collective-permute-done.6.refs_2_ = f32[2,2,128,128]{3,2,1,0:T(8,128)S(1)} collective-permute-done((f32[2,2,128,128]{3,2,1,0:T(8,128)S(1)}, f32[2,2,128,128]{3,2,1,0:T(8,128)S(1)}, u32[]{:S(2)}, u32[]{:S(2)}) %collective-permute-start.6) | collective-permute-done | bytes 262176 | tf_op jit(solution)/shard_map/ppermute | solution.py:386
  24.4 1.2 %collective-permute-start.10 = (f32[2,2,128,128]{3,2,1,0:T(8,128)S(1)}, f32[2,2,128,128]{3,2,1,0:T(8,128)S(1)}, u32[]{:S(2)}, u32[]{:S(2)}) collective-permute-start(f32[2,2,128,128]{3,2,1,0:T(8,128)S(1)} %get-tuple-element.48), channel_id=1, source_target_pairs={{0,2},{1,3},{2,0},{3,1},{4,6},{5,7},{6,4},{7,5},{8,10},{9,11},{10,... | collective-permute-start | bytes 786440 | tf_op jit(solution)/shard_map/ppermute | solution.py:386
  26.5 1.4 %collective-permute-start.12 = (f32[2,2,128,128]{3,2,1,0:T(8,128)S(1)}, f32[2,2,128,128]{3,2,1,0:T(8,128)S(1)}, u32[]{:S(2)}, u32[]{:S(2)}) collective-permute-start(f32[2,2,128,128]{3,2,1,0:T(8,128)S(1)} %get-tuple-element.50), channel_id=1, source_target_pairs={{0,6},{1,7},{2,4},{3,5},{4,2},{5,3},{6,0},{7,1},{8,14},{9,15},{10,... | collective-permute-start | bytes 786440 | tf_op jit(solution)/shard_map/ppermute | solution.py:386
  27.9 3.7 %shard_map.78 = (f32[2304,128]{1,0:T(8,128)S(1)}, f32[2304,128]{1,0:T(8,128)S(1)}, f32[2304,128]{1,0:T(8,128)S(1)}, f32[2304,128]{1,0:T(8,128)S(1)}, f32[2304,128]{1,0:T(8,128)S(1)}) custom-call(f32[8,128,128]{2,1,0:T(8,128)S(1)} %constant_dynamic-update-slice_fusion.own, f32[8,128,128]{2,1,0:T(8,128)S(1)} %collective-permute-done.4.others), custom_call_target="tpu_custom_call" | custom-call | flops 6946816 | bytes 6946816 | tf_op jit(solution)/shard_map/pallas_call | solution.py:29
  31.7 5.9 %shard_map.80 = (f32[2304,128]{1,0:T(8,128)S(1)}, f32[2304,128]{1,0:T(8,128)S(1)}, f32[2304,128]{1,0:T(8,128)S(1)}, f32[8,128]{1,0:T(8,128)S(1)}) custom-call(s32[128]{0:T(128)S(1)} %copy-done.1, s32[4,8]{1,0:T(4,128)S(1)} %bitcast.24, f32[2304,128]{1,0:T(8,128)S(1)} %get-tuple-element.30.refs_0_, f32[2304,128]{1,0:T(8,128)S(1)} %get-tuple-element.31.refs_1_, ...), custom_call_target="tpu_custom_call" | custom-call | flops 10490496 | bytes 10490496 | tf_op jit(solution)/shard_map/pallas_call | solution.py:29
  38.1 1.6 %collective-permute-done.12.refs_12_ = f32[2,2,128,128]{3,2,1,0:T(8,128)S(1)} collective-permute-done((f32[2,2,128,128]{3,2,1,0:T(8,128)S(1)}, f32[2,2,128,128]{3,2,1,0:T(8,128)S(1)}, u32[]{:S(2)}, u32[]{:S(2)}) %collective-permute-start.12) | collective-permute-done | bytes 262176 | tf_op jit(solution)/shard_map/ppermute | solution.py:386
  39.7 5.2 %shard_map.83 = (f32[2304,128]{1,0:T(8,128)S(1)}, f32[4,128,128]{2,1,0:T(8,128)S(1)}, f32[4,136,128]{2,1,0:T(8,128)S(1)}) custom-call(s32[128]{0:T(128)S(1)} %copy-done.1, s32[4,8]{1,0:T(4,128)S(1)} %bitcast.25, f32[8]{0:T(128)S(1)} %copy-done.2, f32[2304,128]{1,0:T(8,128)S(1)} %get-tuple-element.30.refs_0_, f32[2304,128]{1,0:T(8,128)S(1)} %get-tuple-element.31.refs_1_, ...), custom_call_target="tpu_custom_call" | custom-call | flops 12210848 | bytes 12210848 | tf_op jit(solution)/shard_map/pallas_call | solution.py:29
  47.4 1.4 %collective-permute-start.16 = (f32[128,128]{1,0:T(8,128)S(1)}, f32[128,128]{1,0:T(8,128)S(1)}, u32[]{:S(2)}, u32[]{:S(2)}) collective-permute-start(f32[128,128]{1,0:T(8,128)S(1)} %get-tuple-element.60), channel_id=1, source_target_pairs={{0,6},{1,7},{2,4},{3,5},{4,2},{5,3},{6,0},{7,1},{8,14},{9,15},{10,... | collective-permute-start | bytes 196616 | tf_op jit(solution)/shard_map/ppermute | solution.py:386
  48.8 1.2 %collective-permute-start.14 = (f32[128,128]{1,0:T(8,128)S(1)}, f32[128,128]{1,0:T(8,128)S(1)}, u32[]{:S(2)}, u32[]{:S(2)}) collective-permute-start(f32[128,128]{1,0:T(8,128)S(1)} %get-tuple-element.61), channel_id=1, source_target_pairs={{0,2},{1,3},{2,0},{3,1},{4,6},{5,7},{6,4},{7,5},{8,10},{9,11},{10,... | collective-permute-start | bytes 196616 | tf_op jit(solution)/shard_map/ppermute | solution.py:386
  51.0 1.4 %collective-permute-start.22 = (f32[136,128]{1,0:T(8,128)S(1)}, f32[136,128]{1,0:T(8,128)S(1)}, u32[]{:S(2)}, u32[]{:S(2)}) collective-permute-start(f32[136,128]{1,0:T(8,128)S(1)} %get-tuple-element.57), channel_id=1, source_target_pairs={{0,6},{1,7},{2,4},{3,5},{4,2},{5,3},{6,0},{7,1},{8,14},{9,15},{10,... | collective-permute-start | bytes 208904 | tf_op jit(solution)/shard_map/ppermute | solution.py:386
  52.5 1.2 %collective-permute-start.20 = (f32[136,128]{1,0:T(8,128)S(1)}, f32[136,128]{1,0:T(8,128)S(1)}, u32[]{:S(2)}, u32[]{:S(2)}) collective-permute-start(f32[136,128]{1,0:T(8,128)S(1)} %get-tuple-element.58), channel_id=1, source_target_pairs={{0,2},{1,3},{2,0},{3,1},{4,6},{5,7},{6,4},{7,5},{8,10},{9,11},{10,... | collective-permute-start | bytes 208904 | tf_op jit(solution)/shard_map/ppermute | solution.py:386
  53.7 1.6 %collective-permute-start.17 = (f32[128,128]{1,0:T(8,128)S(1)}, f32[128,128]{1,0:T(8,128)S(1)}, u32[]{:S(2)}, u32[]{:S(2)}) collective-permute-start(f32[128,128]{1,0:T(8,128)S(1)} %fusion.1), channel_id=1, source_target_pairs={{0,8},{8,0},{16,24},{24,16},{1,9},{9,1},{17,25},{25,17},{2,10},{10... | collective-permute-start | bytes 196616 | tf_op jit(solution)/shard_map/ppermute | solution.py:386
  55.4 0.9 %collective-permute-done.22 = f32[136,128]{1,0:T(8,128)S(1)} collective-permute-done((f32[136,128]{1,0:T(8,128)S(1)}, f32[136,128]{1,0:T(8,128)S(1)}, u32[]{:S(2)}, u32[]{:S(2)}) %collective-permute-start.22) | collective-permute-done | bytes 69664 | tf_op jit(solution)/shard_map/ppermute | solution.py:386
  56.8 1.6 %collective-permute-start.23 = (f32[128,128]{1,0:T(8,128)S(1)}, f32[128,128]{1,0:T(8,128)S(1)}, u32[]{:S(2)}, u32[]{:S(2)}) collective-permute-start(f32[128,128]{1,0:T(8,128)S(1)} %slice.48), channel_id=1, source_target_pairs={{0,8},{8,0},{16,24},{24,16},{1,9},{9,1},{17,25},{25,17},{2,10},{10... | collective-permute-start | bytes 196616 | tf_op jit(solution)/shard_map/ppermute | solution.py:386
  58.5 2.7 %collective-permute-start.18 = (f32[128,128]{1,0:T(8,128)S(1)}, f32[128,128]{1,0:T(8,128)S(1)}, u32[]{:S(2)}, u32[]{:S(2)}) collective-permute-start(f32[128,128]{1,0:T(8,128)S(1)} %add.40), channel_id=1, source_target_pairs={{0,16},{8,24},{16,0},{24,8},{1,17},{9,25},{17,1},{25,9},{2,18},{10... | collective-permute-start | bytes 196616 | tf_op jit(solution)/shard_map/ppermute | solution.py:386
  61.3 2.5 %collective-permute-start.24 = (f32[128,128]{1,0:T(8,128)S(1)}, f32[128,128]{1,0:T(8,128)S(1)}, u32[]{:S(2)}, u32[]{:S(2)}) collective-permute-start(f32[128,128]{1,0:T(8,128)S(1)} %slice_add_fusion), channel_id=1, source_target_pairs={{0,16},{8,24},{16,0},{24,8},{1,17},{9,25},{17,1},{25,9},{2,18},{10... | collective-permute-start | bytes 196616 | tf_op jit(solution)/shard_map/ppermute | solution.py:386
  65.2 1.4 %collective-permute-done.24 = f32[128,128]{1,0:T(8,128)S(1)} collective-permute-done((f32[128,128]{1,0:T(8,128)S(1)}, f32[128,128]{1,0:T(8,128)S(1)}, u32[]{:S(2)}, u32[]{:S(2)}) %collective-permute-start.24) | collective-permute-done | bytes 65568 | tf_op jit(solution)/shard_map/ppermute | solution.py:386
  (61 shorter events, 9.0 us)
Async XLA Ops:
  2.0 8.1 %collective-permute-start.2 = (f32[1,128,128]{2,1,0:T(8,128)S(1)}, f32[1,128,128]{2,1,0:T(8,128)S(1)}, u32[]{:S(2)}, u32[]{:S(2)}) collective-permute-start(f32[1,128,128]{2,1,0:T(8,128)S(1)} %get-tuple-element.29), channel_id=1, source_target_pairs={{0,6},{1,7},{2,4},{3,5},{4,2},{5,3},{6,0},{7,1},{8,14},{9,15},{10,... | collective-permute-start | bytes 196616 | tf_op jit(solution)/shard_map/ppermute | solution.py:386
  6.0 5.7 %collective-permute-start.1 = (f32[1,128,128]{2,1,0:T(8,128)S(1)}, f32[1,128,128]{2,1,0:T(8,128)S(1)}, u32[]{:S(2)}, u32[]{:S(2)}) collective-permute-start(f32[1,128,128]{2,1,0:T(8,128)S(1)} %get-tuple-element.29), channel_id=1, source_target_pairs={{0,4},{1,5},{2,6},{3,7},{4,0},{5,1},{6,2},{7,3},{8,12},{9,13},{10,... | collective-permute-start | bytes 196616 | tf_op jit(solution)/shard_map/ppermute | solution.py:386
  6.5 5.5 %collective-permute-start = (f32[1,128,128]{2,1,0:T(8,128)S(1)}, f32[1,128,128]{2,1,0:T(8,128)S(1)}, u32[]{:S(2)}, u32[]{:S(2)}) collective-permute-start(f32[1,128,128]{2,1,0:T(8,128)S(1)} %get-tuple-element.29), channel_id=1, source_target_pairs={{0,2},{1,3},{2,0},{3,1},{4,6},{5,7},{6,4},{7,5},{8,10},{9,11},{10,... | collective-permute-start | bytes 196616 | tf_op jit(solution)/shard_map/ppermute | solution.py:386
  8.0 16.3 %collective-permute-start.9 = (f32[2,4,128,128]{3,2,1,0:T(8,128)S(1)}, f32[2,4,128,128]{3,2,1,0:T(8,128)S(1)}, u32[]{:S(2)}, u32[]{:S(2)}) collective-permute-start(f32[2,4,128,128]{3,2,1,0:T(8,128)S(1)} %get-tuple-element.46), channel_id=1, source_target_pairs={{0,1},{1,0},{2,3},{3,2},{4,5},{5,4},{6,7},{7,6},{8,9},{9,8},{10,11... | collective-permute-start | bytes 1572872 | tf_op jit(solution)/shard_map/ppermute | solution.py:386
  8.1 10.5 %collective-permute-start.5 = (f32[2,2,128,128]{3,2,1,0:T(8,128)S(1)}, f32[2,2,128,128]{3,2,1,0:T(8,128)S(1)}, u32[]{:S(2)}, u32[]{:S(2)}) collective-permute-start(f32[2,2,128,128]{3,2,1,0:T(8,128)S(1)} %get-tuple-element.36), channel_id=1, source_target_pairs={{0,2},{1,3},{2,0},{3,1},{4,6},{5,7},{6,4},{7,5},{8,10},{9,11},{10,... | collective-permute-start | bytes 786440 | tf_op jit(solution)/shard_map/ppermute | solution.py:386
  10.0 14.0 %collective-permute-start.6 = (f32[2,2,128,128]{3,2,1,0:T(8,128)S(1)}, f32[2,2,128,128]{3,2,1,0:T(8,128)S(1)}, u32[]{:S(2)}, u32[]{:S(2)}) collective-permute-start(f32[2,2,128,128]{3,2,1,0:T(8,128)S(1)} %get-tuple-element.37), channel_id=1, source_target_pairs={{0,4},{1,5},{2,6},{3,7},{4,0},{5,1},{6,2},{7,3},{8,12},{9,13},{10,... | collective-permute-start | bytes 786440 | tf_op jit(solution)/shard_map/ppermute | solution.py:386
  11.6 12.5 %collective-permute-start.7 = (f32[2,2,128,128]{3,2,1,0:T(8,128)S(1)}, f32[2,2,128,128]{3,2,1,0:T(8,128)S(1)}, u32[]{:S(2)}, u32[]{:S(2)}) collective-permute-start(f32[2,2,128,128]{3,2,1,0:T(8,128)S(1)} %get-tuple-element.38), channel_id=1, source_target_pairs={{0,6},{1,7},{2,4},{3,5},{4,2},{5,3},{6,0},{7,1},{8,14},{9,15},{10,... | collective-permute-start | bytes 786440 | tf_op jit(solution)/shard_map/ppermute | solution.py:386
  12.0 6.5 %collective-permute-start.3 = (f32[3,128,128]{2,1,0:T(8,128)S(1)}, f32[3,128,128]{2,1,0:T(8,128)S(1)}, u32[]{:S(2)}, u32[]{:S(2)}) collective-permute-start(f32[3,128,128]{2,1,0:T(8,128)S(1)} %pad_maximum_fusion), channel_id=1, source_target_pairs={{0,8},{8,0},{16,24},{24,16},{1,9},{9,1},{17,25},{25,17},{2,10},{10... | collective-permute-start | bytes 589832 | tf_op jit(solution)/shard_map/ppermute | solution.py:386
  18.5 9.5 %collective-permute-start.4 = (f32[8,128,128]{2,1,0:T(8,128)S(1)}, f32[8,128,128]{2,1,0:T(8,128)S(1)}, u32[]{:S(2)}, u32[]{:S(2)}) collective-permute-start(f32[8,128,128]{2,1,0:T(8,128)S(1)} %constant_dynamic-update-slice_fusion.own), channel_id=1, source_target_pairs={{0,1},{1,0},{2,3},{3,2},{4,5},{5,4},{6,7},{7,6},{8,9},{9,8},{10,11... | collective-permute-start | bytes 1572872 | tf_op jit(solution)/shard_map/ppermute | solution.py:386
  24.2 7.4 %collective-permute-start.8 = (f32[4,2,128,128]{3,2,1,0:T(8,128)S(1)}, f32[4,2,128,128]{3,2,1,0:T(8,128)S(1)}, u32[]{:S(2)}, u32[]{:S(2)}) collective-permute-start(f32[4,2,128,128]{3,2,1,0:T(8,128)S(1)} %get-tuple-element.40), channel_id=1, source_target_pairs={{0,1},{1,0},{2,3},{3,2},{4,5},{5,4},{6,7},{7,6},{8,9},{9,8},{10,11... | collective-permute-start | bytes 1572872 | tf_op jit(solution)/shard_map/ppermute | solution.py:386
  24.4 13.2 %collective-permute-start.10 = (f32[2,2,128,128]{3,2,1,0:T(8,128)S(1)}, f32[2,2,128,128]{3,2,1,0:T(8,128)S(1)}, u32[]{:S(2)}, u32[]{:S(2)}) collective-permute-start(f32[2,2,128,128]{3,2,1,0:T(8,128)S(1)} %get-tuple-element.48), channel_id=1, source_target_pairs={{0,2},{1,3},{2,0},{3,1},{4,6},{5,7},{6,4},{7,5},{8,10},{9,11},{10,... | collective-permute-start | bytes 786440 | tf_op jit(solution)/shard_map/ppermute | solution.py:386
  25.6 12.5 %collective-permute-start.11 = (f32[2,2,128,128]{3,2,1,0:T(8,128)S(1)}, f32[2,2,128,128]{3,2,1,0:T(8,128)S(1)}, u32[]{:S(2)}, u32[]{:S(2)}) collective-permute-start(f32[2,2,128,128]{3,2,1,0:T(8,128)S(1)} %get-tuple-element.49), channel_id=1, source_target_pairs={{0,4},{1,5},{2,6},{3,7},{4,0},{5,1},{6,2},{7,3},{8,12},{9,13},{10,... | collective-permute-start | bytes 786440 | tf_op jit(solution)/shard_map/ppermute | solution.py:386
  26.5 13.2 %collective-permute-start.12 = (f32[2,2,128,128]{3,2,1,0:T(8,128)S(1)}, f32[2,2,128,128]{3,2,1,0:T(8,128)S(1)}, u32[]{:S(2)}, u32[]{:S(2)}) collective-permute-start(f32[2,2,128,128]{3,2,1,0:T(8,128)S(1)} %get-tuple-element.50), channel_id=1, source_target_pairs={{0,6},{1,7},{2,4},{3,5},{4,2},{5,3},{6,0},{7,1},{8,14},{9,15},{10,... | collective-permute-start | bytes 786440 | tf_op jit(solution)/shard_map/ppermute | solution.py:386
  44.9 5.1 %collective-permute-start.19 = (f32[4,136,128]{2,1,0:T(8,128)S(1)}, f32[4,136,128]{2,1,0:T(8,128)S(1)}, u32[]{:S(2)}, u32[]{:S(2)}) collective-permute-start(f32[4,136,128]{2,1,0:T(8,128)S(1)} %get-tuple-element.55), channel_id=1, source_target_pairs={{0,1},{1,0},{2,3},{3,2},{4,5},{5,4},{6,7},{7,6},{8,9},{9,8},{10,11... | collective-permute-start | bytes 835592 | tf_op jit(solution)/shard_map/ppermute | solution.py:386
  46.5 5.9 %collective-permute-start.15 = (f32[128,128]{1,0:T(8,128)S(1)}, f32[128,128]{1,0:T(8,128)S(1)}, u32[]{:S(2)}, u32[]{:S(2)}) collective-permute-start(f32[128,128]{1,0:T(8,128)S(1)} %get-tuple-element.59), channel_id=1, source_target_pairs={{0,4},{1,5},{2,6},{3,7},{4,0},{5,1},{6,2},{7,3},{8,12},{9,13},{10,... | collective-permute-start | bytes 196616 | tf_op jit(solution)/shard_map/ppermute | solution.py:386
  47.4 6.3 %collective-permute-start.16 = (f32[128,128]{1,0:T(8,128)S(1)}, f32[128,128]{1,0:T(8,128)S(1)}, u32[]{:S(2)}, u32[]{:S(2)}) collective-permute-start(f32[128,128]{1,0:T(8,128)S(1)} %get-tuple-element.60), channel_id=1, source_target_pairs={{0,6},{1,7},{2,4},{3,5},{4,2},{5,3},{6,0},{7,1},{8,14},{9,15},{10,... | collective-permute-start | bytes 196616 | tf_op jit(solution)/shard_map/ppermute | solution.py:386
  48.8 4.9 %collective-permute-start.14 = (f32[128,128]{1,0:T(8,128)S(1)}, f32[128,128]{1,0:T(8,128)S(1)}, u32[]{:S(2)}, u32[]{:S(2)}) collective-permute-start(f32[128,128]{1,0:T(8,128)S(1)} %get-tuple-element.61), channel_id=1, source_target_pairs={{0,2},{1,3},{2,0},{3,1},{4,6},{5,7},{6,4},{7,5},{8,10},{9,11},{10,... | collective-permute-start | bytes 196616 | tf_op jit(solution)/shard_map/ppermute | solution.py:386
  50.1 5.2 %collective-permute-start.21 = (f32[136,128]{1,0:T(8,128)S(1)}, f32[136,128]{1,0:T(8,128)S(1)}, u32[]{:S(2)}, u32[]{:S(2)}) collective-permute-start(f32[136,128]{1,0:T(8,128)S(1)} %get-tuple-element.56), channel_id=1, source_target_pairs={{0,4},{1,5},{2,6},{3,7},{4,0},{5,1},{6,2},{7,3},{8,12},{9,13},{10,... | collective-permute-start | bytes 208904 | tf_op jit(solution)/shard_map/ppermute | solution.py:386
  51.0 5.3 %collective-permute-start.22 = (f32[136,128]{1,0:T(8,128)S(1)}, f32[136,128]{1,0:T(8,128)S(1)}, u32[]{:S(2)}, u32[]{:S(2)}) collective-permute-start(f32[136,128]{1,0:T(8,128)S(1)} %get-tuple-element.57), channel_id=1, source_target_pairs={{0,6},{1,7},{2,4},{3,5},{4,2},{5,3},{6,0},{7,1},{8,14},{9,15},{10,... | collective-permute-start | bytes 208904 | tf_op jit(solution)/shard_map/ppermute | solution.py:386
  52.5 4.3 %collective-permute-start.20 = (f32[136,128]{1,0:T(8,128)S(1)}, f32[136,128]{1,0:T(8,128)S(1)}, u32[]{:S(2)}, u32[]{:S(2)}) collective-permute-start(f32[136,128]{1,0:T(8,128)S(1)} %get-tuple-element.58), channel_id=1, source_target_pairs={{0,2},{1,3},{2,0},{3,1},{4,6},{5,7},{6,4},{7,5},{8,10},{9,11},{10,... | collective-permute-start | bytes 208904 | tf_op jit(solution)/shard_map/ppermute | solution.py:386
  53.7 4.8 %collective-permute-start.17 = (f32[128,128]{1,0:T(8,128)S(1)}, f32[128,128]{1,0:T(8,128)S(1)}, u32[]{:S(2)}, u32[]{:S(2)}) collective-permute-start(f32[128,128]{1,0:T(8,128)S(1)} %fusion.1), channel_id=1, source_target_pairs={{0,8},{8,0},{16,24},{24,16},{1,9},{9,1},{17,25},{25,17},{2,10},{10... | collective-permute-start | bytes 196616 | tf_op jit(solution)/shard_map/ppermute | solution.py:386
  56.8 4.5 %collective-permute-start.23 = (f32[128,128]{1,0:T(8,128)S(1)}, f32[128,128]{1,0:T(8,128)S(1)}, u32[]{:S(2)}, u32[]{:S(2)}) collective-permute-start(f32[128,128]{1,0:T(8,128)S(1)} %slice.48), channel_id=1, source_target_pairs={{0,8},{8,0},{16,24},{24,16},{1,9},{9,1},{17,25},{25,17},{2,10},{10... | collective-permute-start | bytes 196616 | tf_op jit(solution)/shard_map/ppermute | solution.py:386
  58.5 6.6 %collective-permute-start.18 = (f32[128,128]{1,0:T(8,128)S(1)}, f32[128,128]{1,0:T(8,128)S(1)}, u32[]{:S(2)}, u32[]{:S(2)}) collective-permute-start(f32[128,128]{1,0:T(8,128)S(1)} %add.40), channel_id=1, source_target_pairs={{0,16},{8,24},{16,0},{24,8},{1,17},{9,25},{17,1},{25,9},{2,18},{10... | collective-permute-start | bytes 196616 | tf_op jit(solution)/shard_map/ppermute | solution.py:386
  61.3 5.2 %collective-permute-start.24 = (f32[128,128]{1,0:T(8,128)S(1)}, f32[128,128]{1,0:T(8,128)S(1)}, u32[]{:S(2)}, u32[]{:S(2)}) collective-permute-start(f32[128,128]{1,0:T(8,128)S(1)} %slice_add_fusion), channel_id=1, source_target_pairs={{0,16},{8,24},{16,0},{24,8},{1,17},{9,25},{17,1},{25,9},{2,18},{10... | collective-permute-start | bytes 196616 | tf_op jit(solution)/shard_map/ppermute | solution.py:386
  (5 other events, 34.0 us)

commit v7 on v6

--- a/solution.py
+++ b/solution.py
@@ -115,14 +115,14 @@
     size = fetched.shape[0]
     first = lax.rem(lax.axis_index("pat"), share) * size
     pairs = [(conductivity.at[pl.ds(first, size)], fetched)]
-    for step, out in enumerate(refs[:-1]):
+    for step, out in enumerate(refs[:-1], start=1):
         pairs.append((forward.at[:, pl.ds(CORES * (chip ^ step), CORES)], out))
     copy_all(pairs, refs[-1])
 
 
-def stage_adjoint_kernel(adjoint, own, give, sems):
-    core = my_place()[1]
-    pairs = []
+def stage_rest_kernel(forward, adjoint, kept, own, give, sems):
+    chip, core, _ = my_place()
+    pairs = [(forward.at[:, pl.ds(CORES * chip, CORES)], kept)]
     for plane in range(own.shape[0]):
         for other in range(own.shape[1]):
             pairs.append((adjoint.at[plane, CORES * other + 1 - core], give.at[plane, other]))
@@ -411,24 +411,25 @@
 
     fetched, *sends = call(
         functools.partial(stage_kernel, share),
-        [shape(plane_count // share, *plane)] + [shape(plane_count, CORES, *plane)] * chips,
+        [shape(plane_count // share, *plane)]
+        + [shape(plane_count, CORES, *plane)] * (chips - 1),
         (in_place(conductivity), in_place(warm_forward)),
         [HBM, HBM],
-        scratch=[pltpu.SemaphoreType.DMA((1 + chips,))],
-    )
-    sigma_got, blocks, adjoint_blocks = {}, {0: sends[0]}, {}
+        scratch=[pltpu.SemaphoreType.DMA((chips,))],
+    )
+    sigma_got, blocks, adjoint_blocks = {}, {}, {}
     for step in range(1, chips):
         sigma_got[step] = chip_swap(fetched, step)
-        blocks[step] = chip_swap(sends[step], step)
+        blocks[step] = chip_swap(sends[step - 1], step)
     fetched = [sigma_got[step] for step in range(1, chips)]
+    blocks[0], own, give = call(
+        stage_rest_kernel,
+        [shape(plane_count, CORES, *plane)] + [shape(plane_count, chips, *plane)] * 2,
+        (in_place(warm_forward), in_place(warm_adjoint)),
+        [HBM, HBM],
+        scratch=[pltpu.SemaphoreType.DMA((1 + 2 * chips * plane_count,))],
+    )
     blocks = [blocks[step] for step in range(chips)]
-    own, give = call(
-        stage_adjoint_kernel,
-        [shape(plane_count, chips, *plane)] * 2,
-        (in_place(warm_adjoint),),
-        [HBM],
-        scratch=[pltpu.SemaphoreType.DMA((2 * chips * plane_count,))],
-    )
     got = core_swap(give)
     packed = call(
         pack_kernel, [shape(CORES, plane_count, *plane)] * chips, (own, got), [VMEM, VMEM]

time: 67.4 us -> 65 us (0.964)
  waiting for transfers between devices: 16.4 us -> 13.8 us
    ppermute x25, waiting for transfers between devices: 16.4 us -> 13.8 us  [swap(): return lax.ppermute(values, axis, [(i, i ^ bit) for i in range(size)])]
  transfers between devices with their start and end apart: 25 -> 25, of which waited for: 10 -> 8; matrix products, arithmetic and copies ran while one was open for 1% -> 1% of each run, Pallas kernels for 18% -> 18%
where the time goes in v7:
time: 65 us; the launch traced here: 64.8 us
  starting transfers between devices  30.3 us (47%)
  Pallas kernels  18.3 us (28%)
  waiting for transfers between devices  13.8 us (21%)
  between operations  0.91 us (1%)
  other arithmetic  0.83 us (1%)
    ppermute x25, starting transfers between devices, swap(): return lax.ppermute(values, axis, [(i, i ^ bit) for i in range(size)])  30.3 us
    pallas_call x8, Pallas kernels, call(): pl.pallas_call(body, out_shape=out_shape, in_specs=in_specs, out_specs=[V...  18.3 us
    ppermute x25, waiting for transfers between devices, swap(): return lax.ppermute(values, axis, [(i, i ^ bit) for i in range(size)])  13.8 us
  transfers between devices with their start and end apart: 25, of which 8 were waited for; matrix products, arithmetic and copies ran while one was open for 1% of the time, Pallas kernels for 18%

profile of v7, /device:TPU:0, one launch (start us, length us, event | category | flops | bytes accessed | tf_op | source)
XLA Modules:
  0.0 64.8 jit_solution(7978810346934095314)
XLA Ops:
  0.6 1.2 %shard_map.77 = (f32[1,128,128]{2,1,0:T(8,128)S(1)}, f32[2,2,128,128]{3,2,1,0:T(8,128)S(1)}, f32[2,2,128,128]{3,2,1,0:T(8,128)S(1)}, f32[2,2,128,128]{3,2,1,0:T(8,128)S(1)}) custom-call(f32[2,128,128]{2,1,0:T(8,128)} %conductivity.1, f32[2,8,128,128]{3,2,1,0:T(8,128)} %forward.3), custom_call_target="tpu_custom_call" | custom-call | flops 2031616 | bytes 2031616 | tf_op jit(solution)/shard_map/pallas_call | solution.py:29
  1.8 4.0 %collective-permute-start.2 = (f32[1,128,128]{2,1,0:T(8,128)S(1)}, f32[1,128,128]{2,1,0:T(8,128)S(1)}, u32[]{:S(2)}, u32[]{:S(2)}) collective-permute-start(f32[1,128,128]{2,1,0:T(8,128)S(1)} %get-tuple-element.29), channel_id=1, source_target_pairs={{0,6},{1,7},{2,4},{3,5},{4,2},{5,3},{6,0},{7,1},{8,14},{9,15},{10,... | collective-permute-start | bytes 196616 | tf_op jit(solution)/shard_map/ppermute | solution.py:386
  6.5 1.9 %collective-permute-start.5 = (f32[2,2,128,128]{3,2,1,0:T(8,128)S(1)}, f32[2,2,128,128]{3,2,1,0:T(8,128)S(1)}, u32[]{:S(2)}, u32[]{:S(2)}) collective-permute-start(f32[2,2,128,128]{3,2,1,0:T(8,128)S(1)} %get-tuple-element.36), channel_id=1, source_target_pairs={{0,2},{1,3},{2,0},{3,1},{4,6},{5,7},{6,4},{7,5},{8,10},{9,11},{10,... | collective-permute-start | bytes 786440 | tf_op jit(solution)/shard_map/ppermute | solution.py:386
  8.4 1.5 %collective-permute-start.6 = (f32[2,2,128,128]{3,2,1,0:T(8,128)S(1)}, f32[2,2,128,128]{3,2,1,0:T(8,128)S(1)}, u32[]{:S(2)}, u32[]{:S(2)}) collective-permute-start(f32[2,2,128,128]{3,2,1,0:T(8,128)S(1)} %get-tuple-element.37), channel_id=1, source_target_pairs={{0,4},{1,5},{2,6},{3,7},{4,0},{5,1},{6,2},{7,3},{8,12},{9,13},{10,... | collective-permute-start | bytes 786440 | tf_op jit(solution)/shard_map/ppermute | solution.py:386
  9.9 1.4 %shard_map.79 = (f32[2,2,128,128]{3,2,1,0:T(8,128)S(1)}, f32[2,4,128,128]{3,2,1,0:T(8,128)S(1)}, f32[2,4,128,128]{3,2,1,0:T(8,128)S(1)}) custom-call(f32[2,8,128,128]{3,2,1,0:T(8,128)} %forward.3, f32[2,8,128,128]{3,2,1,0:T(8,128)} %adjoint.1), custom_call_target="tpu_custom_call" | custom-call | flops 3407872 | bytes 3407872 | tf_op jit(solution)/shard_map/pallas_call | solution.py:29
  11.7 1.8 %collective-permute-start.3 = (f32[3,128,128]{2,1,0:T(8,128)S(1)}, f32[3,128,128]{2,1,0:T(8,128)S(1)}, u32[]{:S(2)}, u32[]{:S(2)}) collective-permute-start(f32[3,128,128]{2,1,0:T(8,128)S(1)} %pad_maximum_fusion), channel_id=1, source_target_pairs={{0,8},{8,0},{16,24},{24,16},{1,9},{9,1},{17,25},{25,17},{2,10},{10... | collective-permute-start | bytes 589832 | tf_op jit(solution)/shard_map/ppermute | solution.py:386
  13.6 5.5 %collective-permute-done.3 = f32[3,128,128]{2,1,0:T(8,128)S(1)} collective-permute-done((f32[3,128,128]{2,1,0:T(8,128)S(1)}, f32[3,128,128]{2,1,0:T(8,128)S(1)}, u32[]{:S(2)}, u32[]{:S(2)}) %collective-permute-start.3) | collective-permute-done | bytes 196640 | tf_op jit(solution)/shard_map/ppermute | solution.py:386
  19.2 2.6 %collective-permute-done.7.refs_3_ = f32[2,2,128,128]{3,2,1,0:T(8,128)S(1)} collective-permute-done((f32[2,2,128,128]{3,2,1,0:T(8,128)S(1)}, f32[2,2,128,128]{3,2,1,0:T(8,128)S(1)}, u32[]{:S(2)}, u32[]{:S(2)}) %collective-permute-start.7) | collective-permute-done | bytes 262176 | tf_op jit(solution)/shard_map/ppermute | solution.py:386
  22.1 1.1 %collective-permute-start.10 = (f32[2,2,128,128]{3,2,1,0:T(8,128)S(1)}, f32[2,2,128,128]{3,2,1,0:T(8,128)S(1)}, u32[]{:S(2)}, u32[]{:S(2)}) collective-permute-start(f32[2,2,128,128]{3,2,1,0:T(8,128)S(1)} %get-tuple-element.48), channel_id=1, source_target_pairs={{0,2},{1,3},{2,0},{3,1},{4,6},{5,7},{6,4},{7,5},{8,10},{9,11},{10,... | collective-permute-start | bytes 786440 | tf_op jit(solution)/shard_map/ppermute | solution.py:386
  24.1 1.5 %collective-permute-start.12 = (f32[2,2,128,128]{3,2,1,0:T(8,128)S(1)}, f32[2,2,128,128]{3,2,1,0:T(8,128)S(1)}, u32[]{:S(2)}, u32[]{:S(2)}) collective-permute-start(f32[2,2,128,128]{3,2,1,0:T(8,128)S(1)} %get-tuple-element.50), channel_id=1, source_target_pairs={{0,6},{1,7},{2,4},{3,5},{4,2},{5,3},{6,0},{7,1},{8,14},{9,15},{10,... | collective-permute-start | bytes 786440 | tf_op jit(solution)/shard_map/ppermute | solution.py:386
  25.6 3.7 %shard_map.78 = (f32[2304,128]{1,0:T(8,128)S(1)}, f32[2304,128]{1,0:T(8,128)S(1)}, f32[2304,128]{1,0:T(8,128)S(1)}, f32[2304,128]{1,0:T(8,128)S(1)}, f32[2304,128]{1,0:T(8,128)S(1)}) custom-call(f32[8,128,128]{2,1,0:T(8,128)S(1)} %constant_dynamic-update-slice_fusion.own, f32[8,128,128]{2,1,0:T(8,128)S(1)} %collective-permute-done.4.others), custom_call_target="tpu_custom_call" | custom-call | flops 6946816 | bytes 6946816 | tf_op jit(solution)/shard_map/pallas_call | solution.py:29
  29.4 5.9 %shard_map.81 = (f32[2304,128]{1,0:T(8,128)S(1)}, f32[2304,128]{1,0:T(8,128)S(1)}, f32[2304,128]{1,0:T(8,128)S(1)}, f32[8,128]{1,0:T(8,128)S(1)}) custom-call(s32[128]{0:T(128)S(1)} %copy-done.1, s32[4,8]{1,0:T(4,128)S(1)} %bitcast.24, f32[2304,128]{1,0:T(8,128)S(1)} %get-tuple-element.30.refs_0_, f32[2304,128]{1,0:T(8,128)S(1)} %get-tuple-element.31.refs_1_, ...), custom_call_target="tpu_custom_call" | custom-call | flops 10490496 | bytes 10490496 | tf_op jit(solution)/shard_map/pallas_call | solution.py:29
  35.3 1.9 %collective-permute-done.11.refs_11_ = f32[2,2,128,128]{3,2,1,0:T(8,128)S(1)} collective-permute-done((f32[2,2,128,128]{3,2,1,0:T(8,128)S(1)}, f32[2,2,128,128]{3,2,1,0:T(8,128)S(1)}, u32[]{:S(2)}, u32[]{:S(2)}) %collective-permute-start.11) | collective-permute-done | bytes 262176 | tf_op jit(solution)/shard_map/ppermute | solution.py:386
  37.2 5.2 %shard_map.83 = (f32[2304,128]{1,0:T(8,128)S(1)}, f32[4,128,128]{2,1,0:T(8,128)S(1)}, f32[4,136,128]{2,1,0:T(8,128)S(1)}) custom-call(s32[128]{0:T(128)S(1)} %copy-done.1, s32[4,8]{1,0:T(4,128)S(1)} %bitcast.25, f32[8]{0:T(128)S(1)} %copy-done.2, f32[2304,128]{1,0:T(8,128)S(1)} %get-tuple-element.30.refs_0_, f32[2304,128]{1,0:T(8,128)S(1)} %get-tuple-element.31.refs_1_, ...), custom_call_target="tpu_custom_call" | custom-call | flops 12210848 | bytes 12210848 | tf_op jit(solution)/shard_map/pallas_call | solution.py:29
  44.0 1.0 %collective-permute-start.15 = (f32[128,128]{1,0:T(8,128)S(1)}, f32[128,128]{1,0:T(8,128)S(1)}, u32[]{:S(2)}, u32[]{:S(2)}) collective-permute-start(f32[128,128]{1,0:T(8,128)S(1)} %get-tuple-element.59), channel_id=1, source_target_pairs={{0,4},{1,5},{2,6},{3,7},{4,0},{5,1},{6,2},{7,3},{8,12},{9,13},{10,... | collective-permute-start | bytes 196616 | tf_op jit(solution)/shard_map/ppermute | solution.py:386
  45.0 1.5 %collective-permute-start.16 = (f32[128,128]{1,0:T(8,128)S(1)}, f32[128,128]{1,0:T(8,128)S(1)}, u32[]{:S(2)}, u32[]{:S(2)}) collective-permute-start(f32[128,128]{1,0:T(8,128)S(1)} %get-tuple-element.60), channel_id=1, source_target_pairs={{0,6},{1,7},{2,4},{3,5},{4,2},{5,3},{6,0},{7,1},{8,14},{9,15},{10,... | collective-permute-start | bytes 196616 | tf_op jit(solution)/shard_map/ppermute | solution.py:386
  46.6 1.0 %collective-permute-start.14 = (f32[128,128]{1,0:T(8,128)S(1)}, f32[128,128]{1,0:T(8,128)S(1)}, u32[]{:S(2)}, u32[]{:S(2)}) collective-permute-start(f32[128,128]{1,0:T(8,128)S(1)} %get-tuple-element.61), channel_id=1, source_target_pairs={{0,2},{1,3},{2,0},{3,1},{4,6},{5,7},{6,4},{7,5},{8,10},{9,11},{10,... | collective-permute-start | bytes 196616 | tf_op jit(solution)/shard_map/ppermute | solution.py:386
  48.7 1.5 %collective-permute-start.22 = (f32[136,128]{1,0:T(8,128)S(1)}, f32[136,128]{1,0:T(8,128)S(1)}, u32[]{:S(2)}, u32[]{:S(2)}) collective-permute-start(f32[136,128]{1,0:T(8,128)S(1)} %get-tuple-element.57), channel_id=1, source_target_pairs={{0,6},{1,7},{2,4},{3,5},{4,2},{5,3},{6,0},{7,1},{8,14},{9,15},{10,... | collective-permute-start | bytes 208904 | tf_op jit(solution)/shard_map/ppermute | solution.py:386
  50.2 1.0 %collective-permute-start.20 = (f32[136,128]{1,0:T(8,128)S(1)}, f32[136,128]{1,0:T(8,128)S(1)}, u32[]{:S(2)}, u32[]{:S(2)}) collective-permute-start(f32[136,128]{1,0:T(8,128)S(1)} %get-tuple-element.58), channel_id=1, source_target_pairs={{0,2},{1,3},{2,0},{3,1},{4,6},{5,7},{6,4},{7,5},{8,10},{9,11},{10,... | collective-permute-start | bytes 208904 | tf_op jit(solution)/shard_map/ppermute | solution.py:386
  51.3 1.6 %collective-permute-start.17 = (f32[128,128]{1,0:T(8,128)S(1)}, f32[128,128]{1,0:T(8,128)S(1)}, u32[]{:S(2)}, u32[]{:S(2)}) collective-permute-start(f32[128,128]{1,0:T(8,128)S(1)} %fusion.1), channel_id=1, source_target_pairs={{0,8},{8,0},{16,24},{24,16},{1,9},{9,1},{17,25},{25,17},{2,10},{10... | collective-permute-start | bytes 196616 | tf_op jit(solution)/shard_map/ppermute | solution.py:386
  54.5 1.6 %collective-permute-start.23 = (f32[128,128]{1,0:T(8,128)S(1)}, f32[128,128]{1,0:T(8,128)S(1)}, u32[]{:S(2)}, u32[]{:S(2)}) collective-permute-start(f32[128,128]{1,0:T(8,128)S(1)} %slice.48), channel_id=1, source_target_pairs={{0,8},{8,0},{16,24},{24,16},{1,9},{9,1},{17,25},{25,17},{2,10},{10... | collective-permute-start | bytes 196616 | tf_op jit(solution)/shard_map/ppermute | solution.py:386
  56.2 2.7 %collective-permute-start.18 = (f32[128,128]{1,0:T(8,128)S(1)}, f32[128,128]{1,0:T(8,128)S(1)}, u32[]{:S(2)}, u32[]{:S(2)}) collective-permute-start(f32[128,128]{1,0:T(8,128)S(1)} %add.40), channel_id=1, source_target_pairs={{0,16},{8,24},{16,0},{24,8},{1,17},{9,25},{17,1},{25,9},{2,18},{10... | collective-permute-start | bytes 196616 | tf_op jit(solution)/shard_map/ppermute | solution.py:386
  58.9 2.8 %collective-permute-start.24 = (f32[128,128]{1,0:T(8,128)S(1)}, f32[128,128]{1,0:T(8,128)S(1)}, u32[]{:S(2)}, u32[]{:S(2)}) collective-permute-start(f32[128,128]{1,0:T(8,128)S(1)} %slice_add_fusion), channel_id=1, source_target_pairs={{0,16},{8,24},{16,0},{24,8},{1,17},{9,25},{17,1},{25,9},{2,18},{10... | collective-permute-start | bytes 196616 | tf_op jit(solution)/shard_map/ppermute | solution.py:386
  62.8 1.3 %collective-permute-done.24 = f32[128,128]{1,0:T(8,128)S(1)} collective-permute-done((f32[128,128]{1,0:T(8,128)S(1)}, f32[128,128]{1,0:T(8,128)S(1)}, u32[]{:S(2)}, u32[]{:S(2)}) %collective-permute-start.24) | collective-permute-done | bytes 65568 | tf_op jit(solution)/shard_map/ppermute | solution.py:386
  (61 shorter events, 8.5 us)
Async XLA Ops:
  1.8 9.5 %collective-permute-start.2 = (f32[1,128,128]{2,1,0:T(8,128)S(1)}, f32[1,128,128]{2,1,0:T(8,128)S(1)}, u32[]{:S(2)}, u32[]{:S(2)}) collective-permute-start(f32[1,128,128]{2,1,0:T(8,128)S(1)} %get-tuple-element.29), channel_id=1, source_target_pairs={{0,6},{1,7},{2,4},{3,5},{4,2},{5,3},{6,0},{7,1},{8,14},{9,15},{10,... | collective-permute-start | bytes 196616 | tf_op jit(solution)/shard_map/ppermute | solution.py:386
  5.8 5.9 %collective-permute-start.1 = (f32[1,128,128]{2,1,0:T(8,128)S(1)}, f32[1,128,128]{2,1,0:T(8,128)S(1)}, u32[]{:S(2)}, u32[]{:S(2)}) collective-permute-start(f32[1,128,128]{2,1,0:T(8,128)S(1)} %get-tuple-element.29), channel_id=1, source_target_pairs={{0,4},{1,5},{2,6},{3,7},{4,0},{5,1},{6,2},{7,3},{8,12},{9,13},{10,... | collective-permute-start | bytes 196616 | tf_op jit(solution)/shard_map/ppermute | solution.py:386
  6.3 5.4 %collective-permute-start = (f32[1,128,128]{2,1,0:T(8,128)S(1)}, f32[1,128,128]{2,1,0:T(8,128)S(1)}, u32[]{:S(2)}, u32[]{:S(2)}) collective-permute-start(f32[1,128,128]{2,1,0:T(8,128)S(1)} %get-tuple-element.29), channel_id=1, source_target_pairs={{0,2},{1,3},{2,0},{3,1},{4,6},{5,7},{6,4},{7,5},{8,10},{9,11},{10,... | collective-permute-start | bytes 196616 | tf_op jit(solution)/shard_map/ppermute | solution.py:386
  6.5 12.8 %collective-permute-start.5 = (f32[2,2,128,128]{3,2,1,0:T(8,128)S(1)}, f32[2,2,128,128]{3,2,1,0:T(8,128)S(1)}, u32[]{:S(2)}, u32[]{:S(2)}) collective-permute-start(f32[2,2,128,128]{3,2,1,0:T(8,128)S(1)} %get-tuple-element.36), channel_id=1, source_target_pairs={{0,2},{1,3},{2,0},{3,1},{4,6},{5,7},{6,4},{7,5},{8,10},{9,11},{10,... | collective-permute-start | bytes 786440 | tf_op jit(solution)/shard_map/ppermute | solution.py:386
  8.4 10.9 %collective-permute-start.6 = (f32[2,2,128,128]{3,2,1,0:T(8,128)S(1)}, f32[2,2,128,128]{3,2,1,0:T(8,128)S(1)}, u32[]{:S(2)}, u32[]{:S(2)}) collective-permute-start(f32[2,2,128,128]{3,2,1,0:T(8,128)S(1)} %get-tuple-element.37), channel_id=1, source_target_pairs={{0,4},{1,5},{2,6},{3,7},{4,0},{5,1},{6,2},{7,3},{8,12},{9,13},{10,... | collective-permute-start | bytes 786440 | tf_op jit(solution)/shard_map/ppermute | solution.py:386
  11.3 10.5 %collective-permute-start.7 = (f32[2,2,128,128]{3,2,1,0:T(8,128)S(1)}, f32[2,2,128,128]{3,2,1,0:T(8,128)S(1)}, u32[]{:S(2)}, u32[]{:S(2)}) collective-permute-start(f32[2,2,128,128]{3,2,1,0:T(8,128)S(1)} %get-tuple-element.38), channel_id=1, source_target_pairs={{0,6},{1,7},{2,4},{3,5},{4,2},{5,3},{6,0},{7,1},{8,14},{9,15},{10,... | collective-permute-start | bytes 786440 | tf_op jit(solution)/shard_map/ppermute | solution.py:386
  11.7 10.3 %collective-permute-start.9 = (f32[2,4,128,128]{3,2,1,0:T(8,128)S(1)}, f32[2,4,128,128]{3,2,1,0:T(8,128)S(1)}, u32[]{:S(2)}, u32[]{:S(2)}) collective-permute-start(f32[2,4,128,128]{3,2,1,0:T(8,128)S(1)} %get-tuple-element.46), channel_id=1, source_target_pairs={{0,1},{1,0},{2,3},{3,2},{4,5},{5,4},{6,7},{7,6},{8,9},{9,8},{10,11... | collective-permute-start | bytes 1572872 | tf_op jit(solution)/shard_map/ppermute | solution.py:386
  11.7 7.4 %collective-permute-start.3 = (f32[3,128,128]{2,1,0:T(8,128)S(1)}, f32[3,128,128]{2,1,0:T(8,128)S(1)}, u32[]{:S(2)}, u32[]{:S(2)}) collective-permute-start(f32[3,128,128]{2,1,0:T(8,128)S(1)} %pad_maximum_fusion), channel_id=1, source_target_pairs={{0,8},{8,0},{16,24},{24,16},{1,9},{9,1},{17,25},{25,17},{2,10},{10... | collective-permute-start | bytes 589832 | tf_op jit(solution)/shard_map/ppermute | solution.py:386
  19.1 6.5 %collective-permute-start.4 = (f32[8,128,128]{2,1,0:T(8,128)S(1)}, f32[8,128,128]{2,1,0:T(8,128)S(1)}, u32[]{:S(2)}, u32[]{:S(2)}) collective-permute-start(f32[8,128,128]{2,1,0:T(8,128)S(1)} %constant_dynamic-update-slice_fusion.own), channel_id=1, source_target_pairs={{0,1},{1,0},{2,3},{3,2},{4,5},{5,4},{6,7},{7,6},{8,9},{9,8},{10,11... | collective-permute-start | bytes 1572872 | tf_op jit(solution)/shard_map/ppermute | solution.py:386
  21.9 7.4 %collective-permute-start.8 = (f32[4,2,128,128]{3,2,1,0:T(8,128)S(1)}, f32[4,2,128,128]{3,2,1,0:T(8,128)S(1)}, u32[]{:S(2)}, u32[]{:S(2)}) collective-permute-start(f32[4,2,128,128]{3,2,1,0:T(8,128)S(1)} %get-tuple-element.40), channel_id=1, source_target_pairs={{0,1},{1,0},{2,3},{3,2},{4,5},{5,4},{6,7},{7,6},{8,9},{9,8},{10,11... | collective-permute-start | bytes 1572872 | tf_op jit(solution)/shard_map/ppermute | solution.py:386
  22.1 13.2 %collective-permute-start.10 = (f32[2,2,128,128]{3,2,1,0:T(8,128)S(1)}, f32[2,2,128,128]{3,2,1,0:T(8,128)S(1)}, u32[]{:S(2)}, u32[]{:S(2)}) collective-permute-start(f32[2,2,128,128]{3,2,1,0:T(8,128)S(1)} %get-tuple-element.48), channel_id=1, source_target_pairs={{0,2},{1,3},{2,0},{3,1},{4,6},{5,7},{6,4},{7,5},{8,10},{9,11},{10,... | collective-permute-start | bytes 786440 | tf_op jit(solution)/shard_map/ppermute | solution.py:386
  23.2 14.0 %collective-permute-start.11 = (f32[2,2,128,128]{3,2,1,0:T(8,128)S(1)}, f32[2,2,128,128]{3,2,1,0:T(8,128)S(1)}, u32[]{:S(2)}, u32[]{:S(2)}) collective-permute-start(f32[2,2,128,128]{3,2,1,0:T(8,128)S(1)} %get-tuple-element.49), channel_id=1, source_target_pairs={{0,4},{1,5},{2,6},{3,7},{4,0},{5,1},{6,2},{7,3},{8,12},{9,13},{10,... | collective-permute-start | bytes 786440 | tf_op jit(solution)/shard_map/ppermute | solution.py:386
  24.1 13.1 %collective-permute-start.12 = (f32[2,2,128,128]{3,2,1,0:T(8,128)S(1)}, f32[2,2,128,128]{3,2,1,0:T(8,128)S(1)}, u32[]{:S(2)}, u32[]{:S(2)}) collective-permute-start(f32[2,2,128,128]{3,2,1,0:T(8,128)S(1)} %get-tuple-element.50), channel_id=1, source_target_pairs={{0,6},{1,7},{2,4},{3,5},{4,2},{5,3},{6,0},{7,1},{8,14},{9,15},{10,... | collective-permute-start | bytes 786440 | tf_op jit(solution)/shard_map/ppermute | solution.py:386
  42.5 5.1 %collective-permute-start.19 = (f32[4,136,128]{2,1,0:T(8,128)S(1)}, f32[4,136,128]{2,1,0:T(8,128)S(1)}, u32[]{:S(2)}, u32[]{:S(2)}) collective-permute-start(f32[4,136,128]{2,1,0:T(8,128)S(1)} %get-tuple-element.55), channel_id=1, source_target_pairs={{0,1},{1,0},{2,3},{3,2},{4,5},{5,4},{6,7},{7,6},{8,9},{9,8},{10,11... | collective-permute-start | bytes 835592 | tf_op jit(solution)/shard_map/ppermute | solution.py:386
  44.0 6.1 %collective-permute-start.15 = (f32[128,128]{1,0:T(8,128)S(1)}, f32[128,128]{1,0:T(8,128)S(1)}, u32[]{:S(2)}, u32[]{:S(2)}) collective-permute-start(f32[128,128]{1,0:T(8,128)S(1)} %get-tuple-element.59), channel_id=1, source_target_pairs={{0,4},{1,5},{2,6},{3,7},{4,0},{5,1},{6,2},{7,3},{8,12},{9,13},{10,... | collective-permute-start | bytes 196616 | tf_op jit(solution)/shard_map/ppermute | solution.py:386
  45.0 6.2 %collective-permute-start.16 = (f32[128,128]{1,0:T(8,128)S(1)}, f32[128,128]{1,0:T(8,128)S(1)}, u32[]{:S(2)}, u32[]{:S(2)}) collective-permute-start(f32[128,128]{1,0:T(8,128)S(1)} %get-tuple-element.60), channel_id=1, source_target_pairs={{0,6},{1,7},{2,4},{3,5},{4,2},{5,3},{6,0},{7,1},{8,14},{9,15},{10,... | collective-permute-start | bytes 196616 | tf_op jit(solution)/shard_map/ppermute | solution.py:386
  46.6 4.7 %collective-permute-start.14 = (f32[128,128]{1,0:T(8,128)S(1)}, f32[128,128]{1,0:T(8,128)S(1)}, u32[]{:S(2)}, u32[]{:S(2)}) collective-permute-start(f32[128,128]{1,0:T(8,128)S(1)} %get-tuple-element.61), channel_id=1, source_target_pairs={{0,2},{1,3},{2,0},{3,1},{4,6},{5,7},{6,4},{7,5},{8,10},{9,11},{10,... | collective-permute-start | bytes 196616 | tf_op jit(solution)/shard_map/ppermute | solution.py:386
  47.7 5.2 %collective-permute-start.21 = (f32[136,128]{1,0:T(8,128)S(1)}, f32[136,128]{1,0:T(8,128)S(1)}, u32[]{:S(2)}, u32[]{:S(2)}) collective-permute-start(f32[136,128]{1,0:T(8,128)S(1)} %get-tuple-element.56), channel_id=1, source_target_pairs={{0,4},{1,5},{2,6},{3,7},{4,0},{5,1},{6,2},{7,3},{8,12},{9,13},{10,... | collective-permute-start | bytes 208904 | tf_op jit(solution)/shard_map/ppermute | solution.py:386
  48.7 5.2 %collective-permute-start.22 = (f32[136,128]{1,0:T(8,128)S(1)}, f32[136,128]{1,0:T(8,128)S(1)}, u32[]{:S(2)}, u32[]{:S(2)}) collective-permute-start(f32[136,128]{1,0:T(8,128)S(1)} %get-tuple-element.57), channel_id=1, source_target_pairs={{0,6},{1,7},{2,4},{3,5},{4,2},{5,3},{6,0},{7,1},{8,14},{9,15},{10,... | collective-permute-start | bytes 208904 | tf_op jit(solution)/shard_map/ppermute | solution.py:386
  50.2 4.3 %collective-permute-start.20 = (f32[136,128]{1,0:T(8,128)S(1)}, f32[136,128]{1,0:T(8,128)S(1)}, u32[]{:S(2)}, u32[]{:S(2)}) collective-permute-start(f32[136,128]{1,0:T(8,128)S(1)} %get-tuple-element.58), channel_id=1, source_target_pairs={{0,2},{1,3},{2,0},{3,1},{4,6},{5,7},{6,4},{7,5},{8,10},{9,11},{10,... | collective-permute-start | bytes 208904 | tf_op jit(solution)/shard_map/ppermute | solution.py:386
  51.3 4.9 %collective-permute-start.17 = (f32[128,128]{1,0:T(8,128)S(1)}, f32[128,128]{1,0:T(8,128)S(1)}, u32[]{:S(2)}, u32[]{:S(2)}) collective-permute-start(f32[128,128]{1,0:T(8,128)S(1)} %fusion.1), channel_id=1, source_target_pairs={{0,8},{8,0},{16,24},{24,16},{1,9},{9,1},{17,25},{25,17},{2,10},{10... | collective-permute-start | bytes 196616 | tf_op jit(solution)/shard_map/ppermute | solution.py:386
  54.5 4.3 %collective-permute-start.23 = (f32[128,128]{1,0:T(8,128)S(1)}, f32[128,128]{1,0:T(8,128)S(1)}, u32[]{:S(2)}, u32[]{:S(2)}) collective-permute-start(f32[128,128]{1,0:T(8,128)S(1)} %slice.48), channel_id=1, source_target_pairs={{0,8},{8,0},{16,24},{24,16},{1,9},{9,1},{17,25},{25,17},{2,10},{10... | collective-permute-start | bytes 196616 | tf_op jit(solution)/shard_map/ppermute | solution.py:386
  56.2 6.6 %collective-permute-start.18 = (f32[128,128]{1,0:T(8,128)S(1)}, f32[128,128]{1,0:T(8,128)S(1)}, u32[]{:S(2)}, u32[]{:S(2)}) collective-permute-start(f32[128,128]{1,0:T(8,128)S(1)} %add.40), channel_id=1, source_target_pairs={{0,16},{8,24},{16,0},{24,8},{1,17},{9,25},{17,1},{25,9},{2,18},{10... | collective-permute-start | bytes 196616 | tf_op jit(solution)/shard_map/ppermute | solution.py:386
  58.9 5.2 %collective-permute-start.24 = (f32[128,128]{1,0:T(8,128)S(1)}, f32[128,128]{1,0:T(8,128)S(1)}, u32[]{:S(2)}, u32[]{:S(2)}) collective-permute-start(f32[128,128]{1,0:T(8,128)S(1)} %slice_add_fusion), channel_id=1, source_target_pairs={{0,16},{8,24},{16,0},{24,8},{1,17},{9,25},{17,1},{25,9},{2,18},{10... | collective-permute-start | bytes 196616 | tf_op jit(solution)/shard_map/ppermute | solution.py:386
  (5 other events, 33.9 us)

commit v8 on v7

--- a/solution.py
+++ b/solution.py
@@ -241,7 +241,7 @@
         at(applied, value=product)
         return squares + fold(here * here), products + fold(here * product)
 
-    squares, products = each_chunk(size, height, second, (nothing, nothing))
+    squares, products = each_chunk(size, height, second, (nothing, nothing), 2 * ROWS)
     current, energy = total(squares), total(products)
     step_size = current / energy
 
@@ -259,7 +259,7 @@
         products = products + fold(here * at(applied))
         return squares, products, energies + fold(here * (here - 2.0 * sums))
 
-    squares, products, energies = each_chunk(size, height, third, (nothing,) * 3)
+    squares, products, energies = each_chunk(size, height, third, (nothing,) * 3, 2 * ROWS)
     following, cross, own = total(squares), total(products), total(energies)
     ratio = following / current
     last_size = following / (own + ratio * (2.0 * cross + ratio * energy))
@@ -270,7 +270,7 @@
         end(at, at(scale) * moved)
         return carry
 
-    each_chunk(size, height, fifth, 0)
+    each_chunk(size, height, fifth, 0, 2 * ROWS)
 
 
 def electrode(place, electrodes, patterns, which):

time: 65 us -> 64.5 us (level)
  Pallas kernels: 18.3 us -> 17.3 us
    pallas_call x8, Pallas kernels: 18.3 us -> 17.3 us  [call(): pl.pallas_call(body, out_shape=out_shape, in_specs=in_specs, out_specs=[V...]
where the time goes in v8:
time: 64.5 us; the launch traced here: 64.3 us
  starting transfers between devices  30.3 us (47%)
  Pallas kernels  17.3 us (27%)
  waiting for transfers between devices  14.3 us (22%)
  between operations  0.91 us (1%)
  other arithmetic  0.83 us (1%)
    ppermute x25, starting transfers between devices, swap(): return lax.ppermute(values, axis, [(i, i ^ bit) for i in range(size)])  30.3 us
    pallas_call x8, Pallas kernels, call(): pl.pallas_call(body, out_shape=out_shape, in_specs=in_specs, out_specs=[V...  17.3 us
    ppermute x25, waiting for transfers between devices, swap(): return lax.ppermute(values, axis, [(i, i ^ bit) for i in range(size)])  14.3 us
  transfers between devices with their start and end apart: 25, of which 8 were waited for; matrix products, arithmetic and copies ran while one was open for 1% of the time, Pallas kernels for 18%

profile of v8, /device:TPU:0, one launch (start us, length us, event | category | flops | bytes accessed | tf_op | source)
XLA Modules:
  0.0 64.3 jit_solution(2080438102702426586)
XLA Ops:
  0.6 1.2 %shard_map.77 = (f32[1,128,128]{2,1,0:T(8,128)S(1)}, f32[2,2,128,128]{3,2,1,0:T(8,128)S(1)}, f32[2,2,128,128]{3,2,1,0:T(8,128)S(1)}, f32[2,2,128,128]{3,2,1,0:T(8,128)S(1)}) custom-call(f32[2,128,128]{2,1,0:T(8,128)} %conductivity.1, f32[2,8,128,128]{3,2,1,0:T(8,128)} %forward.3), custom_call_target="tpu_custom_call" | custom-call | flops 2031616 | bytes 2031616 | tf_op jit(solution)/shard_map/pallas_call | solution.py:29
  1.8 4.0 %collective-permute-start.2 = (f32[1,128,128]{2,1,0:T(8,128)S(1)}, f32[1,128,128]{2,1,0:T(8,128)S(1)}, u32[]{:S(2)}, u32[]{:S(2)}) collective-permute-start(f32[1,128,128]{2,1,0:T(8,128)S(1)} %get-tuple-element.29), channel_id=1, source_target_pairs={{0,6},{1,7},{2,4},{3,5},{4,2},{5,3},{6,0},{7,1},{8,14},{9,15},{10,... | collective-permute-start | bytes 196616 | tf_op jit(solution)/shard_map/ppermute | solution.py:386
  6.5 1.9 %collective-permute-start.5 = (f32[2,2,128,128]{3,2,1,0:T(8,128)S(1)}, f32[2,2,128,128]{3,2,1,0:T(8,128)S(1)}, u32[]{:S(2)}, u32[]{:S(2)}) collective-permute-start(f32[2,2,128,128]{3,2,1,0:T(8,128)S(1)} %get-tuple-element.36), channel_id=1, source_target_pairs={{0,2},{1,3},{2,0},{3,1},{4,6},{5,7},{6,4},{7,5},{8,10},{9,11},{10,... | collective-permute-start | bytes 786440 | tf_op jit(solution)/shard_map/ppermute | solution.py:386
  8.4 1.5 %collective-permute-start.6 = (f32[2,2,128,128]{3,2,1,0:T(8,128)S(1)}, f32[2,2,128,128]{3,2,1,0:T(8,128)S(1)}, u32[]{:S(2)}, u32[]{:S(2)}) collective-permute-start(f32[2,2,128,128]{3,2,1,0:T(8,128)S(1)} %get-tuple-element.37), channel_id=1, source_target_pairs={{0,4},{1,5},{2,6},{3,7},{4,0},{5,1},{6,2},{7,3},{8,12},{9,13},{10,... | collective-permute-start | bytes 786440 | tf_op jit(solution)/shard_map/ppermute | solution.py:386
  9.9 1.4 %shard_map.79 = (f32[2,2,128,128]{3,2,1,0:T(8,128)S(1)}, f32[2,4,128,128]{3,2,1,0:T(8,128)S(1)}, f32[2,4,128,128]{3,2,1,0:T(8,128)S(1)}) custom-call(f32[2,8,128,128]{3,2,1,0:T(8,128)} %forward.3, f32[2,8,128,128]{3,2,1,0:T(8,128)} %adjoint.1), custom_call_target="tpu_custom_call" | custom-call | flops 3407872 | bytes 3407872 | tf_op jit(solution)/shard_map/pallas_call | solution.py:29
  11.7 1.8 %collective-permute-start.3 = (f32[3,128,128]{2,1,0:T(8,128)S(1)}, f32[3,128,128]{2,1,0:T(8,128)S(1)}, u32[]{:S(2)}, u32[]{:S(2)}) collective-permute-start(f32[3,128,128]{2,1,0:T(8,128)S(1)} %pad_maximum_fusion), channel_id=1, source_target_pairs={{0,8},{8,0},{16,24},{24,16},{1,9},{9,1},{17,25},{25,17},{2,10},{10... | collective-permute-start | bytes 589832 | tf_op jit(solution)/shard_map/ppermute | solution.py:386
  13.6 5.5 %collective-permute-done.3 = f32[3,128,128]{2,1,0:T(8,128)S(1)} collective-permute-done((f32[3,128,128]{2,1,0:T(8,128)S(1)}, f32[3,128,128]{2,1,0:T(8,128)S(1)}, u32[]{:S(2)}, u32[]{:S(2)}) %collective-permute-start.3) | collective-permute-done | bytes 196640 | tf_op jit(solution)/shard_map/ppermute | solution.py:386
  19.2 2.6 %collective-permute-done.7.refs_3_ = f32[2,2,128,128]{3,2,1,0:T(8,128)S(1)} collective-permute-done((f32[2,2,128,128]{3,2,1,0:T(8,128)S(1)}, f32[2,2,128,128]{3,2,1,0:T(8,128)S(1)}, u32[]{:S(2)}, u32[]{:S(2)}) %collective-permute-start.7) | collective-permute-done | bytes 262176 | tf_op jit(solution)/shard_map/ppermute | solution.py:386
  22.1 1.1 %collective-permute-start.10 = (f32[2,2,128,128]{3,2,1,0:T(8,128)S(1)}, f32[2,2,128,128]{3,2,1,0:T(8,128)S(1)}, u32[]{:S(2)}, u32[]{:S(2)}) collective-permute-start(f32[2,2,128,128]{3,2,1,0:T(8,128)S(1)} %get-tuple-element.48), channel_id=1, source_target_pairs={{0,2},{1,3},{2,0},{3,1},{4,6},{5,7},{6,4},{7,5},{8,10},{9,11},{10,... | collective-permute-start | bytes 786440 | tf_op jit(solution)/shard_map/ppermute | solution.py:386
  24.1 1.5 %collective-permute-start.12 = (f32[2,2,128,128]{3,2,1,0:T(8,128)S(1)}, f32[2,2,128,128]{3,2,1,0:T(8,128)S(1)}, u32[]{:S(2)}, u32[]{:S(2)}) collective-permute-start(f32[2,2,128,128]{3,2,1,0:T(8,128)S(1)} %get-tuple-element.50), channel_id=1, source_target_pairs={{0,6},{1,7},{2,4},{3,5},{4,2},{5,3},{6,0},{7,1},{8,14},{9,15},{10,... | collective-permute-start | bytes 786440 | tf_op jit(solution)/shard_map/ppermute | solution.py:386
  25.6 3.7 %shard_map.78 = (f32[2304,128]{1,0:T(8,128)S(1)}, f32[2304,128]{1,0:T(8,128)S(1)}, f32[2304,128]{1,0:T(8,128)S(1)}, f32[2304,128]{1,0:T(8,128)S(1)}, f32[2304,128]{1,0:T(8,128)S(1)}) custom-call(f32[8,128,128]{2,1,0:T(8,128)S(1)} %constant_dynamic-update-slice_fusion.own, f32[8,128,128]{2,1,0:T(8,128)S(1)} %collective-permute-done.4.others), custom_call_target="tpu_custom_call" | custom-call | flops 6946816 | bytes 6946816 | tf_op jit(solution)/shard_map/pallas_call | solution.py:29
  29.4 5.4 %shard_map.81 = (f32[2304,128]{1,0:T(8,128)S(1)}, f32[2304,128]{1,0:T(8,128)S(1)}, f32[2304,128]{1,0:T(8,128)S(1)}, f32[8,128]{1,0:T(8,128)S(1)}) custom-call(s32[128]{0:T(128)S(1)} %copy-done.1, s32[4,8]{1,0:T(4,128)S(1)} %bitcast.24, f32[2304,128]{1,0:T(8,128)S(1)} %get-tuple-element.30.refs_0_, f32[2304,128]{1,0:T(8,128)S(1)} %get-tuple-element.31.refs_1_, ...), custom_call_target="tpu_custom_call" | custom-call | flops 10490496 | bytes 10490496 | tf_op jit(solution)/shard_map/pallas_call | solution.py:29
  34.8 2.4 %collective-permute-done.11.refs_11_ = f32[2,2,128,128]{3,2,1,0:T(8,128)S(1)} collective-permute-done((f32[2,2,128,128]{3,2,1,0:T(8,128)S(1)}, f32[2,2,128,128]{3,2,1,0:T(8,128)S(1)}, u32[]{:S(2)}, u32[]{:S(2)}) %collective-permute-start.11) | collective-permute-done | bytes 262176 | tf_op jit(solution)/shard_map/ppermute | solution.py:386
  37.2 4.7 %shard_map.83 = (f32[2304,128]{1,0:T(8,128)S(1)}, f32[4,128,128]{2,1,0:T(8,128)S(1)}, f32[4,136,128]{2,1,0:T(8,128)S(1)}) custom-call(s32[128]{0:T(128)S(1)} %copy-done.1, s32[4,8]{1,0:T(4,128)S(1)} %bitcast.25, f32[8]{0:T(128)S(1)} %copy-done.2, f32[2304,128]{1,0:T(8,128)S(1)} %get-tuple-element.30.refs_0_, f32[2304,128]{1,0:T(8,128)S(1)} %get-tuple-element.31.refs_1_, ...), custom_call_target="tpu_custom_call" | custom-call | flops 12210848 | bytes 12210848 | tf_op jit(solution)/shard_map/pallas_call | solution.py:29
  43.6 1.0 %collective-permute-start.15 = (f32[128,128]{1,0:T(8,128)S(1)}, f32[128,128]{1,0:T(8,128)S(1)}, u32[]{:S(2)}, u32[]{:S(2)}) collective-permute-start(f32[128,128]{1,0:T(8,128)S(1)} %get-tuple-element.59), channel_id=1, source_target_pairs={{0,4},{1,5},{2,6},{3,7},{4,0},{5,1},{6,2},{7,3},{8,12},{9,13},{10,... | collective-permute-start | bytes 196616 | tf_op jit(solution)/shard_map/ppermute | solution.py:386
  44.5 1.5 %collective-permute-start.16 = (f32[128,128]{1,0:T(8,128)S(1)}, f32[128,128]{1,0:T(8,128)S(1)}, u32[]{:S(2)}, u32[]{:S(2)}) collective-permute-start(f32[128,128]{1,0:T(8,128)S(1)} %get-tuple-element.60), channel_id=1, source_target_pairs={{0,6},{1,7},{2,4},{3,5},{4,2},{5,3},{6,0},{7,1},{8,14},{9,15},{10,... | collective-permute-start | bytes 196616 | tf_op jit(solution)/shard_map/ppermute | solution.py:386
  46.1 1.0 %collective-permute-start.14 = (f32[128,128]{1,0:T(8,128)S(1)}, f32[128,128]{1,0:T(8,128)S(1)}, u32[]{:S(2)}, u32[]{:S(2)}) collective-permute-start(f32[128,128]{1,0:T(8,128)S(1)} %get-tuple-element.61), channel_id=1, source_target_pairs={{0,2},{1,3},{2,0},{3,1},{4,6},{5,7},{6,4},{7,5},{8,10},{9,11},{10,... | collective-permute-start | bytes 196616 | tf_op jit(solution)/shard_map/ppermute | solution.py:386
  48.2 1.5 %collective-permute-start.22 = (f32[136,128]{1,0:T(8,128)S(1)}, f32[136,128]{1,0:T(8,128)S(1)}, u32[]{:S(2)}, u32[]{:S(2)}) collective-permute-start(f32[136,128]{1,0:T(8,128)S(1)} %get-tuple-element.57), channel_id=1, source_target_pairs={{0,6},{1,7},{2,4},{3,5},{4,2},{5,3},{6,0},{7,1},{8,14},{9,15},{10,... | collective-permute-start | bytes 208904 | tf_op jit(solution)/shard_map/ppermute | solution.py:386
  49.7 1.0 %collective-permute-start.20 = (f32[136,128]{1,0:T(8,128)S(1)}, f32[136,128]{1,0:T(8,128)S(1)}, u32[]{:S(2)}, u32[]{:S(2)}) collective-permute-start(f32[136,128]{1,0:T(8,128)S(1)} %get-tuple-element.58), channel_id=1, source_target_pairs={{0,2},{1,3},{2,0},{3,1},{4,6},{5,7},{6,4},{7,5},{8,10},{9,11},{10,... | collective-permute-start | bytes 208904 | tf_op jit(solution)/shard_map/ppermute | solution.py:386
  50.8 1.6 %collective-permute-start.17 = (f32[128,128]{1,0:T(8,128)S(1)}, f32[128,128]{1,0:T(8,128)S(1)}, u32[]{:S(2)}, u32[]{:S(2)}) collective-permute-start(f32[128,128]{1,0:T(8,128)S(1)} %fusion.1), channel_id=1, source_target_pairs={{0,8},{8,0},{16,24},{24,16},{1,9},{9,1},{17,25},{25,17},{2,10},{10... | collective-permute-start | bytes 196616 | tf_op jit(solution)/shard_map/ppermute | solution.py:386
  54.0 1.6 %collective-permute-start.23 = (f32[128,128]{1,0:T(8,128)S(1)}, f32[128,128]{1,0:T(8,128)S(1)}, u32[]{:S(2)}, u32[]{:S(2)}) collective-permute-start(f32[128,128]{1,0:T(8,128)S(1)} %slice.48), channel_id=1, source_target_pairs={{0,8},{8,0},{16,24},{24,16},{1,9},{9,1},{17,25},{25,17},{2,10},{10... | collective-permute-start | bytes 196616 | tf_op jit(solution)/shard_map/ppermute | solution.py:386
  55.7 2.7 %collective-permute-start.18 = (f32[128,128]{1,0:T(8,128)S(1)}, f32[128,128]{1,0:T(8,128)S(1)}, u32[]{:S(2)}, u32[]{:S(2)}) collective-permute-start(f32[128,128]{1,0:T(8,128)S(1)} %add.40), channel_id=1, source_target_pairs={{0,16},{8,24},{16,0},{24,8},{1,17},{9,25},{17,1},{25,9},{2,18},{10... | collective-permute-start | bytes 196616 | tf_op jit(solution)/shard_map/ppermute | solution.py:386
  58.4 2.8 %collective-permute-start.24 = (f32[128,128]{1,0:T(8,128)S(1)}, f32[128,128]{1,0:T(8,128)S(1)}, u32[]{:S(2)}, u32[]{:S(2)}) collective-permute-start(f32[128,128]{1,0:T(8,128)S(1)} %slice_add_fusion), channel_id=1, source_target_pairs={{0,16},{8,24},{16,0},{24,8},{1,17},{9,25},{17,1},{25,9},{2,18},{10... | collective-permute-start | bytes 196616 | tf_op jit(solution)/shard_map/ppermute | solution.py:386
  62.3 1.3 %collective-permute-done.24 = f32[128,128]{1,0:T(8,128)S(1)} collective-permute-done((f32[128,128]{1,0:T(8,128)S(1)}, f32[128,128]{1,0:T(8,128)S(1)}, u32[]{:S(2)}, u32[]{:S(2)}) %collective-permute-start.24) | collective-permute-done | bytes 65568 | tf_op jit(solution)/shard_map/ppermute | solution.py:386
  (61 shorter events, 8.5 us)
Async XLA Ops:
  1.8 9.5 %collective-permute-start.2 = (f32[1,128,128]{2,1,0:T(8,128)S(1)}, f32[1,128,128]{2,1,0:T(8,128)S(1)}, u32[]{:S(2)}, u32[]{:S(2)}) collective-permute-start(f32[1,128,128]{2,1,0:T(8,128)S(1)} %get-tuple-element.29), channel_id=1, source_target_pairs={{0,6},{1,7},{2,4},{3,5},{4,2},{5,3},{6,0},{7,1},{8,14},{9,15},{10,... | collective-permute-start | bytes 196616 | tf_op jit(solution)/shard_map/ppermute | solution.py:386
  5.8 5.9 %collective-permute-start.1 = (f32[1,128,128]{2,1,0:T(8,128)S(1)}, f32[1,128,128]{2,1,0:T(8,128)S(1)}, u32[]{:S(2)}, u32[]{:S(2)}) collective-permute-start(f32[1,128,128]{2,1,0:T(8,128)S(1)} %get-tuple-element.29), channel_id=1, source_target_pairs={{0,4},{1,5},{2,6},{3,7},{4,0},{5,1},{6,2},{7,3},{8,12},{9,13},{10,... | collective-permute-start | bytes 196616 | tf_op jit(solution)/shard_map/ppermute | solution.py:386
  6.3 5.4 %collective-permute-start = (f32[1,128,128]{2,1,0:T(8,128)S(1)}, f32[1,128,128]{2,1,0:T(8,128)S(1)}, u32[]{:S(2)}, u32[]{:S(2)}) collective-permute-start(f32[1,128,128]{2,1,0:T(8,128)S(1)} %get-tuple-element.29), channel_id=1, source_target_pairs={{0,2},{1,3},{2,0},{3,1},{4,6},{5,7},{6,4},{7,5},{8,10},{9,11},{10,... | collective-permute-start | bytes 196616 | tf_op jit(solution)/shard_map/ppermute | solution.py:386
  6.5 12.8 %collective-permute-start.5 = (f32[2,2,128,128]{3,2,1,0:T(8,128)S(1)}, f32[2,2,128,128]{3,2,1,0:T(8,128)S(1)}, u32[]{:S(2)}, u32[]{:S(2)}) collective-permute-start(f32[2,2,128,128]{3,2,1,0:T(8,128)S(1)} %get-tuple-element.36), channel_id=1, source_target_pairs={{0,2},{1,3},{2,0},{3,1},{4,6},{5,7},{6,4},{7,5},{8,10},{9,11},{10,... | collective-permute-start | bytes 786440 | tf_op jit(solution)/shard_map/ppermute | solution.py:386
  8.4 10.9 %collective-permute-start.6 = (f32[2,2,128,128]{3,2,1,0:T(8,128)S(1)}, f32[2,2,128,128]{3,2,1,0:T(8,128)S(1)}, u32[]{:S(2)}, u32[]{:S(2)}) collective-permute-start(f32[2,2,128,128]{3,2,1,0:T(8,128)S(1)} %get-tuple-element.37), channel_id=1, source_target_pairs={{0,4},{1,5},{2,6},{3,7},{4,0},{5,1},{6,2},{7,3},{8,12},{9,13},{10,... | collective-permute-start | bytes 786440 | tf_op jit(solution)/shard_map/ppermute | solution.py:386
  11.3 10.5 %collective-permute-start.7 = (f32[2,2,128,128]{3,2,1,0:T(8,128)S(1)}, f32[2,2,128,128]{3,2,1,0:T(8,128)S(1)}, u32[]{:S(2)}, u32[]{:S(2)}) collective-permute-start(f32[2,2,128,128]{3,2,1,0:T(8,128)S(1)} %get-tuple-element.38), channel_id=1, source_target_pairs={{0,6},{1,7},{2,4},{3,5},{4,2},{5,3},{6,0},{7,1},{8,14},{9,15},{10,... | collective-permute-start | bytes 786440 | tf_op jit(solution)/shard_map/ppermute | solution.py:386
  11.7 10.3 %collective-permute-start.9 = (f32[2,4,128,128]{3,2,1,0:T(8,128)S(1)}, f32[2,4,128,128]{3,2,1,0:T(8,128)S(1)}, u32[]{:S(2)}, u32[]{:S(2)}) collective-permute-start(f32[2,4,128,128]{3,2,1,0:T(8,128)S(1)} %get-tuple-element.46), channel_id=1, source_target_pairs={{0,1},{1,0},{2,3},{3,2},{4,5},{5,4},{6,7},{7,6},{8,9},{9,8},{10,11... | collective-permute-start | bytes 1572872 | tf_op jit(solution)/shard_map/ppermute | solution.py:386
  11.7 7.4 %collective-permute-start.3 = (f32[3,128,128]{2,1,0:T(8,128)S(1)}, f32[3,128,128]{2,1,0:T(8,128)S(1)}, u32[]{:S(2)}, u32[]{:S(2)}) collective-permute-start(f32[3,128,128]{2,1,0:T(8,128)S(1)} %pad_maximum_fusion), channel_id=1, source_target_pairs={{0,8},{8,0},{16,24},{24,16},{1,9},{9,1},{17,25},{25,17},{2,10},{10... | collective-permute-start | bytes 589832 | tf_op jit(solution)/shard_map/ppermute | solution.py:386
  19.1 6.5 %collective-permute-start.4 = (f32[8,128,128]{2,1,0:T(8,128)S(1)}, f32[8,128,128]{2,1,0:T(8,128)S(1)}, u32[]{:S(2)}, u32[]{:S(2)}) collective-permute-start(f32[8,128,128]{2,1,0:T(8,128)S(1)} %constant_dynamic-update-slice_fusion.own), channel_id=1, source_target_pairs={{0,1},{1,0},{2,3},{3,2},{4,5},{5,4},{6,7},{7,6},{8,9},{9,8},{10,11... | collective-permute-start | bytes 1572872 | tf_op jit(solution)/shard_map/ppermute | solution.py:386
  21.9 7.4 %collective-permute-start.8 = (f32[4,2,128,128]{3,2,1,0:T(8,128)S(1)}, f32[4,2,128,128]{3,2,1,0:T(8,128)S(1)}, u32[]{:S(2)}, u32[]{:S(2)}) collective-permute-start(f32[4,2,128,128]{3,2,1,0:T(8,128)S(1)} %get-tuple-element.40), channel_id=1, source_target_pairs={{0,1},{1,0},{2,3},{3,2},{4,5},{5,4},{6,7},{7,6},{8,9},{9,8},{10,11... | collective-permute-start | bytes 1572872 | tf_op jit(solution)/shard_map/ppermute | solution.py:386
  22.1 12.7 %collective-permute-start.10 = (f32[2,2,128,128]{3,2,1,0:T(8,128)S(1)}, f32[2,2,128,128]{3,2,1,0:T(8,128)S(1)}, u32[]{:S(2)}, u32[]{:S(2)}) collective-permute-start(f32[2,2,128,128]{3,2,1,0:T(8,128)S(1)} %get-tuple-element.48), channel_id=1, source_target_pairs={{0,2},{1,3},{2,0},{3,1},{4,6},{5,7},{6,4},{7,5},{8,10},{9,11},{10,... | collective-permute-start | bytes 786440 | tf_op jit(solution)/shard_map/ppermute | solution.py:386
  23.2 14.0 %collective-permute-start.11 = (f32[2,2,128,128]{3,2,1,0:T(8,128)S(1)}, f32[2,2,128,128]{3,2,1,0:T(8,128)S(1)}, u32[]{:S(2)}, u32[]{:S(2)}) collective-permute-start(f32[2,2,128,128]{3,2,1,0:T(8,128)S(1)} %get-tuple-element.49), channel_id=1, source_target_pairs={{0,4},{1,5},{2,6},{3,7},{4,0},{5,1},{6,2},{7,3},{8,12},{9,13},{10,... | collective-permute-start | bytes 786440 | tf_op jit(solution)/shard_map/ppermute | solution.py:386
  24.1 13.1 %collective-permute-start.12 = (f32[2,2,128,128]{3,2,1,0:T(8,128)S(1)}, f32[2,2,128,128]{3,2,1,0:T(8,128)S(1)}, u32[]{:S(2)}, u32[]{:S(2)}) collective-permute-start(f32[2,2,128,128]{3,2,1,0:T(8,128)S(1)} %get-tuple-element.50), channel_id=1, source_target_pairs={{0,6},{1,7},{2,4},{3,5},{4,2},{5,3},{6,0},{7,1},{8,14},{9,15},{10,... | collective-permute-start | bytes 786440 | tf_op jit(solution)/shard_map/ppermute | solution.py:386
  42.0 5.1 %collective-permute-start.19 = (f32[4,136,128]{2,1,0:T(8,128)S(1)}, f32[4,136,128]{2,1,0:T(8,128)S(1)}, u32[]{:S(2)}, u32[]{:S(2)}) collective-permute-start(f32[4,136,128]{2,1,0:T(8,128)S(1)} %get-tuple-element.55), channel_id=1, source_target_pairs={{0,1},{1,0},{2,3},{3,2},{4,5},{5,4},{6,7},{7,6},{8,9},{9,8},{10,11... | collective-permute-start | bytes 835592 | tf_op jit(solution)/shard_map/ppermute | solution.py:386
  43.6 6.1 %collective-permute-start.15 = (f32[128,128]{1,0:T(8,128)S(1)}, f32[128,128]{1,0:T(8,128)S(1)}, u32[]{:S(2)}, u32[]{:S(2)}) collective-permute-start(f32[128,128]{1,0:T(8,128)S(1)} %get-tuple-element.59), channel_id=1, source_target_pairs={{0,4},{1,5},{2,6},{3,7},{4,0},{5,1},{6,2},{7,3},{8,12},{9,13},{10,... | collective-permute-start | bytes 196616 | tf_op jit(solution)/shard_map/ppermute | solution.py:386
  44.5 6.2 %collective-permute-start.16 = (f32[128,128]{1,0:T(8,128)S(1)}, f32[128,128]{1,0:T(8,128)S(1)}, u32[]{:S(2)}, u32[]{:S(2)}) collective-permute-start(f32[128,128]{1,0:T(8,128)S(1)} %get-tuple-element.60), channel_id=1, source_target_pairs={{0,6},{1,7},{2,4},{3,5},{4,2},{5,3},{6,0},{7,1},{8,14},{9,15},{10,... | collective-permute-start | bytes 196616 | tf_op jit(solution)/shard_map/ppermute | solution.py:386
  46.1 4.7 %collective-permute-start.14 = (f32[128,128]{1,0:T(8,128)S(1)}, f32[128,128]{1,0:T(8,128)S(1)}, u32[]{:S(2)}, u32[]{:S(2)}) collective-permute-start(f32[128,128]{1,0:T(8,128)S(1)} %get-tuple-element.61), channel_id=1, source_target_pairs={{0,2},{1,3},{2,0},{3,1},{4,6},{5,7},{6,4},{7,5},{8,10},{9,11},{10,... | collective-permute-start | bytes 196616 | tf_op jit(solution)/shard_map/ppermute | solution.py:386
  47.2 5.2 %collective-permute-start.21 = (f32[136,128]{1,0:T(8,128)S(1)}, f32[136,128]{1,0:T(8,128)S(1)}, u32[]{:S(2)}, u32[]{:S(2)}) collective-permute-start(f32[136,128]{1,0:T(8,128)S(1)} %get-tuple-element.56), channel_id=1, source_target_pairs={{0,4},{1,5},{2,6},{3,7},{4,0},{5,1},{6,2},{7,3},{8,12},{9,13},{10,... | collective-permute-start | bytes 208904 | tf_op jit(solution)/shard_map/ppermute | solution.py:386
  48.2 5.2 %collective-permute-start.22 = (f32[136,128]{1,0:T(8,128)S(1)}, f32[136,128]{1,0:T(8,128)S(1)}, u32[]{:S(2)}, u32[]{:S(2)}) collective-permute-start(f32[136,128]{1,0:T(8,128)S(1)} %get-tuple-element.57), channel_id=1, source_target_pairs={{0,6},{1,7},{2,4},{3,5},{4,2},{5,3},{6,0},{7,1},{8,14},{9,15},{10,... | collective-permute-start | bytes 208904 | tf_op jit(solution)/shard_map/ppermute | solution.py:386
  49.7 4.3 %collective-permute-start.20 = (f32[136,128]{1,0:T(8,128)S(1)}, f32[136,128]{1,0:T(8,128)S(1)}, u32[]{:S(2)}, u32[]{:S(2)}) collective-permute-start(f32[136,128]{1,0:T(8,128)S(1)} %get-tuple-element.58), channel_id=1, source_target_pairs={{0,2},{1,3},{2,0},{3,1},{4,6},{5,7},{6,4},{7,5},{8,10},{9,11},{10,... | collective-permute-start | bytes 208904 | tf_op jit(solution)/shard_map/ppermute | solution.py:386
  50.8 4.9 %collective-permute-start.17 = (f32[128,128]{1,0:T(8,128)S(1)}, f32[128,128]{1,0:T(8,128)S(1)}, u32[]{:S(2)}, u32[]{:S(2)}) collective-permute-start(f32[128,128]{1,0:T(8,128)S(1)} %fusion.1), channel_id=1, source_target_pairs={{0,8},{8,0},{16,24},{24,16},{1,9},{9,1},{17,25},{25,17},{2,10},{10... | collective-permute-start | bytes 196616 | tf_op jit(solution)/shard_map/ppermute | solution.py:386
  54.0 4.3 %collective-permute-start.23 = (f32[128,128]{1,0:T(8,128)S(1)}, f32[128,128]{1,0:T(8,128)S(1)}, u32[]{:S(2)}, u32[]{:S(2)}) collective-permute-start(f32[128,128]{1,0:T(8,128)S(1)} %slice.48), channel_id=1, source_target_pairs={{0,8},{8,0},{16,24},{24,16},{1,9},{9,1},{17,25},{25,17},{2,10},{10... | collective-permute-start | bytes 196616 | tf_op jit(solution)/shard_map/ppermute | solution.py:386
  55.7 6.6 %collective-permute-start.18 = (f32[128,128]{1,0:T(8,128)S(1)}, f32[128,128]{1,0:T(8,128)S(1)}, u32[]{:S(2)}, u32[]{:S(2)}) collective-permute-start(f32[128,128]{1,0:T(8,128)S(1)} %add.40), channel_id=1, source_target_pairs={{0,16},{8,24},{16,0},{24,8},{1,17},{9,25},{17,1},{25,9},{2,18},{10... | collective-permute-start | bytes 196616 | tf_op jit(solution)/shard_map/ppermute | solution.py:386
  58.4 5.2 %collective-permute-start.24 = (f32[128,128]{1,0:T(8,128)S(1)}, f32[128,128]{1,0:T(8,128)S(1)}, u32[]{:S(2)}, u32[]{:S(2)}) collective-permute-start(f32[128,128]{1,0:T(8,128)S(1)} %slice_add_fusion), channel_id=1, source_target_pairs={{0,16},{8,24},{16,0},{24,8},{1,17},{9,25},{17,1},{25,9},{2,18},{10... | collective-permute-start | bytes 196616 | tf_op jit(solution)/shard_map/ppermute | solution.py:386
  (5 other events, 33.9 us)
